TPU v7x, 32 devices: a whole 2x2x4 slice. The times are simulated.
32 devices in a mesh: az: 8 (over z, x), rx: 4 (over y, core).
Axes of the slice: x: 2, y: 2, z: 4, core: 2. Of those that a mesh axis runs over, the one named last changes fastest.
Arguments:
- adjoint: float32 [5, 8, 128, 512], P(None, 'az', None, 'rx'), may hold values from -6 to 6
- density: float32 [8, 128, 512], P('az', None, 'rx'), may hold values from 0.6 to 1.4
- velocity: float32 [3, 8, 128, 512], P(None, 'az', None, 'rx'), may hold values from -0.9 to 0.9
- pressure: float32 [8, 128, 512], P('az', None, 'rx'), may hold values from 0.5 to 0.9
- fwh_cell: int32 [8, 4, 256], P('az', 'rx'), may hold values from 0 to 16383
- fwh_bin: int32 [8, 4, 256], P('az', 'rx'), may hold values from 0 to 255
- fwh_weight: float32 [8, 4, 256], P('az', 'rx'), may hold values from -6 to 6
- fwh_count: int32 [8, 4], P('az', 'rx'), may hold values from 1 to 256, as said below
Outputs:
- section: float32 [5, 8, 128, 512], P(None, 'az', None, 'rx')
- signal: float32 [256], P(('az', 'rx'))
Inputs may be any that keep to these rules, and one draw needn't show every extreme that they name: `fwh_count`: slots at or after a device's count are unused; some device has all 256 slots live.
All inputs are finite; a program needn't handle non-finite values.
Results may differ from a plain program's by a relative error of at most 0.00017.
Values sent between devices are 32-bit elements; how exact they have to be, the bound alone decides.
No kernel may reach another device: no remote copies, remote signals or barrier semaphores. Data moves between devices by JAX's collectives and lax.ppermute only.
A program may use at most 64 MiB of HBM per device.

v0:
```python
import math

import jax
import jax.numpy as jnp
from jax import lax
from jax.sharding import PartitionSpec as P

BIN_DEV = 8


ALPHA_FILTER = 0.495
COEF_ZERO = 11.0 / 16.0 + 5.0 * ALPHA_FILTER / 8.0
COEF_ONE = 15.0 / 32.0 + 17.0 * ALPHA_FILTER / 16.0
COEF_TWO = -3.0 / 16.0 + 3.0 * ALPHA_FILTER / 8.0
COEF_THREE = 1.0 / 32.0 - ALPHA_FILTER / 16.0
ALPHA_DERIV = 1.0 / 3.0
NEAR_COEF = 14.0 / 9.0
FAR_COEF = 1.0 / 9.0
AXIAL_STEP = 0.02
RADIAL_STEP = 0.02
INNER_RADIUS = 0.3
SECTION_STEP = 0.004
GAMMA_GAS = 1.4


def padded_2(shard, sides, width):
    for axis, dim in sides:
        size, length = (lax.axis_size(axis), shard.shape[dim])
        up = [(i, (i + 1) % size) for i in range(size - 1)]
        down = [(j, i) for i, j in up]
        last = lax.slice_in_dim(shard, length - width, length, axis=dim)
        leading = lax.slice_in_dim(shard, 0, width, axis=dim)
        before = lax.ppermute(last, axis, up)
        after = lax.ppermute(leading, axis, down)
        shard = jnp.concatenate([before, shard, after], axis=dim)
    return shard


def mode_gains(count):
    angle = jnp.arange(count, dtype=jnp.int32).astype(jnp.float32) * (2.0 * math.pi / count)
    cosine = jnp.cos(angle)
    filter_gain = (
        COEF_ZERO
        + COEF_ONE * cosine
        + COEF_TWO * jnp.cos(2.0 * angle)
        + COEF_THREE * jnp.cos(3.0 * angle)
    ) / (1.0 + 2.0 * ALPHA_FILTER * cosine)
    spacing = 2.0 * math.pi / count
    deriv_gain = (
        filter_gain
        * (NEAR_COEF * jnp.sin(angle) + 0.5 * FAR_COEF * jnp.sin(2.0 * angle))
        / (spacing * (1.0 + 2.0 * ALPHA_DERIV * cosine))
    )
    return (filter_gain, deriv_gain)


def kernel_values(offsets, count, filter_gain, deriv_gain):
    modes = jnp.arange(count, dtype=jnp.int32)
    phase = jnp.mod(offsets[..., None] * modes, count).astype(jnp.float32) * (2.0 * math.pi / count)
    smooth = jnp.sum(filter_gain * jnp.cos(phase), axis=-1) / count
    slope = -jnp.sum(deriv_gain * jnp.sin(phase), axis=-1) / count
    return (smooth, slope)


def central(padded, axis, width, step):

    def piece_at(start):
        return lax.slice_in_dim(padded, start, start + width, axis=axis)

    return (
        45.0 * (piece_at(4) - piece_at(2))
        - 9.0 * (piece_at(5) - piece_at(1))
        + (piece_at(6) - piece_at(0))
    ) / (60.0 * step)


def adjoint_flux(grad_axial, grad_radial, grad_theta, density, velocity, pressure):
    axial_vel, radial_vel, swirl_vel = (velocity[0], velocity[1], velocity[2])
    stiff = GAMMA_GAS * pressure
    inverse = 1.0 / density
    mass_term = axial_vel * grad_axial[0] + radial_vel * grad_radial[0] + swirl_vel * grad_theta[0]
    axial_term = (
        density * grad_axial[0]
        + axial_vel * grad_axial[1]
        + stiff * grad_axial[4]
        + radial_vel * grad_radial[1]
        + swirl_vel * grad_theta[1]
    )
    radial_term = (
        axial_vel * grad_axial[2]
        + density * grad_radial[0]
        + radial_vel * grad_radial[2]
        + stiff * grad_radial[4]
        + swirl_vel * grad_theta[2]
    )
    swirl_term = (
        axial_vel * grad_axial[3]
        + radial_vel * grad_radial[3]
        + density * grad_theta[0]
        + swirl_vel * grad_theta[3]
        + stiff * grad_theta[4]
    )
    energy_term = (
        inverse * grad_axial[1]
        + axial_vel * grad_axial[4]
        + inverse * grad_radial[2]
        + radial_vel * grad_radial[4]
        + inverse * grad_theta[3]
        + swirl_vel * grad_theta[4]
    )
    return jnp.stack([mass_term, axial_term, radial_term, swirl_term, energy_term])


def local(adjoint, density, velocity, pressure, fwh_cell, fwh_bin, fwh_weight, fwh_count):
    fields, local_theta, radial_cells, axial_cells = adjoint.shape
    count = local_theta * lax.axis_size("az")
    filter_gain, deriv_gain = mode_gains(count)
    piece = lax.all_gather(adjoint, "az", axis=1, tiled=True)
    width = piece.shape[1]
    targets = lax.axis_index("az") * local_theta + jnp.arange(local_theta, dtype=jnp.int32)
    sources = jnp.arange(width, dtype=jnp.int32)
    offsets = jnp.mod(targets[:, None] - sources[None, :], count)
    smooth, slope = kernel_values(offsets, count, filter_gain, deriv_gain)
    filtered = jnp.einsum("ij,cjrx->cirx", smooth, piece, precision=lax.Precision.HIGHEST)
    dtheta = jnp.einsum("ij,cjrx->cirx", slope, piece, precision=lax.Precision.HIGHEST)
    pad_axial = padded_2(filtered, (("rx", 3),), 3)
    daxial = central(pad_axial, 3, axial_cells, AXIAL_STEP)
    pad_radial = jnp.pad(filtered, ((0, 0), (0, 0), (3, 3), (0, 0)))
    dradial = central(pad_radial, 2, radial_cells, RADIAL_STEP)
    radius = (
        INNER_RADIUS
        + (jnp.arange(radial_cells, dtype=jnp.int32).astype(jnp.float32) + 0.5) * RADIAL_STEP
    ).reshape(radial_cells, 1)
    flux = adjoint_flux(daxial, dradial, dtheta / radius, density, velocity, pressure)
    section = filtered + SECTION_STEP * flux
    slot_cells = fwh_cell[0, 0]
    slot_bins = fwh_bin[0, 0]
    slot_weights = fwh_weight[0, 0]
    live = jnp.arange(slot_cells.shape[0], dtype=jnp.int32) < fwh_count[0, 0]
    picked = jnp.take(section.reshape(fields, -1), slot_cells, axis=1)
    values = jnp.where(live, slot_weights * (picked[4] + picked[1]), 0.0)
    totals = jax.ops.segment_sum(
        values, slot_bins, num_segments=BIN_DEV * lax.axis_size("az") * lax.axis_size("rx")
    )
    signal = lax.psum_scatter(totals, ("az", "rx"), scatter_dimension=0, tiled=True)
    return (section, signal)


def solution(mesh):
    placed = (
        P(None, "az", None, "rx"),
        P("az", None, "rx"),
        P(None, "az", None, "rx"),
        P("az", None, "rx"),
        P("az", "rx", None),
        P("az", "rx", None),
        P("az", "rx", None),
        P("az", "rx"),
    )
    return jax.shard_map(
        local,
        mesh=mesh,
        in_specs=placed,
        out_specs=(P(None, "az", None, "rx"), P(("az", "rx"))),
        check_vma=False,
    )
```

profile of v0, /device:TPU:0, one launch (start us, length us, event | category | flops | bytes accessed | tf_op | source)
XLA Modules:
  0.0 143.3 jit_solution(1472916147521559716)
XLA Ops:
  7.2 0.0 all-gather.2.cloned.1.call-start
  7.2 0.7 all-gather.2.cloned.1.call-update
  8.6 0.1 multiply_divide_fusion
  8.6 0.7 compare_select_fusion
  9.3 0.2 multiply_reduce_fusion
  9.6 0.7 compare_and_fusion
  10.3 57.3 %all-gather.2.cloned.1.call-done = f32[5,8,128,128]{3,2,1,0:T(8,128)} async-done(((f32[5,1,128,128]{3,2,1,0:T(8,128)}), f32[5,8,128,128]{3,2,1,0:T(8,128)}) %all-gather.2.cloned.1.call-update) | async-done | bytes 2621456 | tf_op jit(solution)/shard_map/all_gather | solution.py:118
  67.6 5.4 %fusion.2 = f32[1,5,128,128]{3,0,2,1:T(1,128)S(1)} fusion(f32[5,8,128,128]{3,2,1,0:T(8,128)} %all-gather.2.cloned.1.call-done, f32[8]{0:T(128)S(1)} %get-tuple-element.3), kind=kOutput, calls=%fused_computation.4 | convolution fusion | flops 7864328 | bytes 2949152 | tf_op jit(solution)/shard_map/ij,cjrx->cirx/dot_general | solution.py:124
  73.0 0.2 fusion.62
  73.2 1.3 collective-permute-start
  74.5 3.1 %collective-permute-start.1 = (f32[5,1,128,3]{3,2,1,0:T(8,128)S(1)}, f32[5,1,128,3]{3,2,1,0:T(8,128)S(1)}, u32[]{:S(2)}, u32[]{:S(2)}) collective-permute-start(f32[5,1,128,3]{3,2,1,0:T(8,128)S(1)} %get-tuple-element.7), channel_id=1, source_target_pairs={{0,1},{1,2},{2,3},{4,5},{5,6},{6,7},{8,9},{9,10},{10,11},{12,13},{... | collective-permute-start | bytes 23048 | tf_op jit(solution)/shard_map/ppermute | solution.py:33
  77.5 0.0 copy-done
  77.5 0.0 copy-start.1
  77.5 0.0 copy-start.3
  77.6 0.0 copy-start.4
  77.6 3.6 %fusion = f32[1,5,128,128]{3,0,2,1:T(1,128)S(1)} fusion(f32[5,8,128,128]{3,2,1,0:T(8,128)S(1)} %copy-done, f32[8]{0:T(128)S(1)} %get-tuple-element.2), kind=kOutput, calls=%fused_computation.2 | convolution fusion | flops 7864336 | bytes 2949152 | tf_op jit(solution)/shard_map/ij,cjrx->cirx/dot_general | solution.py:125
  81.1 0.1 broadcast_divide_fusion
  81.2 0.0 collective-permute-done
  81.2 0.0 collective-permute-done.1
  81.3 1.1 fusion.9
  82.4 0.0 copy-done.1
  82.5 0.0 copy-done.3
  82.5 0.0 copy-done.4
  82.7 0.0 copy-start.2
  82.7 0.0 copy-start.5
  82.7 4.7 %copy.13 = f32[5,128,128]{0,2,1:T(8,128)} copy(f32[5,128,128]{2,1,0:T(8,128)S(1)} %multiply_add_fusion) | data formatting | bytes 655360 | tf_op jit(solution)/shard_map/add | solution.py:135
  87.4 4.1 %gather_fusion = f32[256,5]{1,0:T(8,128)S(1)} fusion(f32[5,16384]{0,1:T(8,128)} %bitcast.150, s32[1024]{0:T(1024)S(1)} %pad_clamp_fusion), kind=kCustom, calls=%fused_computation | custom fusion | bytes 11264 | tf_op jit(solution)/shard_map/jit(_take)/gather | solution.py:140
  91.5 0.1 select_bitcast_fusion
  91.6 0.2 fusion.16
  91.9 2.5 %scatter_custom_fusion = f32[256]{0:T(256)S(1)} fusion(s32[256]{0:T(256)} %bitcast.159, f32[256]{0:T(256)S(1)} %compare_select_fusion.4, f32[]{:T(128)} %constant.83.clone.1), kind=kCustom, calls=%fused_computation.103 | custom fusion | flops 256 | bytes 1536 | tf_op jit(solution)/shard_map/scatter-add | solution.py:142
  94.3 41.5 %all-reduce.1 = f32[256]{0:T(256)S(1)} all-reduce(f32[256]{0:T(256)S(1)} %scatter_custom_fusion), channel_id=2, replica_groups=mesh['az'=8,'rx'=4] {'az','rx'}, use_global_device_ids=true, to_apply=%region_3.4.clone | all-reduce | flops 256 | bytes 2048
  135.9 0.6 dynamic-slice
  (13 shorter events, 0.3 us)
Async XLA Ops:
  7.2 60.4 %all-gather.2.cloned.1.call-start = ((), (), s32[]{:S(2)}) async-start(), calls=%async_computation | async-start | bytes 2949120 | tf_op jit(solution)/shard_map/all_gather | solution.py:118
  67.6 10.0 %copy-start = (f32[5,8,128,128]{3,2,1,0:T(8,128)S(1)}, f32[5,8,128,128]{3,2,1,0:T(8,128)}, u32[]{:S(2)}) copy-start(f32[5,8,128,128]{3,2,1,0:T(8,128)} %all-gather.2.cloned.1.call-done) | copy-start | bytes 7864324
  73.2 8.1 %collective-permute-start = (f32[5,1,128,3]{3,2,1,0:T(8,128)S(1)}, f32[5,1,128,3]{3,2,1,0:T(8,128)S(1)}, u32[]{:S(2)}, u32[]{:S(2)}) collective-permute-start(f32[5,1,128,3]{3,2,1,0:T(8,128)S(1)} %get-tuple-element.6), channel_id=1, source_target_pairs={{1,0},{2,1},{3,2},{5,4},{6,5},{7,6},{9,8},{10,9},{11,10},{13,12},{... | collective-permute-start | bytes 23048 | tf_op jit(solution)/shard_map/ppermute | solution.py:34
  74.5 6.8 %collective-permute-start.1 = (f32[5,1,128,3]{3,2,1,0:T(8,128)S(1)}, f32[5,1,128,3]{3,2,1,0:T(8,128)S(1)}, u32[]{:S(2)}, u32[]{:S(2)}) collective-permute-start(f32[5,1,128,3]{3,2,1,0:T(8,128)S(1)} %get-tuple-element.7), channel_id=1, source_target_pairs={{0,1},{1,2},{2,3},{4,5},{5,6},{6,7},{8,9},{9,10},{10,11},{12,13},{... | collective-permute-start | bytes 23048 | tf_op jit(solution)/shard_map/ppermute | solution.py:33
  77.5 4.9 %copy-start.1 = (f32[3,1,128,128]{3,2,1,0:T(8,128)S(1)}, f32[3,1,128,128]{3,2,1,0:T(8,128)}, u32[]{:S(2)}) copy-start(f32[3,1,128,128]{3,2,1,0:T(8,128)} %param.10) | copy-start | bytes 589828
  77.5 4.9 %copy-start.3 = (f32[1,128,128]{2,1,0:T(8,128)S(1)}, f32[1,128,128]{2,1,0:T(8,128)}, u32[]{:S(2)}) copy-start(f32[1,128,128]{2,1,0:T(8,128)} %param.9) | copy-start | bytes 196612
  77.6 4.9 %copy-start.4 = (f32[1,128,128]{2,1,0:T(8,128)S(1)}, f32[1,128,128]{2,1,0:T(8,128)}, u32[]{:S(2)}) copy-start(f32[1,128,128]{2,1,0:T(8,128)} %param.11) | copy-start | bytes 196612
  82.7 4.7 %copy-start.2 = (f32[5,128,128]{2,1,0:T(8,128)}, f32[5,128,128]{2,1,0:T(8,128)S(1)}, u32[]{:S(2)}) copy-start(f32[5,128,128]{2,1,0:T(8,128)S(1)} %multiply_add_fusion) | copy-start | bytes 983044
  82.7 9.2 %copy-start.5 = (f32[1,1,256]{2,1,0:T(1,128)S(1)}, f32[1,1,256]{2,1,0:T(1,128)}, u32[]{:S(2)}) copy-start(f32[1,1,256]{2,1,0:T(1,128)} %param.14) | copy-start | bytes 3076
Sparse Core Ops, SparseCore 0:
  10.2 57.3 all-gather.1
where the time goes:
time: 144 us; the launch traced here: 143 us
  waiting for transfers between devices  58 us (40%)
  blocking collectives  41.5 us (29%)
  between operations  14.9 us (10%)
  local copies, waits for them, and re-layouts  9.59 us (7%)
  matrix products  8.98 us (6%)
  other arithmetic  5.92 us (4%)
  starting transfers between devices  4.38 us (3%)
    all_gather x1, waiting for transfers between devices, local(): piece = lax.all_gather(adjoint, 'az', axis=1, tiled=True)  57.3 us
    unnamed x1, blocking collectives  41.5 us
    dot_general x1, matrix products, local(): jnp.einsum('ij,cjrx->cirx', smooth, piece, precision=lax.Precision.HIGHEST)  5.43 us
    add x1, local copies, waits for them, and re-layouts, local(): section = filtered + SECTION_STEP * flux  4.71 us
    gather x1, local copies, waits for them, and re-layouts, local(): picked = jnp.take(section.reshape(fields, -1), slot_cells, axis=1)  4.1 us
    dot_general x1, matrix products, local(): jnp.einsum('ij,cjrx->cirx', slope, piece, precision=lax.Precision.HIGHEST)  3.56 us
    ppermute x1, starting transfers between devices, padded_2(): before = lax.ppermute(last, axis, up)  3.05 us
  transfers between devices with their start and end apart: 3, of which 1 were waited for; matrix products, arithmetic and copies ran while one was open for 4% of the time, Pallas kernels for 0%

commit v1 on v0

v1 whole, which is shorter than its diff:
```python
import functools
import math

import jax
import jax.numpy as jnp
import numpy as np
from jax import lax
from jax.experimental import pallas as pl
from jax.experimental.pallas import tpu as pltpu
from jax.sharding import PartitionSpec as P

BIN_DEV = 8
LANES = 128
SUB = 4
EDGE = 3
SLOT = 16

ALPHA_FILTER = 0.495
COEF_ZERO = 11.0 / 16.0 + 5.0 * ALPHA_FILTER / 8.0
COEF_ONE = 15.0 / 32.0 + 17.0 * ALPHA_FILTER / 16.0
COEF_TWO = -3.0 / 16.0 + 3.0 * ALPHA_FILTER / 8.0
COEF_THREE = 1.0 / 32.0 - ALPHA_FILTER / 16.0
ALPHA_DERIV = 1.0 / 3.0
NEAR_COEF = 14.0 / 9.0
FAR_COEF = 1.0 / 9.0
AXIAL_STEP = 0.02
RADIAL_STEP = 0.02
INNER_RADIUS = 0.3
SECTION_STEP = 0.004
GAMMA_GAS = 1.4
HIGHEST = lax.Precision.HIGHEST


def kernel_values(count):
    modes = np.arange(count)
    angle = modes * (2.0 * math.pi / count)
    cosine = np.cos(angle)
    filter_gain = (
        COEF_ZERO
        + COEF_ONE * cosine
        + COEF_TWO * np.cos(2.0 * angle)
        + COEF_THREE * np.cos(3.0 * angle)
    ) / (1.0 + 2.0 * ALPHA_FILTER * cosine)
    spacing = 2.0 * math.pi / count
    deriv_gain = (
        filter_gain
        * (NEAR_COEF * np.sin(angle) + 0.5 * FAR_COEF * np.sin(2.0 * angle))
        / (spacing * (1.0 + 2.0 * ALPHA_DERIV * cosine))
    )
    phase = np.mod(modes[:, None] * modes[None, :], count) * (2.0 * math.pi / count)
    smooth = np.sum(filter_gain * np.cos(phase), axis=-1) / count
    slope = -np.sum(deriv_gain * np.sin(phase), axis=-1) / count
    return smooth, slope


def dot_up(weights, values):
    total = None
    for weight, value in zip(weights, values, strict=True):
        term = np.float32(weight) * value
        total = term if total is None else total + term
    return total


def convolve(kernel, sums, diffs):
    half = len(sums)
    first, second = [], []
    for i in range(half):
        near = [kernel[(i - j) % (2 * half)] for j in range(half)]
        far = [kernel[(i - j + half) % (2 * half)] for j in range(half)]
        even = dot_up([0.5 * (n + f) for n, f in zip(near, far)], sums)
        odd = dot_up([0.5 * (n - f) for n, f in zip(near, far)], diffs)
        first.append(even + odd)
        second.append(even - odd)
    return first + second


def pack_body(blocks, source, target):
    fields, radial = source.shape[0], source.shape[2]
    for field in range(fields):
        for row in range(0, radial, 2 * SUB):
            tile = source[field, 0, pl.ds(row, 2 * SUB), :]
            at = (field * radial + row) // SUB
            for part in range(2):
                target[(at + part) // blocks, (at + part) % blocks] = tile[
                    part * SUB : (part + 1) * SUB
                ]


def filter_body(thetas, width, blocks, smooth, slope, source, target):
    half = thetas // 2

    for b in range(width):

        @pl.loop(0, blocks)
        def _(j, b=b):
            values = [source[t * width + b, j] for t in range(thetas)]
            sums = [values[t] + values[t + half] for t in range(half)]
            diffs = [values[t] - values[t + half] for t in range(half)]
            for t, value in enumerate(convolve(smooth, sums, diffs)):
                target[t * width + b, j] = value
            for t, value in enumerate(convolve(slope, sums, diffs)):
                target[t * width + b, blocks + j] = value

    lane = lax.broadcasted_iota(jnp.int32, (SUB, LANES), 1)
    right_side = lane < EDGE
    for t in range(thetas):
        for b in range(width):
            packed = jnp.zeros((SUB, LANES), jnp.float32)
            before, after = b - 1, b + 1
            if width == 1:
                before, after = b, b
            for j in range(blocks):
                zero = jnp.zeros((SUB, LANES), jnp.float32)
                left = target[t * width + before, j] if before >= 0 else zero
                right = target[t * width + after, j] if after < width else zero
                edges = jnp.where(right_side, right, left)
                edges = pltpu.roll(edges, SLOT * j + EDGE, 1)
                mine = (lane >= SLOT * j) & (lane < SLOT * j + 2 * EDGE)
                packed = jnp.where(mine, edges, packed)
            target[t * width + b, 2 * blocks] = packed


def final_body(
    blocks,
    devices,
    pieces,
    density,
    velocity,
    pressure,
    cells,
    bins,
    weights,
    live_count,
    section,
    totals,
    filtered,
    slopes,
    halos,
    picked,
):
    fields, radial = section.shape[0], section.shape[2]
    tile = 2 * SUB
    per_field = radial // SUB
    pad = jnp.zeros((tile, LANES), jnp.float32)
    for field in range(fields):
        filtered[field, pl.ds(0, tile), :] = pad
        filtered[field, pl.ds(tile + radial, tile), :] = pad
    for at in range(fields * per_field):
        field, row = at // per_field, SUB * (at % per_field)
        piece, j = at // blocks, at % blocks
        filtered[field, pl.ds(tile + row, SUB), :] = pieces[piece, j]
        slopes[field, pl.ds(row, SUB), :] = pieces[piece, blocks + j]
        edges = pltpu.roll(pieces[piece, 2 * blocks], LANES - (SLOT * j + EDGE), 1)
        halos[field, pl.ds(row, SUB), :] = edges

    lane = lax.broadcasted_iota(jnp.int32, (tile, LANES), 1)
    sub = lax.broadcasted_iota(jnp.int32, (tile, LANES), 0)
    unit = SECTION_STEP / (60.0 * AXIAL_STEP)
    axial = [np.float32(c * unit) for c in (45.0, -9.0, 1.0)]
    unit = SECTION_STEP / (60.0 * RADIAL_STEP)
    radially = [np.float32(c * unit) for c in (45.0, -9.0, 1.0)]

    for row in range(0, radial, tile):
        rows = pl.ds(row, tile)
        middle, g, e, s = [], [], [], []
        cell_radius = INNER_RADIUS + ((sub + row).astype(jnp.float32) + 0.5) * RADIAL_STEP
        stretch = SECTION_STEP / cell_radius
        for field in range(fields):
            here = filtered[field, pl.ds(tile + row, tile), :]
            edge = halos[field, rows, :]
            total = None
            for k in range(1, EDGE + 1):
                ahead = pltpu.roll(jnp.where(lane < k, edge, here), LANES - k, 1)
                behind = pltpu.roll(jnp.where(lane >= LANES - k, edge, here), k, 1)
                term = axial[k - 1] * (ahead - behind)
                total = term if total is None else total + term
            g.append(total)
            total = None
            for k in range(1, EDGE + 1):
                above = filtered[field, pl.ds(tile + row + k, tile), :]
                below = filtered[field, pl.ds(tile + row - k, tile), :]
                term = radially[k - 1] * (above - below)
                total = term if total is None else total + term
            e.append(total)
            s.append(slopes[field, rows, :] * stretch)
            middle.append(here)
        rho = density[0, rows, :]
        u, v, w = (velocity[i, 0, rows, :] for i in range(3))
        stiff = GAMMA_GAS * pressure[0, rows, :]
        inverse = 1.0 / rho
        moved = [u * g[i] + v * e[i] + w * s[i] for i in range(fields)]
        out = [
            middle[0] + moved[0],
            middle[1] + (moved[1] + rho * g[0] + stiff * g[4]),
            middle[2] + (moved[2] + rho * e[0] + stiff * e[4]),
            middle[3] + (moved[3] + rho * s[0] + stiff * s[4]),
            middle[4] + (moved[4] + inverse * (g[1] + e[2] + s[3])),
        ]
        for field in range(fields):
            section[field, 0, rows, :] = out[field]
        picked[rows, :] = out[4] + out[1]

    slots = cells.shape[2]
    cell = cells[0]
    shift = LANES.bit_length() - 1
    column = lax.broadcasted_iota(jnp.int32, (LANES, slots), 0)
    chosen = jnp.where(column == (cell & (LANES - 1)), 1.0, 0.0)
    lines = jnp.dot(picked[...], chosen, precision=HIGHEST, preferred_element_type=jnp.float32)
    line = lax.broadcasted_iota(jnp.int32, (radial, slots), 0)
    lines = jnp.where(line == lax.shift_right_logical(cell, shift), lines, 0.0)
    values = weights[0] * jnp.sum(lines, axis=0, keepdims=True)
    order = lax.broadcasted_iota(jnp.int32, (1, slots), 1)
    values = jnp.where(order < live_count[0, 0], values, 0.0)
    own_bin = bins[0]
    owner = lax.broadcasted_iota(jnp.int32, (devices, slots), 0)
    spread = jnp.where(owner == own_bin // BIN_DEV, values, 0.0)
    place = lax.broadcasted_iota(jnp.int32, (LANES, slots), 0)
    within = jnp.where(place == own_bin % BIN_DEV, 1.0, 0.0)
    totals[...] = lax.dot_general(
        spread,
        within,
        (((1,), (1,)), ((), ())),
        precision=HIGHEST,
        preferred_element_type=jnp.float32,
    )


def whole_block():
    return pl.BlockSpec(memory_space=pltpu.VMEM)


def local(adjoint, density, velocity, pressure, fwh_cell, fwh_bin, fwh_weight, fwh_count):
    fields, local_theta, radial, axial_cells = adjoint.shape
    thetas, blocks_x = lax.axis_size("az"), lax.axis_size("rx")
    devices = thetas * blocks_x
    assert local_theta == 1 and axial_cells == LANES
    lines = fields * radial // SUB
    everyone = lines % devices == 0
    group = ("az", "rx") if everyone else ("az",)
    members = devices if everyone else thetas
    width = members // thetas
    blocks = lines // members
    params = pltpu.CompilerParams(vmem_limit_bytes=32 * 1024 * 1024)
    f32 = jnp.float32

    pieces = pl.pallas_call(
        functools.partial(pack_body, blocks),
        out_shape=jax.ShapeDtypeStruct((members, blocks, SUB, LANES), f32),
        in_specs=[whole_block()],
        out_specs=whole_block(),
        compiler_params=params,
        name="pack",
    )(adjoint)
    pieces = lax.all_to_all(pieces, group, 0, 0, tiled=True)
    smooth, slope = kernel_values(thetas)
    pieces = pl.pallas_call(
        functools.partial(filter_body, thetas, width, blocks, smooth, slope),
        out_shape=jax.ShapeDtypeStruct((members, 2 * blocks + 1, SUB, LANES), f32),
        in_specs=[whole_block()],
        out_specs=whole_block(),
        compiler_params=params,
        name="azimuth",
    )(pieces)
    if not everyone:
        own = pieces[:, 2 * blocks]
        up = [(i, i + 1) for i in range(blocks_x - 1)]
        down = [(j, i) for i, j in up]
        before, after = lax.ppermute(own, "rx", up), lax.ppermute(own, "rx", down)
        lane = jnp.arange(LANES, dtype=jnp.int32) % SLOT
        pieces = pieces.at[:, 2 * blocks].set(jnp.where(lane < EDGE, before, after))
    pieces = lax.all_to_all(pieces, group, 0, 0, tiled=True)
    section, totals = pl.pallas_call(
        functools.partial(final_body, blocks, devices),
        out_shape=(
            jax.ShapeDtypeStruct(adjoint.shape, f32),
            jax.ShapeDtypeStruct((devices, LANES), f32),
        ),
        in_specs=[whole_block()] * 7 + [pl.BlockSpec(memory_space=pltpu.SMEM)],
        out_specs=(whole_block(), whole_block()),
        scratch_shapes=[
            pltpu.VMEM((fields, radial + 4 * SUB, LANES), f32),
            pltpu.VMEM((fields, radial, LANES), f32),
            pltpu.VMEM((fields, radial, LANES), f32),
            pltpu.VMEM((radial, LANES), f32),
        ],
        compiler_params=params,
        name="section",
    )(pieces, density, velocity, pressure, fwh_cell, fwh_bin, fwh_weight, fwh_count)
    totals = lax.all_to_all(totals, ("az", "rx"), 0, 0, tiled=True)
    return section, jnp.sum(totals, axis=0)[:BIN_DEV]


def solution(mesh):
    placed = (
        P(None, "az", None, "rx"),
        P("az", None, "rx"),
        P(None, "az", None, "rx"),
        P("az", None, "rx"),
        P("az", "rx", None),
        P("az", "rx", None),
        P("az", "rx", None),
        P("az", "rx"),
    )
    return jax.shard_map(
        local,
        mesh=mesh,
        in_specs=placed,
        out_specs=(P(None, "az", None, "rx"), P(("az", "rx"))),
        check_vma=False,
    )
```

time: 144 us -> 57.3 us (0.40)
  waiting for transfers between devices: 58 us -> 18.5 us
  between operations: 14.9 us -> 1.36 us
  blocking collectives: 41.5 us -> 29.6 us
  matrix products: 8.98 us -> 0 us
  local copies, waits for them, and re-layouts: 9.59 us -> 0.99 us
  other arithmetic: 5.92 us -> 0.56 us
  Pallas kernels: 0 us -> 3.26 us
  starting transfers between devices: 4.38 us -> 2.77 us
    all_gather x1 -> x0, waiting for transfers between devices: 57.3 us -> none  [local(): piece = lax.all_gather(adjoint, 'az', axis=1, tiled=True)]
    unnamed x1 -> x0, blocking collectives: 41.5 us -> none
    all_to_all x0 -> x2, blocking collectives: none -> 29.6 us  [the longest x1 19.1 us: local(): pieces = lax.all_to_all(pieces, group, 0, 0, tiled=True)]
    all_to_all x0 -> x1, waiting for transfers between devices: none -> 18.5 us  [local(): pieces = lax.all_to_all(pieces, group, 0, 0, tiled=True)]
    dot_general x2 -> x0, matrix products: 8.98 us -> none  [the longest x1 5.43 us: local(): jnp.einsum('ij,cjrx->cirx', smooth, piece, precision=lax.Precision.HIGHEST)]
    add x1 -> x0, local copies, waits for them, and re-layouts: 4.71 us -> none  [local(): section = filtered + SECTION_STEP * flux]
    ppermute x2 -> x0, starting transfers between devices: 4.34 us -> none  [the longest x1 3.05 us: padded_2(): before = lax.ppermute(last, axis, up)]
    gather x1 -> x0, local copies, waits for them, and re-layouts: 4.1 us -> none  [local(): picked = jnp.take(section.reshape(fields, -1), slot_cells, axis=1)]
  transfers between devices with their start and end apart: 3 -> 1, of which waited for: 1 -> 1; matrix products, arithmetic and copies ran while one was open for 4% -> 0% of each run, Pallas kernels for 0% -> 0%
where the time goes in v1:
time: 57.3 us; the launch traced here: 57 us
  blocking collectives  29.6 us (52%)
  waiting for transfers between devices  18.5 us (32%)
  Pallas kernels  3.26 us (6%)
  starting transfers between devices  2.77 us (5%)
  between operations  1.36 us (2%)
  local copies, waits for them, and re-layouts  0.99 us (2%)
    all_to_all x1, blocking collectives, local(): pieces = lax.all_to_all(pieces, group, 0, 0, tiled=True)  19.1 us
    all_to_all x1, waiting for transfers between devices, local(): pieces = lax.all_to_all(pieces, group, 0, 0, tiled=True)  18.5 us
    all_to_all x1, blocking collectives, local(): totals = lax.all_to_all(totals, ('az', 'rx'), 0, 0, tiled=True)  10.5 us
    all_to_all x1, starting transfers between devices, local(): pieces = lax.all_to_all(pieces, group, 0, 0, tiled=True)  2.77 us
    pallas_call x1, Pallas kernels, local(): pl.pallas_call(functools.partial(final_body, blocks, devices), out_shape=...  1.64 us
    pallas_call x1, Pallas kernels, local(): pl.pallas_call(functools.partial(filter_body, thetas, width, blocks, smoo...  1.58 us
  transfers between devices with their start and end apart: 1, of which 1 were waited for; matrix products, arithmetic and copies ran while one was open for 0% of the time, Pallas kernels for 0%

profile of v1, /device:TPU:0, one launch (start us, length us, event | category | flops | bytes accessed | tf_op | source)
XLA Modules:
  0.0 57.0 jit_solution(1928561033538859205)
XLA Ops:
  0.6 0.0 copy-start
  0.6 1.0 %copy-done = f32[5,1,128,128]{3,2,1,0:T(8,128)S(1)} copy-done((f32[5,1,128,128]{3,2,1,0:T(8,128)S(1)}, f32[5,1,128,128]{3,2,1,0:T(8,128)}, u32[]{:S(2)}) %copy-start) | copy-done | bytes 327704
  1.6 19.1 %all_to_all.19.source = f32[32,5,4,128]{3,2,1,0:T(4,128)S(1)} all-to-all(f32[32,5,4,128]{3,2,1,0:T(4,128)S(1)} %pack.1), channel_id=1, replica_groups=mesh['az'=8,'rx'=4] {'az','rx'}, dimensions={0} | all-to-all | bytes 655360 | tf_op jit(solution)/shard_map/all_to_all | solution.py:254
  20.7 1.6 %azimuth.1 = f32[32,11,4,128]{3,2,1,0:T(4,128)} custom-call(f32[32,5,4,128]{3,2,1,0:T(4,128)S(1)} %all_to_all.19.source), custom_call_target="tpu_custom_call" | custom-call | tf_op jit(solution)/shard_map/azimuth/pallas_call | solution.py:256
  22.3 0.0 copy-start.1
  22.3 0.0 copy-start.2
  22.3 0.0 copy-start.3
  22.3 0.0 copy-start.5
  22.3 0.0 copy-start.6
  22.3 2.8 %all-to-all-start.1 = ((f32[32,11,4,128]{3,2,1,0:T(4,128)}), f32[32,11,4,128]{3,2,1,0:T(4,128)S(1)}, u32[]{:S(2)}, u32[]{:S(2)}) async-start(f32[32,11,4,128]{3,2,1,0:T(4,128)} %azimuth.1), calls=%async_computation.1 | async-start | bytes 1441792 | tf_op jit(solution)/shard_map/all_to_all | solution.py:271
  25.1 0.0 copy-start.4
  25.8 18.5 %all-to-all-done.1.pieces = f32[32,11,4,128]{3,2,1,0:T(4,128)S(1)} async-done(((f32[32,11,4,128]{3,2,1,0:T(4,128)}), f32[32,11,4,128]{3,2,1,0:T(4,128)S(1)}, u32[]{:S(2)}, u32[]{:S(2)}) %all-to-all-start.1) | async-done | bytes 720928 | tf_op jit(solution)/shard_map/all_to_all | solution.py:271
  44.3 0.0 copy-done.1
  44.3 0.0 copy-done.2
  44.3 0.0 copy-done.3
  44.3 0.0 copy-done.5
  44.3 0.0 copy-done.6
  44.3 0.0 copy-done.4
  44.4 1.6 %section.1 = (f32[5,1,128,128]{3,2,1,0:T(8,128)}, f32[32,128]{1,0:T(8,128)S(1)}) custom-call(f32[32,11,4,128]{3,2,1,0:T(4,128)S(1)} %all-to-all-done.1.pieces, f32[1,128,128]{2,1,0:T(8,128)S(1)} %copy-done.2, f32[3,1,128,128]{3,2,1,0:T(8,128)S(1)} %copy-done.1, f32[1,128,128]{2,1,0:T(8,128)S(1)} %copy-done.3, s32[1,1,256]{2,1,0:T(1,128)S(1)} %copy-done.4, ...), custom_call_target="tpu_custom_call" | custom-call | tf_op jit(solution)/shard_map/section/pallas_call | solution.py:272
  46.0 10.5 %all_to_all.20 = f32[32,1,128]{2,1,0:T(1,128)S(1)} all-to-all(f32[32,1,128]{2,1,0:T(1,128)S(1)} %bitcast.4), channel_id=1, replica_groups=mesh['az'=8,'rx'=4] {'az','rx'}, dimensions={0} | all-to-all | bytes 32768 | tf_op jit(solution)/shard_map/all_to_all | solution.py:289
  56.5 0.6 reduce_sum.9
  (1 shorter events, 0.0 us)
Async XLA Ops:
  0.6 1.0 %copy-start = (f32[5,1,128,128]{3,2,1,0:T(8,128)S(1)}, f32[5,1,128,128]{3,2,1,0:T(8,128)}, u32[]{:S(2)}) copy-start(f32[5,1,128,128]{3,2,1,0:T(8,128)} %source.1) | copy-start | bytes 983044
  22.3 22.0 %copy-start.1 = (f32[3,1,128,128]{3,2,1,0:T(8,128)S(1)}, f32[3,1,128,128]{3,2,1,0:T(8,128)}, u32[]{:S(2)}) copy-start(f32[3,1,128,128]{3,2,1,0:T(8,128)} %velocity.1) | copy-start | bytes 589828
  22.3 22.0 %copy-start.2 = (f32[1,128,128]{2,1,0:T(8,128)S(1)}, f32[1,128,128]{2,1,0:T(8,128)}, u32[]{:S(2)}) copy-start(f32[1,128,128]{2,1,0:T(8,128)} %density.1) | copy-start | bytes 196612
  22.3 22.0 %copy-start.3 = (f32[1,128,128]{2,1,0:T(8,128)S(1)}, f32[1,128,128]{2,1,0:T(8,128)}, u32[]{:S(2)}) copy-start(f32[1,128,128]{2,1,0:T(8,128)} %pressure.1) | copy-start | bytes 196612
  22.3 22.0 %copy-start.5 = (s32[1,1,256]{2,1,0:T(1,128)S(1)}, s32[1,1,256]{2,1,0:T(1,128)}, u32[]{:S(2)}) copy-start(s32[1,1,256]{2,1,0:T(1,128)} %bins.1) | copy-start | bytes 3076
  22.3 22.0 %copy-start.6 = (f32[1,1,256]{2,1,0:T(1,128)S(1)}, f32[1,1,256]{2,1,0:T(1,128)}, u32[]{:S(2)}) copy-start(f32[1,1,256]{2,1,0:T(1,128)} %weights.1) | copy-start | bytes 3076
  22.3 22.0 %all-to-all-start.1 = ((f32[32,11,4,128]{3,2,1,0:T(4,128)}), f32[32,11,4,128]{3,2,1,0:T(4,128)S(1)}, u32[]{:S(2)}, u32[]{:S(2)}) async-start(f32[32,11,4,128]{3,2,1,0:T(4,128)} %azimuth.1), calls=%async_computation.1 | async-start | bytes 1441792 | tf_op jit(solution)/shard_map/all_to_all | solution.py:271
  25.1 19.2 %copy-start.4 = (s32[1,1,256]{2,1,0:T(1,128)S(1)}, s32[1,1,256]{2,1,0:T(1,128)}, u32[]{:S(2)}) copy-start(s32[1,1,256]{2,1,0:T(1,128)} %cells.1) | copy-start | bytes 3076

commit v2 on v1

v2 whole, which is shorter than its diff:
```python
import functools
import math

import jax
import jax.numpy as jnp
import numpy as np
from jax import lax
from jax.experimental import pallas as pl
from jax.experimental.pallas import tpu as pltpu
from jax.sharding import PartitionSpec as P

BIN_DEV = 8
LANES = 128
TILE = 8
EDGE = 3
SLOT = 8

ALPHA_FILTER = 0.495
COEF_ZERO = 11.0 / 16.0 + 5.0 * ALPHA_FILTER / 8.0
COEF_ONE = 15.0 / 32.0 + 17.0 * ALPHA_FILTER / 16.0
COEF_TWO = -3.0 / 16.0 + 3.0 * ALPHA_FILTER / 8.0
COEF_THREE = 1.0 / 32.0 - ALPHA_FILTER / 16.0
ALPHA_DERIV = 1.0 / 3.0
NEAR_COEF = 14.0 / 9.0
FAR_COEF = 1.0 / 9.0
AXIAL_STEP = 0.02
RADIAL_STEP = 0.02
INNER_RADIUS = 0.3
SECTION_STEP = 0.004
GAMMA_GAS = 1.4
HIGHEST = lax.Precision.HIGHEST


def kernel_values(count):
    modes = np.arange(count)
    angle = modes * (2.0 * math.pi / count)
    cosine = np.cos(angle)
    filter_gain = (
        COEF_ZERO
        + COEF_ONE * cosine
        + COEF_TWO * np.cos(2.0 * angle)
        + COEF_THREE * np.cos(3.0 * angle)
    ) / (1.0 + 2.0 * ALPHA_FILTER * cosine)
    spacing = 2.0 * math.pi / count
    deriv_gain = (
        filter_gain
        * (NEAR_COEF * np.sin(angle) + 0.5 * FAR_COEF * np.sin(2.0 * angle))
        / (spacing * (1.0 + 2.0 * ALPHA_DERIV * cosine))
    )
    phase = np.mod(modes[:, None] * modes[None, :], count) * (2.0 * math.pi / count)
    smooth = np.sum(filter_gain * np.cos(phase), axis=-1) / count
    slope = -np.sum(deriv_gain * np.sin(phase), axis=-1) / count
    return smooth, slope


def ring_order(count):
    return list(range(0, count, 2)) + list(range(count - 1, 0, -2))


def ring_weights(count):
    order = ring_order(count)
    smooth, slope = kernel_values(count)
    rows = []
    for i in range(count):
        at = order.index(i)
        hops = [0]
        for s in range(1, count // 2):
            hops += [-s, s]
        hops.append(count // 2)
        away = [(i - order[(at + hop) % count]) % count for hop in hops]
        rows.append([smooth[d] for d in away] + [slope[d] for d in away])
    return np.array(rows, np.float32)


def packed_edges(tiles):
    lane = lax.broadcasted_iota(jnp.int32, (TILE, LANES), 1)
    packed = jnp.zeros((TILE, LANES), jnp.float32)
    for k, tile in enumerate(tiles):
        moved = pltpu.roll(tile, (SLOT * k + EDGE) % LANES, 1)
        packed = jnp.where(lax.shift_right_logical(lane, 3) == k, moved, packed)
    return packed


def edges_body(source, edges):
    fields, radial = source.shape[0], source.shape[2]
    for field in range(fields):
        tiles = [source[field, 0, pl.ds(row, TILE), :] for row in range(0, radial, TILE)]
        edges[field] = packed_edges(tiles)


def partial_body(blocks, weights, source, *refs):
    count = weights.shape[1] // 2
    halves, (smooth, slope, edges) = refs[: 2 * blocks], refs[2 * blocks :]
    fields, radial = source.shape[0], source.shape[2]
    half = halves[0].shape[0]
    for field in range(fields):
        tiles = []
        for row in range(0, radial, TILE):
            at = field * radial + row
            value = source[field, 0, pl.ds(row, TILE), :]
            first, second = weights[0, 0] * value, weights[0, count] * value
            for k in range(blocks):
                value = halves[2 * k + at // half][pl.ds(at % half, TILE), :]
                first = first + weights[0, 1 + k] * value
                second = second + weights[0, count + 1 + k] * value
            smooth[pl.ds(at, TILE), :] = first
            slope[pl.ds(at, TILE), :] = second
            tiles.append(first)
        edges[field] = packed_edges(tiles)


def final_body(
    devices,
    weights,
    live_count,
    smooth,
    slope,
    last_first,
    last_second,
    raw_before,
    raw_after,
    sum_before,
    sum_after,
    density,
    velocity,
    pressure,
    cells,
    bins,
    slot_weights,
    section,
    totals,
    filtered,
    picked,
):
    fields, radial = section.shape[0], section.shape[2]
    count = weights.shape[1] // 2
    half = last_first.shape[0]
    last_weight, last_slope = weights[0, count - 1], weights[0, 2 * count - 1]

    def last(at):
        source = last_first if at < half else last_second
        return source[pl.ds(at % half, TILE), :]

    lane = lax.broadcasted_iota(jnp.int32, (TILE, LANES), 1)
    sub = lax.broadcasted_iota(jnp.int32, (TILE, LANES), 0)
    pad = jnp.zeros((TILE, LANES), jnp.float32)
    halos = []
    for field in range(fields):
        filtered[field, pl.ds(0, TILE), :] = pad
        filtered[field, pl.ds(TILE + radial, TILE), :] = pad
        for row in range(0, radial, TILE):
            at = field * radial + row
            value = smooth[pl.ds(at, TILE), :] + last_weight * last(at)
            filtered[field, pl.ds(TILE + row, TILE), :] = value
        before = sum_before[field] + last_weight * raw_before[field]
        after = sum_after[field] + last_weight * raw_after[field]
        halos.append(jnp.where((lane & (SLOT - 1)) < EDGE, before, after))

    unit = SECTION_STEP / (60.0 * AXIAL_STEP)
    axial = [np.float32(c * unit) for c in (45.0, -9.0, 1.0)]
    unit = SECTION_STEP / (60.0 * RADIAL_STEP)
    radially = [np.float32(c * unit) for c in (45.0, -9.0, 1.0)]

    for row in range(0, radial, TILE):
        rows = pl.ds(row, TILE)
        middle, g, e, s = [], [], [], []
        cell_radius = INNER_RADIUS + ((sub + row).astype(jnp.float32) + 0.5) * RADIAL_STEP
        stretch = SECTION_STEP / cell_radius
        for field in range(fields):
            here = filtered[field, pl.ds(TILE + row, TILE), :]
            edge = pltpu.roll(halos[field], LANES - (SLOT * (row // TILE) + EDGE), 1)
            total = None
            for k in range(1, EDGE + 1):
                ahead = pltpu.roll(jnp.where(lane < k, edge, here), LANES - k, 1)
                behind = pltpu.roll(jnp.where(lane >= LANES - k, edge, here), k, 1)
                term = axial[k - 1] * (ahead - behind)
                total = term if total is None else total + term
            g.append(total)
            total = None
            for k in range(1, EDGE + 1):
                above = filtered[field, pl.ds(TILE + row + k, TILE), :]
                below = filtered[field, pl.ds(TILE + row - k, TILE), :]
                term = radially[k - 1] * (above - below)
                total = term if total is None else total + term
            e.append(total)
            at = field * radial + row
            s.append((slope[pl.ds(at, TILE), :] + last_slope * last(at)) * stretch)
            middle.append(here)
        rho = density[0, rows, :]
        u, v, w = (velocity[i, 0, rows, :] for i in range(3))
        stiff = GAMMA_GAS * pressure[0, rows, :]
        inverse = 1.0 / rho
        moved = [u * g[i] + v * e[i] + w * s[i] for i in range(fields)]
        out = [
            middle[0] + moved[0],
            middle[1] + (moved[1] + rho * g[0] + stiff * g[4]),
            middle[2] + (moved[2] + rho * e[0] + stiff * e[4]),
            middle[3] + (moved[3] + rho * s[0] + stiff * s[4]),
            middle[4] + (moved[4] + inverse * (g[1] + e[2] + s[3])),
        ]
        for field in range(fields):
            section[field, 0, rows, :] = out[field]
        picked[rows, :] = out[4] + out[1]

    slots = cells.shape[2]
    cell = cells[0]
    shift = LANES.bit_length() - 1
    column = lax.broadcasted_iota(jnp.int32, (LANES, slots), 0)
    chosen = jnp.where(column == (cell & (LANES - 1)), 1.0, 0.0)
    lines = jnp.dot(picked[...], chosen, precision=HIGHEST, preferred_element_type=jnp.float32)
    line = lax.broadcasted_iota(jnp.int32, (radial, slots), 0)
    lines = jnp.where(line == lax.shift_right_logical(cell, shift), lines, 0.0)
    values = slot_weights[0] * jnp.sum(lines, axis=0, keepdims=True)
    order = lax.broadcasted_iota(jnp.int32, (1, slots), 1)
    values = jnp.where(order < live_count[0, 0], values, 0.0)
    own_bin = bins[0]
    owner = lax.broadcasted_iota(jnp.int32, (devices, slots), 0)
    spread = jnp.where(owner == own_bin // BIN_DEV, values, 0.0)
    place = lax.broadcasted_iota(jnp.int32, (LANES, slots), 0)
    within = jnp.where(place == own_bin % BIN_DEV, 1.0, 0.0)
    totals[...] = lax.dot_general(
        spread,
        within,
        (((1,), (1,)), ((), ())),
        precision=HIGHEST,
        preferred_element_type=jnp.float32,
    )


def in_vmem(count):
    return [pl.BlockSpec(memory_space=pltpu.VMEM)] * count


def in_smem(count):
    return [pl.BlockSpec(memory_space=pltpu.SMEM)] * count


def local(adjoint, density, velocity, pressure, fwh_cell, fwh_bin, fwh_weight, fwh_count):
    fields, local_theta, radial, axial_cells = adjoint.shape
    thetas, blocks_x = lax.axis_size("az"), lax.axis_size("rx")
    devices = thetas * blocks_x
    assert local_theta == 1 and axial_cells == LANES and thetas % 2 == 0
    assert radial % TILE == 0 and radial // TILE * SLOT <= LANES
    params = pltpu.CompilerParams(vmem_limit_bytes=40 * 1024 * 1024)
    f32 = jnp.float32
    rows = fields * radial
    half = rows // 2
    edge_shape = jax.ShapeDtypeStruct((fields, TILE, LANES), f32)

    table = jnp.asarray(ring_weights(thetas))
    weights = lax.dynamic_slice_in_dim(table, lax.axis_index("az"), 1, axis=0)

    order = ring_order(thetas)
    onward = [(order[i], order[(i + 1) % thetas]) for i in range(thetas)]
    back = [(b, a) for a, b in onward]
    across = {order[i]: order[(i + thetas // 2) % thetas] for i in range(thetas)}

    flat = adjoint.reshape(rows, LANES)
    own = [flat[:half], flat[half:]]
    edges = pl.pallas_call(
        edges_body,
        out_shape=edge_shape,
        in_specs=in_vmem(1),
        out_specs=in_vmem(1)[0],
        compiler_params=params,
        name="edges",
    )(adjoint)

    def beyond(step):
        return [
            (i * blocks_x + b, across[i] * blocks_x + b + step)
            for i in range(thetas)
            for b in range(blocks_x)
            if 0 <= b + step < blocks_x
        ]

    from_left, from_right, halves = list(own), list(own), []
    raw_before = raw_after = None
    for step in range(1, thetas // 2):
        left, right = [], []
        for part in range(2):
            left.append(lax.ppermute(from_left[part], "az", onward))
            right.append(lax.ppermute(from_right[part], "az", back))
        from_left, from_right = left, right
        halves += left + right
        if step == 1:
            raw_before = lax.ppermute(edges, ("az", "rx"), beyond(1))
            raw_after = lax.ppermute(edges, ("az", "rx"), beyond(-1))
    last_first = lax.ppermute(from_left[0], "az", onward)
    last_second = lax.ppermute(from_right[1], "az", back)

    blocks = len(halves) // 2
    smooth, slope, sums = pl.pallas_call(
        functools.partial(partial_body, blocks),
        out_shape=(
            jax.ShapeDtypeStruct((rows, LANES), f32),
            jax.ShapeDtypeStruct((rows, LANES), f32),
            edge_shape,
        ),
        in_specs=in_smem(1) + in_vmem(1 + 2 * blocks),
        out_specs=tuple(in_vmem(3)),
        compiler_params=params,
        name="partial",
    )(weights, adjoint, *halves)
    up = [(i, i + 1) for i in range(blocks_x - 1)]
    down = [(j, i) for i, j in up]
    sum_before, sum_after = lax.ppermute(sums, "rx", up), lax.ppermute(sums, "rx", down)

    section, totals = pl.pallas_call(
        functools.partial(final_body, devices),
        out_shape=(
            jax.ShapeDtypeStruct(adjoint.shape, f32),
            jax.ShapeDtypeStruct((devices, LANES), f32),
        ),
        in_specs=in_smem(2) + in_vmem(14),
        out_specs=tuple(in_vmem(2)),
        scratch_shapes=[
            pltpu.VMEM((fields, radial + 2 * TILE, LANES), f32),
            pltpu.VMEM((radial, LANES), f32),
        ],
        compiler_params=params,
        name="section",
    )(
        weights,
        fwh_count,
        smooth,
        slope,
        last_first,
        last_second,
        raw_before,
        raw_after,
        sum_before,
        sum_after,
        density,
        velocity,
        pressure,
        fwh_cell,
        fwh_bin,
        fwh_weight,
    )
    totals = lax.all_to_all(totals, ("az", "rx"), 0, 0, tiled=True)
    return section, jnp.sum(totals, axis=0)[:BIN_DEV]


def solution(mesh):
    placed = (
        P(None, "az", None, "rx"),
        P("az", None, "rx"),
        P(None, "az", None, "rx"),
        P("az", None, "rx"),
        P("az", "rx", None),
        P("az", "rx", None),
        P("az", "rx", None),
        P("az", "rx"),
    )
    return jax.shard_map(
        local,
        mesh=mesh,
        in_specs=placed,
        out_specs=(P(None, "az", None, "rx"), P(("az", "rx"))),
        check_vma=False,
    )
```

time: 57.3 us -> 62.9 us (1.098)
  starting transfers between devices: 2.77 us -> 28.4 us
  blocking collectives: 29.6 us -> 14 us
  waiting for transfers between devices: 18.5 us -> 11.2 us
  local copies, waits for them, and re-layouts: 0.99 us -> 2.42 us
  Pallas kernels: 3.26 us -> 4.54 us
    ppermute x0 -> x18, starting transfers between devices: none -> 28.4 us  [the longest x6 11.3 us: local(): left.append(lax.ppermute(from_left[part], 'az', onward))]
    all_to_all x1 -> x0, blocking collectives: 19.1 us -> none  [local(): pieces = lax.all_to_all(pieces, group, 0, 0, tiled=True)]
    all_to_all x1 -> x0, waiting for transfers between devices: 18.5 us -> none  [local(): pieces = lax.all_to_all(pieces, group, 0, 0, tiled=True)]
    ppermute x0 -> x18, waiting for transfers between devices: none -> 11.2 us  [the longest x6 6.65 us: local(): right.append(lax.ppermute(from_right[part], 'az', back))]
    all_to_all x1, blocking collectives: 10.5 us -> 14 us  [local(): totals = lax.all_to_all(totals, ('az', 'rx'), 0, 0, tiled=True)]
    all_to_all x1 -> x0, starting transfers between devices: 2.77 us -> none  [local(): pieces = lax.all_to_all(pieces, group, 0, 0, tiled=True)]
    pallas_call x3, Pallas kernels: 3.26 us -> 4.54 us  [the longest x1 3.47 us: local(): pl.pallas_call(functools.partial(final_body, devices), out_shape=(jax.Sha...]
    slice x0 -> x1, local copies, waits for them, and re-layouts: none -> 1.06 us  [local(): own = [flat[:half], flat[half:]]]
  transfers between devices with their start and end apart: 1 -> 18, of which waited for: 1 -> 4; matrix products, arithmetic and copies ran while one was open for 0% -> 1% of each run, Pallas kernels for 0% -> 2%
where the time goes in v2:
time: 62.9 us; the launch traced here: 62.6 us
  starting transfers between devices  28.4 us (45%)
  blocking collectives  14 us (22%)
  waiting for transfers between devices  11.2 us (18%)
  Pallas kernels  4.54 us (7%)
  local copies, waits for them, and re-layouts  2.42 us (4%)
  between operations  1.44 us (2%)
    all_to_all x1, blocking collectives, local(): totals = lax.all_to_all(totals, ('az', 'rx'), 0, 0, tiled=True)  14 us
    ppermute x6, starting transfers between devices, local(): left.append(lax.ppermute(from_left[part], 'az', onward))  11.3 us
    ppermute x1, starting transfers between devices, local(): lax.ppermute(sums, 'rx', up)  7.55 us
    ppermute x6, waiting for transfers between devices, local(): right.append(lax.ppermute(from_right[part], 'az', back))  6.65 us
    pallas_call x1, Pallas kernels, local(): pl.pallas_call(functools.partial(final_body, devices), out_shape=(jax.Sha...  3.47 us
    ppermute x6, waiting for transfers between devices, local(): left.append(lax.ppermute(from_left[part], 'az', onward))  2.58 us
    ppermute x1, starting transfers between devices, local(): raw_before = lax.ppermute(edges, ('az', 'rx'), beyond(1))  2.49 us
    ppermute x6, starting transfers between devices, local(): right.append(lax.ppermute(from_right[part], 'az', back))  2.39 us
  transfers between devices with their start and end apart: 18, of which 4 were waited for; matrix products, arithmetic and copies ran while one was open for 1% of the time, Pallas kernels for 2%

profile of v2, /device:TPU:0, one launch (start us, length us, event | category | flops | bytes accessed | tf_op | source)
XLA Modules:
  0.0 62.6 jit_solution(16764148176726178320)
XLA Ops:
  0.6 1.1 %fusion = (f32[320,128]{1,0:T(8,128)S(1)}, f32[320,128]{1,0:T(8,128)S(1)}) fusion(f32[640,128]{1,0:T(8,128)} %bitcast.5), kind=kLoop, calls=%fused_computation.1 | loop fusion | bytes 655360 | tf_op jit(solution)/shard_map/slice | solution.py:259
  1.7 3.1 %collective-permute-start = (f32[320,128]{1,0:T(8,128)S(1)}, f32[320,128]{1,0:T(8,128)S(1)}, u32[]{:S(2)}, u32[]{:S(2)}) collective-permute-start(f32[320,128]{1,0:T(8,128)S(1)} %get-tuple-element.13), channel_id=1, source_target_pairs={{0,8},{8,16},{16,24},{24,28},{28,20},{20,12},{12,4},{4,0},{1,9},{9... | collective-permute-start | bytes 491528 | tf_op jit(solution)/shard_map/ppermute | solution.py:282
  4.8 1.9 %collective-permute-start.2 = (f32[320,128]{1,0:T(8,128)S(1)}, f32[320,128]{1,0:T(8,128)S(1)}, u32[]{:S(2)}, u32[]{:S(2)}) collective-permute-start(f32[320,128]{1,0:T(8,128)S(1)} %get-tuple-element.13), channel_id=1, source_target_pairs={{8,0},{16,8},{24,16},{28,24},{20,28},{12,20},{4,12},{0,4},{9,1},{1... | collective-permute-start | bytes 491528 | tf_op jit(solution)/shard_map/ppermute | solution.py:283
  6.7 0.1 collective-permute-start.1
  6.8 2.6 %collective-permute-done.refs_0_ = f32[320,128]{1,0:T(8,128)S(1)} collective-permute-done((f32[320,128]{1,0:T(8,128)S(1)}, f32[320,128]{1,0:T(8,128)S(1)}, u32[]{:S(2)}, u32[]{:S(2)}) %collective-permute-start) | collective-permute-done | bytes 163872 | tf_op jit(solution)/shard_map/ppermute | solution.py:282
  9.4 2.5 %collective-permute-start.4 = (f32[320,128]{1,0:T(8,128)S(1)}, f32[320,128]{1,0:T(8,128)S(1)}, u32[]{:S(2)}, u32[]{:S(2)}) collective-permute-start(f32[320,128]{1,0:T(8,128)S(1)} %collective-permute-done.refs_0_), channel_id=1, source_target_pairs={{0,8},{8,16},{16,24},{24,28},{28,20},{20,12},{12,4},{4,0},{1,9},{9... | collective-permute-start | bytes 491528 | tf_op jit(solution)/shard_map/ppermute | solution.py:282
  11.9 0.0 collective-permute-done.3.refs_3_
  11.9 3.5 %collective-permute-done.2.refs_2_ = f32[320,128]{1,0:T(8,128)S(1)} collective-permute-done((f32[320,128]{1,0:T(8,128)S(1)}, f32[320,128]{1,0:T(8,128)S(1)}, u32[]{:S(2)}, u32[]{:S(2)}) %collective-permute-start.2) | collective-permute-done | bytes 163872 | tf_op jit(solution)/shard_map/ppermute | solution.py:283
  15.4 2.0 %collective-permute-start.5 = (f32[320,128]{1,0:T(8,128)S(1)}, f32[320,128]{1,0:T(8,128)S(1)}, u32[]{:S(2)}, u32[]{:S(2)}) collective-permute-start(f32[320,128]{1,0:T(8,128)S(1)} %collective-permute-done.1.refs_1_), channel_id=1, source_target_pairs={{0,8},{8,16},{16,24},{24,28},{28,20},{20,12},{12,4},{4,0},{1,9},{9... | collective-permute-start | bytes 491528 | tf_op jit(solution)/shard_map/ppermute | solution.py:282
  17.5 1.6 %collective-permute-start.8 = (f32[320,128]{1,0:T(8,128)S(1)}, f32[320,128]{1,0:T(8,128)S(1)}, u32[]{:S(2)}, u32[]{:S(2)}) collective-permute-start(f32[320,128]{1,0:T(8,128)S(1)} %collective-permute-done.4.refs_4_), channel_id=1, source_target_pairs={{0,8},{8,16},{16,24},{24,28},{28,20},{20,12},{12,4},{4,0},{1,9},{9... | collective-permute-start | bytes 491528 | tf_op jit(solution)/shard_map/ppermute | solution.py:282
  19.0 0.0 collective-permute-done.7.refs_7_
  19.0 0.4 collective-permute-start.11
  19.5 3.1 %collective-permute-done.6.refs_6_ = f32[320,128]{1,0:T(8,128)S(1)} collective-permute-done((f32[320,128]{1,0:T(8,128)S(1)}, f32[320,128]{1,0:T(8,128)S(1)}, u32[]{:S(2)}, u32[]{:S(2)}) %collective-permute-start.6) | collective-permute-done | bytes 163872 | tf_op jit(solution)/shard_map/ppermute | solution.py:283
  22.6 0.0 collective-permute-start.10
  22.6 2.0 %collective-permute-start.9 = (f32[320,128]{1,0:T(8,128)S(1)}, f32[320,128]{1,0:T(8,128)S(1)}, u32[]{:S(2)}, u32[]{:S(2)}) collective-permute-start(f32[320,128]{1,0:T(8,128)S(1)} %collective-permute-done.5.refs_5_), channel_id=1, source_target_pairs={{0,8},{8,16},{16,24},{24,28},{28,20},{20,12},{12,4},{4,0},{1,9},{9... | collective-permute-start | bytes 491528 | tf_op jit(solution)/shard_map/ppermute | solution.py:282
  24.6 1.6 %collective-permute-start.12 = (f32[320,128]{1,0:T(8,128)S(1)}, f32[320,128]{1,0:T(8,128)S(1)}, u32[]{:S(2)}, u32[]{:S(2)}) collective-permute-start(f32[320,128]{1,0:T(8,128)S(1)} %collective-permute-done.8.refs_8_), channel_id=1, source_target_pairs={{0,8},{8,16},{16,24},{24,28},{28,20},{20,12},{12,4},{4,0},{1,9},{9... | collective-permute-start | bytes 491528 | tf_op jit(solution)/shard_map/ppermute | solution.py:289
  26.2 0.0 collective-permute-done.11.refs_11_
  26.2 0.4 collective-permute-start.13
  26.6 0.1 edges.1
  26.8 2.5 %collective-permute-start.14 = (f32[5,8,128]{2,1,0:T(8,128)S(1)}, f32[5,8,128]{2,1,0:T(8,128)S(1)}, u32[]{:S(2)}, u32[]{:S(2)}) collective-permute-start(f32[5,8,128]{2,1,0:T(8,128)S(1)} %edges.1), channel_id=1, source_target_pairs={{0,29},{1,30},{2,31},{4,25},{5,26},{6,27},{8,21},{9,22},{10,23},{1... | collective-permute-start | bytes 61448 | tf_op jit(solution)/shard_map/ppermute | solution.py:287
  29.3 0.7 %constant_dynamic-slice_fusion.weights = f32[1,16]{1,0:T(1,128)S(1)} fusion(f32[8,16]{1,0:T(8,128)} %constant.14.clone, s32[]{:T(128)S(6)} %select_n.3), kind=kLoop, calls=%fused_computation | loop fusion | bytes 132 | tf_op jit(solution)/shard_map/dynamic_slice | solution.py:251
  30.0 1.4 %collective-permute-start.15 = (f32[5,8,128]{2,1,0:T(8,128)S(1)}, f32[5,8,128]{2,1,0:T(8,128)S(1)}, u32[]{:S(2)}, u32[]{:S(2)}) collective-permute-start(f32[5,8,128]{2,1,0:T(8,128)S(1)} %edges.1), channel_id=1, source_target_pairs={{1,28},{2,29},{3,30},{5,24},{6,25},{7,26},{9,20},{10,21},{11,22},{... | collective-permute-start | bytes 61448 | tf_op jit(solution)/shard_map/ppermute | solution.py:288
  31.4 0.0 copy-start.5
  31.4 0.0 copy-start.6
  31.5 0.9 %partial.1 = (f32[640,128]{1,0:T(8,128)S(1)}, f32[640,128]{1,0:T(8,128)S(1)}, f32[5,8,128]{2,1,0:T(8,128)S(1)}) custom-call(f32[1,16]{1,0:T(1,128)S(1)} %constant_dynamic-slice_fusion.weights, f32[5,1,128,128]{3,2,1,0:T(8,128)S(1)} %copy-done, f32[320,128]{1,0:T(8,128)S(1)} %collective-permute-done.refs_0_, f32[320,128]{1,0:T(8,128)S(1)} %collective-permute-done.1.refs_1_, ...), custom_call_target="tpu_custom_call" | custom-call | tf_op jit(solution)/shard_map/partial/pallas_call | solution.py:293
  32.4 7.6 %collective-permute-start.16 = (f32[5,8,128]{2,1,0:T(8,128)S(1)}, f32[5,8,128]{2,1,0:T(8,128)S(1)}, u32[]{:S(2)}, u32[]{:S(2)}) collective-permute-start(f32[5,8,128]{2,1,0:T(8,128)S(1)} %get-tuple-element.9), channel_id=1, source_target_pairs={{0,1},{1,2},{2,3},{4,5},{5,6},{6,7},{8,9},{9,10},{10,11},{12,13},{... | collective-permute-start | bytes 61448 | tf_op jit(solution)/shard_map/ppermute | solution.py:307
  40.0 1.3 %collective-permute-start.17 = (f32[5,8,128]{2,1,0:T(8,128)S(1)}, f32[5,8,128]{2,1,0:T(8,128)S(1)}, u32[]{:S(2)}, u32[]{:S(2)}) collective-permute-start(f32[5,8,128]{2,1,0:T(8,128)S(1)} %get-tuple-element.9), channel_id=1, source_target_pairs={{1,0},{2,1},{3,2},{5,4},{6,5},{7,6},{9,8},{10,9},{11,10},{13,12},{... | collective-permute-start | bytes 61448 | tf_op jit(solution)/shard_map/ppermute | solution.py:307
  41.9 2.0 %collective-permute-done.17.sum_after = f32[5,8,128]{2,1,0:T(8,128)S(1)} collective-permute-done((f32[5,8,128]{2,1,0:T(8,128)S(1)}, f32[5,8,128]{2,1,0:T(8,128)S(1)}, u32[]{:S(2)}, u32[]{:S(2)}) %collective-permute-start.17) | collective-permute-done | bytes 20512 | tf_op jit(solution)/shard_map/ppermute | solution.py:307
  44.0 0.6 %copy-done.4 = s32[1,1,256]{2,1,0:T(1,128)S(1)} copy-done((s32[1,1,256]{2,1,0:T(1,128)S(1)}, s32[1,1,256]{2,1,0:T(1,128)}, u32[]{:S(2)}) %copy-start.4) | copy-done | bytes 1048
  44.6 3.5 %section.1 = (f32[5,1,128,128]{3,2,1,0:T(8,128)}, f32[32,128]{1,0:T(8,128)S(1)}) custom-call(f32[1,16]{1,0:T(1,128)S(1)} %constant_dynamic-slice_fusion.weights, s32[1,1]{1,0:T(1,128)S(6)} %copy.12.live_count, f32[640,128]{1,0:T(8,128)S(1)} %get-tuple-element.7.smooth, f32[640,128]{1,0:T(8,128)S(1)} %get-tuple-element.8.slope, ...), custom_call_target="tpu_custom_call" | custom-call | tf_op jit(solution)/shard_map/section/pallas_call | solution.py:309
  48.1 14.0 %all_to_all.9 = f32[32,1,128]{2,1,0:T(1,128)S(1)} all-to-all(f32[32,1,128]{2,1,0:T(1,128)S(1)} %bitcast.6), channel_id=1, replica_groups=mesh['az'=8,'rx'=4] {'az','rx'}, dimensions={0} | all-to-all | bytes 32768 | tf_op jit(solution)/shard_map/all_to_all | solution.py:341
  62.0 0.6 reduce_sum.9
  (25 shorter events, 0.1 us)
Async XLA Ops:
  0.6 26.0 %copy-start = (f32[5,1,128,128]{3,2,1,0:T(8,128)S(1)}, f32[5,1,128,128]{3,2,1,0:T(8,128)}, u32[]{:S(2)}) copy-start(f32[5,1,128,128]{3,2,1,0:T(8,128)} %source.3) | copy-start | bytes 983044
  1.7 7.7 %collective-permute-start = (f32[320,128]{1,0:T(8,128)S(1)}, f32[320,128]{1,0:T(8,128)S(1)}, u32[]{:S(2)}, u32[]{:S(2)}) collective-permute-start(f32[320,128]{1,0:T(8,128)S(1)} %get-tuple-element.13), channel_id=1, source_target_pairs={{0,8},{8,16},{16,24},{24,28},{28,20},{20,12},{12,4},{4,0},{1,9},{9... | collective-permute-start | bytes 491528 | tf_op jit(solution)/shard_map/ppermute | solution.py:282
  4.8 7.1 %collective-permute-start.3 = (f32[320,128]{1,0:T(8,128)S(1)}, f32[320,128]{1,0:T(8,128)S(1)}, u32[]{:S(2)}, u32[]{:S(2)}) collective-permute-start(f32[320,128]{1,0:T(8,128)S(1)} %get-tuple-element.12), channel_id=1, source_target_pairs={{8,0},{16,8},{24,16},{28,24},{20,28},{12,20},{4,12},{0,4},{9,1},{1... | collective-permute-start | bytes 491528 | tf_op jit(solution)/shard_map/ppermute | solution.py:283
  4.8 10.6 %collective-permute-start.2 = (f32[320,128]{1,0:T(8,128)S(1)}, f32[320,128]{1,0:T(8,128)S(1)}, u32[]{:S(2)}, u32[]{:S(2)}) collective-permute-start(f32[320,128]{1,0:T(8,128)S(1)} %get-tuple-element.13), channel_id=1, source_target_pairs={{8,0},{16,8},{24,16},{28,24},{20,28},{12,20},{4,12},{0,4},{9,1},{1... | collective-permute-start | bytes 491528 | tf_op jit(solution)/shard_map/ppermute | solution.py:283
  6.7 8.7 %collective-permute-start.1 = (f32[320,128]{1,0:T(8,128)S(1)}, f32[320,128]{1,0:T(8,128)S(1)}, u32[]{:S(2)}, u32[]{:S(2)}) collective-permute-start(f32[320,128]{1,0:T(8,128)S(1)} %get-tuple-element.12), channel_id=1, source_target_pairs={{0,8},{8,16},{16,24},{24,28},{28,20},{20,12},{12,4},{4,0},{1,9},{9... | collective-permute-start | bytes 491528 | tf_op jit(solution)/shard_map/ppermute | solution.py:282
  9.4 8.0 %collective-permute-start.4 = (f32[320,128]{1,0:T(8,128)S(1)}, f32[320,128]{1,0:T(8,128)S(1)}, u32[]{:S(2)}, u32[]{:S(2)}) collective-permute-start(f32[320,128]{1,0:T(8,128)S(1)} %collective-permute-done.refs_0_), channel_id=1, source_target_pairs={{0,8},{8,16},{16,24},{24,28},{28,20},{20,12},{12,4},{4,0},{1,9},{9... | collective-permute-start | bytes 491528 | tf_op jit(solution)/shard_map/ppermute | solution.py:282
  11.9 7.1 %collective-permute-start.7 = (f32[320,128]{1,0:T(8,128)S(1)}, f32[320,128]{1,0:T(8,128)S(1)}, u32[]{:S(2)}, u32[]{:S(2)}) collective-permute-start(f32[320,128]{1,0:T(8,128)S(1)} %collective-permute-done.3.refs_3_), channel_id=1, source_target_pairs={{8,0},{16,8},{24,16},{28,24},{20,28},{12,20},{4,12},{0,4},{9,1},{1... | collective-permute-start | bytes 491528 | tf_op jit(solution)/shard_map/ppermute | solution.py:283
  15.4 7.1 %collective-permute-start.6 = (f32[320,128]{1,0:T(8,128)S(1)}, f32[320,128]{1,0:T(8,128)S(1)}, u32[]{:S(2)}, u32[]{:S(2)}) collective-permute-start(f32[320,128]{1,0:T(8,128)S(1)} %collective-permute-done.2.refs_2_), channel_id=1, source_target_pairs={{8,0},{16,8},{24,16},{28,24},{20,28},{12,20},{4,12},{0,4},{9,1},{1... | collective-permute-start | bytes 491528 | tf_op jit(solution)/shard_map/ppermute | solution.py:283
  15.4 7.1 %collective-permute-start.5 = (f32[320,128]{1,0:T(8,128)S(1)}, f32[320,128]{1,0:T(8,128)S(1)}, u32[]{:S(2)}, u32[]{:S(2)}) collective-permute-start(f32[320,128]{1,0:T(8,128)S(1)} %collective-permute-done.1.refs_1_), channel_id=1, source_target_pairs={{0,8},{8,16},{16,24},{24,28},{28,20},{20,12},{12,4},{4,0},{1,9},{9... | collective-permute-start | bytes 491528 | tf_op jit(solution)/shard_map/ppermute | solution.py:282
  17.5 7.1 %collective-permute-start.8 = (f32[320,128]{1,0:T(8,128)S(1)}, f32[320,128]{1,0:T(8,128)S(1)}, u32[]{:S(2)}, u32[]{:S(2)}) collective-permute-start(f32[320,128]{1,0:T(8,128)S(1)} %collective-permute-done.4.refs_4_), channel_id=1, source_target_pairs={{0,8},{8,16},{16,24},{24,28},{28,20},{20,12},{12,4},{4,0},{1,9},{9... | collective-permute-start | bytes 491528 | tf_op jit(solution)/shard_map/ppermute | solution.py:282
  19.0 7.1 %collective-permute-start.11 = (f32[320,128]{1,0:T(8,128)S(1)}, f32[320,128]{1,0:T(8,128)S(1)}, u32[]{:S(2)}, u32[]{:S(2)}) collective-permute-start(f32[320,128]{1,0:T(8,128)S(1)} %collective-permute-done.7.refs_7_), channel_id=1, source_target_pairs={{8,0},{16,8},{24,16},{28,24},{20,28},{12,20},{4,12},{0,4},{9,1},{1... | collective-permute-start | bytes 491528 | tf_op jit(solution)/shard_map/ppermute | solution.py:283
  22.6 7.4 %collective-permute-start.10 = (f32[320,128]{1,0:T(8,128)S(1)}, f32[320,128]{1,0:T(8,128)S(1)}, u32[]{:S(2)}, u32[]{:S(2)}) collective-permute-start(f32[320,128]{1,0:T(8,128)S(1)} %collective-permute-done.6.refs_6_), channel_id=1, source_target_pairs={{8,0},{16,8},{24,16},{28,24},{20,28},{12,20},{4,12},{0,4},{9,1},{1... | collective-permute-start | bytes 491528 | tf_op jit(solution)/shard_map/ppermute | solution.py:283
  22.6 8.9 %collective-permute-start.9 = (f32[320,128]{1,0:T(8,128)S(1)}, f32[320,128]{1,0:T(8,128)S(1)}, u32[]{:S(2)}, u32[]{:S(2)}) collective-permute-start(f32[320,128]{1,0:T(8,128)S(1)} %collective-permute-done.5.refs_5_), channel_id=1, source_target_pairs={{0,8},{8,16},{16,24},{24,28},{28,20},{20,12},{12,4},{4,0},{1,9},{9... | collective-permute-start | bytes 491528 | tf_op jit(solution)/shard_map/ppermute | solution.py:282
  24.6 19.3 %collective-permute-start.12 = (f32[320,128]{1,0:T(8,128)S(1)}, f32[320,128]{1,0:T(8,128)S(1)}, u32[]{:S(2)}, u32[]{:S(2)}) collective-permute-start(f32[320,128]{1,0:T(8,128)S(1)} %collective-permute-done.8.refs_8_), channel_id=1, source_target_pairs={{0,8},{8,16},{16,24},{24,28},{28,20},{20,12},{12,4},{4,0},{1,9},{9... | collective-permute-start | bytes 491528 | tf_op jit(solution)/shard_map/ppermute | solution.py:289
  26.2 17.7 %collective-permute-start.13 = (f32[320,128]{1,0:T(8,128)S(1)}, f32[320,128]{1,0:T(8,128)S(1)}, u32[]{:S(2)}, u32[]{:S(2)}) collective-permute-start(f32[320,128]{1,0:T(8,128)S(1)} %collective-permute-done.11.refs_11_), channel_id=1, source_target_pairs={{8,0},{16,8},{24,16},{28,24},{20,28},{12,20},{4,12},{0,4},{9,1},{1... | collective-permute-start | bytes 491528 | tf_op jit(solution)/shard_map/ppermute | solution.py:290
  26.8 13.2 %collective-permute-start.14 = (f32[5,8,128]{2,1,0:T(8,128)S(1)}, f32[5,8,128]{2,1,0:T(8,128)S(1)}, u32[]{:S(2)}, u32[]{:S(2)}) collective-permute-start(f32[5,8,128]{2,1,0:T(8,128)S(1)} %edges.1), channel_id=1, source_target_pairs={{0,29},{1,30},{2,31},{4,25},{5,26},{6,27},{8,21},{9,22},{10,23},{1... | collective-permute-start | bytes 61448 | tf_op jit(solution)/shard_map/ppermute | solution.py:287
  30.0 14.0 %copy-start.1 = (f32[3,1,128,128]{3,2,1,0:T(8,128)S(1)}, f32[3,1,128,128]{3,2,1,0:T(8,128)}, u32[]{:S(2)}) copy-start(f32[3,1,128,128]{3,2,1,0:T(8,128)} %velocity.1) | copy-start | bytes 589828
  30.0 14.0 %copy-start.2 = (f32[1,128,128]{2,1,0:T(8,128)S(1)}, f32[1,128,128]{2,1,0:T(8,128)}, u32[]{:S(2)}) copy-start(f32[1,128,128]{2,1,0:T(8,128)} %density.1) | copy-start | bytes 196612
  30.0 14.0 %copy-start.3 = (f32[1,128,128]{2,1,0:T(8,128)S(1)}, f32[1,128,128]{2,1,0:T(8,128)}, u32[]{:S(2)}) copy-start(f32[1,128,128]{2,1,0:T(8,128)} %pressure.1) | copy-start | bytes 196612
  30.0 11.9 %collective-permute-start.15 = (f32[5,8,128]{2,1,0:T(8,128)S(1)}, f32[5,8,128]{2,1,0:T(8,128)S(1)}, u32[]{:S(2)}, u32[]{:S(2)}) collective-permute-start(f32[5,8,128]{2,1,0:T(8,128)S(1)} %edges.1), channel_id=1, source_target_pairs={{1,28},{2,29},{3,30},{5,24},{6,25},{7,26},{9,20},{10,21},{11,22},{... | collective-permute-start | bytes 61448 | tf_op jit(solution)/shard_map/ppermute | solution.py:288
  31.4 12.5 %copy-start.5 = (s32[1,1,256]{2,1,0:T(1,128)S(1)}, s32[1,1,256]{2,1,0:T(1,128)}, u32[]{:S(2)}) copy-start(s32[1,1,256]{2,1,0:T(1,128)} %bins.1) | copy-start | bytes 3076
  31.4 12.5 %copy-start.6 = (f32[1,1,256]{2,1,0:T(1,128)S(1)}, f32[1,1,256]{2,1,0:T(1,128)}, u32[]{:S(2)}) copy-start(f32[1,1,256]{2,1,0:T(1,128)} %slot_weights.1) | copy-start | bytes 3076
  32.4 9.5 %collective-permute-start.16 = (f32[5,8,128]{2,1,0:T(8,128)S(1)}, f32[5,8,128]{2,1,0:T(8,128)S(1)}, u32[]{:S(2)}, u32[]{:S(2)}) collective-permute-start(f32[5,8,128]{2,1,0:T(8,128)S(1)} %get-tuple-element.9), channel_id=1, source_target_pairs={{0,1},{1,2},{2,3},{4,5},{5,6},{6,7},{8,9},{9,10},{10,11},{12,13},{... | collective-permute-start | bytes 61448 | tf_op jit(solution)/shard_map/ppermute | solution.py:307
  40.0 4.0 %collective-permute-start.17 = (f32[5,8,128]{2,1,0:T(8,128)S(1)}, f32[5,8,128]{2,1,0:T(8,128)S(1)}, u32[]{:S(2)}, u32[]{:S(2)}) collective-permute-start(f32[5,8,128]{2,1,0:T(8,128)S(1)} %get-tuple-element.9), channel_id=1, source_target_pairs={{1,0},{2,1},{3,2},{5,4},{6,5},{7,6},{9,8},{10,9},{11,10},{13,12},{... | collective-permute-start | bytes 61448 | tf_op jit(solution)/shard_map/ppermute | solution.py:307
  43.9 0.7 %copy-start.4 = (s32[1,1,256]{2,1,0:T(1,128)S(1)}, s32[1,1,256]{2,1,0:T(1,128)}, u32[]{:S(2)}) copy-start(s32[1,1,256]{2,1,0:T(1,128)} %cells.1) | copy-start | bytes 3076

commit v3 on v2

--- a/solution.py
+++ b/solution.py
@@ -28,7 +28,6 @@
 INNER_RADIUS = 0.3
 SECTION_STEP = 0.004
 GAMMA_GAS = 1.4
-HIGHEST = lax.Precision.HIGHEST
 
 
 def kernel_values(count):
@@ -81,20 +80,12 @@
     return packed
 
 
-def edges_body(source, edges):
-    fields, radial = source.shape[0], source.shape[2]
-    for field in range(fields):
-        tiles = [source[field, 0, pl.ds(row, TILE), :] for row in range(0, radial, TILE)]
-        edges[field] = packed_edges(tiles)
-
-
 def partial_body(blocks, weights, source, *refs):
     count = weights.shape[1] // 2
-    halves, (smooth, slope, edges) = refs[: 2 * blocks], refs[2 * blocks :]
+    halves, (smooth, slope) = refs[: 2 * blocks], refs[2 * blocks :]
     fields, radial = source.shape[0], source.shape[2]
     half = halves[0].shape[0]
     for field in range(fields):
-        tiles = []
         for row in range(0, radial, TILE):
             at = field * radial + row
             value = source[field, 0, pl.ds(row, TILE), :]
@@ -105,37 +96,81 @@
                 second = second + weights[0, count + 1 + k] * value
             smooth[pl.ds(at, TILE), :] = first
             slope[pl.ds(at, TILE), :] = second
-            tiles.append(first)
+
+
+def finish_body(weights, smooth, last_first, last_second, filtered, edges):
+    fields, count = edges.shape[0], weights.shape[1] // 2
+    half = last_first.shape[0]
+    radial = smooth.shape[0] // fields
+    last_weight = weights[0, count - 1]
+    for field in range(fields):
+        tiles = []
+        for row in range(0, radial, TILE):
+            at = field * radial + row
+            source = last_first if at < half else last_second
+            value = smooth[pl.ds(at, TILE), :] + last_weight * source[pl.ds(at % half, TILE), :]
+            filtered[pl.ds(at, TILE), :] = value
+            tiles.append(value)
         edges[field] = packed_edges(tiles)
 
 
+def slots_body(live_count, cells, bins, slot_weights, column, line, owner, place):
+    slots = cells.shape[2]
+    cell, own_bin = cells[0], bins[0]
+    order = lax.broadcasted_iota(jnp.int32, (1, slots), 1)
+    weight = jnp.where(order < live_count[0, 0], slot_weights[0], 0.0)
+
+    def table(target, index, value):
+        rows = lax.broadcasted_iota(jnp.int32, target.shape, 0)
+        target[...] = jnp.where(rows == index, value, 0.0).astype(target.dtype)
+
+    table(column, cell & (LANES - 1), 1.0)
+    table(line, lax.shift_right_logical(cell, LANES.bit_length() - 1), weight)
+    table(owner, own_bin // BIN_DEV, 1.0)
+    table(place, own_bin % BIN_DEV, 1.0)
+
+
+def three_parts(value):
+    parts = []
+    for _ in range(3):
+        part = value.astype(jnp.bfloat16)
+        parts.append(part)
+        value = value - part.astype(jnp.float32)
+    return jnp.concatenate(parts, axis=0)
+
+
+def add_parts(stacked):
+    rows = stacked.shape[0] // 3
+    return stacked[:rows] + (stacked[rows : 2 * rows] + stacked[2 * rows :])
+
+
 def final_body(
-    devices,
+    blocks_x,
     weights,
-    live_count,
+    place_x,
     smooth,
     slope,
     last_first,
     last_second,
-    raw_before,
-    raw_after,
-    sum_before,
-    sum_after,
+    edges_pair,
+    edges_next,
     density,
     velocity,
     pressure,
-    cells,
-    bins,
-    slot_weights,
+    column,
+    line,
+    owner,
+    place,
     section,
     totals,
     filtered,
+    halos,
     picked,
 ):
     fields, radial = section.shape[0], section.shape[2]
     count = weights.shape[1] // 2
     half = last_first.shape[0]
-    last_weight, last_slope = weights[0, count - 1], weights[0, 2 * count - 1]
+    last_slope = weights[0, 2 * count - 1]
 
     def last(at):
         source = last_first if at < half else last_second
@@ -143,18 +178,19 @@
 
     lane = lax.broadcasted_iota(jnp.int32, (TILE, LANES), 1)
     sub = lax.broadcasted_iota(jnp.int32, (TILE, LANES), 0)
+    odd = (place_x[0, 0] & 1) == 1
+    paired = ((lane & (SLOT - 1)) < EDGE) == odd
+    inner = jnp.where((place_x[0, 0] == 0) | (place_x[0, 0] == blocks_x - 1), 0.0, 1.0)
     pad = jnp.zeros((TILE, LANES), jnp.float32)
-    halos = []
     for field in range(fields):
         filtered[field, pl.ds(0, TILE), :] = pad
         filtered[field, pl.ds(TILE + radial, TILE), :] = pad
+        packed = jnp.where(paired, edges_pair[field], inner * edges_next[field])
         for row in range(0, radial, TILE):
             at = field * radial + row
-            value = smooth[pl.ds(at, TILE), :] + last_weight * last(at)
-            filtered[field, pl.ds(TILE + row, TILE), :] = value
-        before = sum_before[field] + last_weight * raw_before[field]
-        after = sum_after[field] + last_weight * raw_after[field]
-        halos.append(jnp.where((lane & (SLOT - 1)) < EDGE, before, after))
+            filtered[field, pl.ds(TILE + row, TILE), :] = smooth[pl.ds(at, TILE), :]
+            edge = pltpu.roll(packed, LANES - (SLOT * (row // TILE) + EDGE), 1)
+            halos[field, pl.ds(row, TILE), :] = edge
 
     unit = SECTION_STEP / (60.0 * AXIAL_STEP)
     axial = [np.float32(c * unit) for c in (45.0, -9.0, 1.0)]
@@ -168,7 +204,7 @@
         stretch = SECTION_STEP / cell_radius
         for field in range(fields):
             here = filtered[field, pl.ds(TILE + row, TILE), :]
-            edge = pltpu.roll(halos[field], LANES - (SLOT * (row // TILE) + EDGE), 1)
+            edge = halos[field, rows, :]
             total = None
             for k in range(1, EDGE + 1):
                 ahead = pltpu.roll(jnp.where(lane < k, edge, here), LANES - k, 1)
@@ -202,29 +238,20 @@
             section[field, 0, rows, :] = out[field]
         picked[rows, :] = out[4] + out[1]
 
-    slots = cells.shape[2]
-    cell = cells[0]
-    shift = LANES.bit_length() - 1
-    column = lax.broadcasted_iota(jnp.int32, (LANES, slots), 0)
-    chosen = jnp.where(column == (cell & (LANES - 1)), 1.0, 0.0)
-    lines = jnp.dot(picked[...], chosen, precision=HIGHEST, preferred_element_type=jnp.float32)
-    line = lax.broadcasted_iota(jnp.int32, (radial, slots), 0)
-    lines = jnp.where(line == lax.shift_right_logical(cell, shift), lines, 0.0)
-    values = slot_weights[0] * jnp.sum(lines, axis=0, keepdims=True)
-    order = lax.broadcasted_iota(jnp.int32, (1, slots), 1)
-    values = jnp.where(order < live_count[0, 0], values, 0.0)
-    own_bin = bins[0]
-    owner = lax.broadcasted_iota(jnp.int32, (devices, slots), 0)
-    spread = jnp.where(owner == own_bin // BIN_DEV, values, 0.0)
-    place = lax.broadcasted_iota(jnp.int32, (LANES, slots), 0)
-    within = jnp.where(place == own_bin % BIN_DEV, 1.0, 0.0)
-    totals[...] = lax.dot_general(
-        spread,
-        within,
-        (((1,), (1,)), ((), ())),
-        precision=HIGHEST,
-        preferred_element_type=jnp.float32,
+    lines = jnp.dot(three_parts(picked[...]), column[...], preferred_element_type=jnp.float32)
+    values = jnp.sum(line[...] * add_parts(lines), axis=0, keepdims=True)
+    spread = three_parts(owner[...] * values)
+    totals[...] = add_parts(
+        lax.dot_general(
+            spread, place[...], (((1,), (1,)), ((), ())), preferred_element_type=jnp.float32
+        )
     )
+
+
+def store_body(source, target, semaphore):
+    copy = pltpu.make_async_copy(source, target, semaphore)
+    copy.start()
+    copy.wait()
 
 
 def in_vmem(count):
@@ -239,106 +266,118 @@
     fields, local_theta, radial, axial_cells = adjoint.shape
     thetas, blocks_x = lax.axis_size("az"), lax.axis_size("rx")
     devices = thetas * blocks_x
-    assert local_theta == 1 and axial_cells == LANES and thetas % 2 == 0
+    assert local_theta == 1 and axial_cells == LANES and thetas % 2 == 0 and blocks_x % 2 == 0
     assert radial % TILE == 0 and radial // TILE * SLOT <= LANES
     params = pltpu.CompilerParams(vmem_limit_bytes=40 * 1024 * 1024)
     f32 = jnp.float32
     rows = fields * radial
-    half = rows // 2
+    half, slots = rows // 2, fwh_cell.shape[2]
     edge_shape = jax.ShapeDtypeStruct((fields, TILE, LANES), f32)
-
-    table = jnp.asarray(ring_weights(thetas))
-    weights = lax.dynamic_slice_in_dim(table, lax.axis_index("az"), 1, axis=0)
 
     order = ring_order(thetas)
     onward = [(order[i], order[(i + 1) % thetas]) for i in range(thetas)]
     back = [(b, a) for a, b in onward]
-    across = {order[i]: order[(i + thetas // 2) % thetas] for i in range(thetas)}
 
     flat = adjoint.reshape(rows, LANES)
     own = [flat[:half], flat[half:]]
-    edges = pl.pallas_call(
-        edges_body,
-        out_shape=edge_shape,
-        in_specs=in_vmem(1),
-        out_specs=in_vmem(1)[0],
-        compiler_params=params,
-        name="edges",
-    )(adjoint)
-
-    def beyond(step):
-        return [
-            (i * blocks_x + b, across[i] * blocks_x + b + step)
-            for i in range(thetas)
-            for b in range(blocks_x)
-            if 0 <= b + step < blocks_x
-        ]
+    steps = thetas // 2 - 1
 
     from_left, from_right, halves = list(own), list(own), []
-    raw_before = raw_after = None
-    for step in range(1, thetas // 2):
+    for step in range(steps):
         left, right = [], []
         for part in range(2):
             left.append(lax.ppermute(from_left[part], "az", onward))
             right.append(lax.ppermute(from_right[part], "az", back))
         from_left, from_right = left, right
-        halves += left + right
+        if step == 0:
+            weights = lax.dynamic_slice_in_dim(
+                jnp.asarray(ring_weights(thetas)), lax.axis_index("az"), 1, axis=0
+            )
+            tables = pl.pallas_call(
+                slots_body,
+                out_shape=(
+                    jax.ShapeDtypeStruct((LANES, slots), jnp.bfloat16),
+                    jax.ShapeDtypeStruct((radial, slots), f32),
+                    jax.ShapeDtypeStruct((devices, slots), f32),
+                    jax.ShapeDtypeStruct((LANES, slots), jnp.bfloat16),
+                ),
+                in_specs=in_smem(1) + in_vmem(3),
+                out_specs=tuple(in_vmem(4)),
+                compiler_params=params,
+                name="slots",
+            )(fwh_count, fwh_cell, fwh_bin, fwh_weight)
         if step == 1:
-            raw_before = lax.ppermute(edges, ("az", "rx"), beyond(1))
-            raw_after = lax.ppermute(edges, ("az", "rx"), beyond(-1))
+            weights, tables, from_right[1] = lax.optimization_barrier(
+                (weights, tables, from_right[1])
+            )
+        halves += from_left + from_right
     last_first = lax.ppermute(from_left[0], "az", onward)
     last_second = lax.ppermute(from_right[1], "az", back)
 
     blocks = len(halves) // 2
-    smooth, slope, sums = pl.pallas_call(
+    smooth, slope = pl.pallas_call(
         functools.partial(partial_body, blocks),
         out_shape=(
             jax.ShapeDtypeStruct((rows, LANES), f32),
             jax.ShapeDtypeStruct((rows, LANES), f32),
-            edge_shape,
         ),
         in_specs=in_smem(1) + in_vmem(1 + 2 * blocks),
-        out_specs=tuple(in_vmem(3)),
+        out_specs=tuple(in_vmem(2)),
         compiler_params=params,
         name="partial",
     )(weights, adjoint, *halves)
-    up = [(i, i + 1) for i in range(blocks_x - 1)]
-    down = [(j, i) for i, j in up]
-    sum_before, sum_after = lax.ppermute(sums, "rx", up), lax.ppermute(sums, "rx", down)
-
-    section, totals = pl.pallas_call(
-        functools.partial(final_body, devices),
+    filtered, edges = pl.pallas_call(
+        finish_body,
+        out_shape=(jax.ShapeDtypeStruct((rows, LANES), f32), edge_shape),
+        in_specs=in_smem(1) + in_vmem(3),
+        out_specs=tuple(in_vmem(2)),
+        compiler_params=params,
+        name="finish",
+    )(weights, smooth, last_first, last_second)
+    pairs = [(b, b ^ 1) for b in range(blocks_x)]
+    nexts = [(b, (b + (1 if b % 2 else -1)) % blocks_x) for b in range(blocks_x)]
+    edges_next, edges_pair = lax.ppermute(edges, "rx", nexts), lax.ppermute(edges, "rx", pairs)
+    place_x = jnp.reshape(lax.axis_index("rx"), (1, 1))
+
+    held, totals = pl.pallas_call(
+        functools.partial(final_body, blocks_x),
         out_shape=(
             jax.ShapeDtypeStruct(adjoint.shape, f32),
             jax.ShapeDtypeStruct((devices, LANES), f32),
         ),
-        in_specs=in_smem(2) + in_vmem(14),
+        in_specs=in_smem(2) + in_vmem(13),
         out_specs=tuple(in_vmem(2)),
         scratch_shapes=[
             pltpu.VMEM((fields, radial + 2 * TILE, LANES), f32),
+            pltpu.VMEM((fields, radial, LANES), f32),
             pltpu.VMEM((radial, LANES), f32),
         ],
         compiler_params=params,
         name="section",
     )(
         weights,
-        fwh_count,
-        smooth,
+        place_x,
+        filtered,
         slope,
         last_first,
         last_second,
-        raw_before,
-        raw_after,
-        sum_before,
-        sum_after,
+        edges_pair,
+        edges_next,
         density,
         velocity,
         pressure,
-        fwh_cell,
-        fwh_bin,
-        fwh_weight,
+        *tables,
     )
     totals = lax.all_to_all(totals, ("az", "rx"), 0, 0, tiled=True)
+    section = pl.pallas_call(
+        store_body,
+        out_shape=jax.ShapeDtypeStruct(adjoint.shape, f32),
+        in_specs=[pl.BlockSpec(memory_space=pl.ANY)],
+        out_specs=pl.BlockSpec(memory_space=pl.ANY),
+        scratch_shapes=[pltpu.SemaphoreType.DMA],
+        compiler_params=params,
+        name="store",
+    )(held)
     return section, jnp.sum(totals, axis=0)[:BIN_DEV]
 
 

time: 62.9 us -> 51 us (0.81)
  blocking collectives: 14 us -> 0 us
  waiting for transfers between devices: 11.2 us -> 19.8 us
  starting transfers between devices: 28.4 us -> 22.2 us
    all_to_all x1 -> x0, blocking collectives: 14 us -> none  [local(): totals = lax.all_to_all(totals, ('az', 'rx'), 0, 0, tiled=True)]
    ppermute x4 -> x2, starting transfers between devices: 12.8 us -> 1.71 us  [the longest x1 1.64 us: local(): lax.ppermute(edges, 'rx', nexts)]
    ppermute x6, starting transfers between devices: 11.3 us -> 0.82 us  [local(): left.append(lax.ppermute(from_left[part], 'az', onward))]
    ppermute x6, starting transfers between devices: 2.39 us -> 12.6 us  [local(): right.append(lax.ppermute(from_right[part], 'az', back))]
    all_to_all x0 -> x1, waiting for transfers between devices: none -> 6.41 us  [local(): totals = lax.all_to_all(totals, ('az', 'rx'), 0, 0, tiled=True)]
    all_to_all x0 -> x1, starting transfers between devices: none -> 4.97 us  [local(): totals = lax.all_to_all(totals, ('az', 'rx'), 0, 0, tiled=True)]
    ppermute x6, waiting for transfers between devices: 6.65 us -> 8.89 us  [local(): right.append(lax.ppermute(from_right[part], 'az', back))]
    ppermute x1, starting transfers between devices: 0.44 us -> 1.91 us  [local(): last_second = lax.ppermute(from_right[1], 'az', back)]
  transfers between devices with their start and end apart: 18 -> 17, of which waited for: 4 -> 9; matrix products, arithmetic and copies ran while one was open for 1% -> 1% of each run, Pallas kernels for 2% -> 3%
where the time goes in v3:
time: 51 us; the launch traced here: 50.8 us
  starting transfers between devices  22.2 us (44%)
  waiting for transfers between devices  19.8 us (39%)
  Pallas kernels  4.39 us (9%)
  local copies, waits for them, and re-layouts  2.45 us (5%)
  between operations  1.4 us (3%)
  other arithmetic  0.56 us (1%)
    ppermute x6, starting transfers between devices, local(): right.append(lax.ppermute(from_right[part], 'az', back))  12.6 us
    ppermute x6, waiting for transfers between devices, local(): right.append(lax.ppermute(from_right[part], 'az', back))  8.89 us
    all_to_all x1, waiting for transfers between devices, local(): totals = lax.all_to_all(totals, ('az', 'rx'), 0, 0, tiled=True)  6.41 us
    all_to_all x1, starting transfers between devices, local(): totals = lax.all_to_all(totals, ('az', 'rx'), 0, 0, tiled=True)  4.97 us
    pallas_call x1, Pallas kernels, local(): pl.pallas_call(functools.partial(final_body, blocks_x), out_shape=(jax.Sh...  2.04 us
    ppermute x1, starting transfers between devices, local(): last_second = lax.ppermute(from_right[1], 'az', back)  1.91 us
    ppermute x1, starting transfers between devices, local(): lax.ppermute(edges, 'rx', nexts)  1.64 us
    ppermute x1, waiting for transfers between devices, local(): lax.ppermute(edges, 'rx', nexts)  1.63 us
  transfers between devices with their start and end apart: 17, of which 9 were waited for; matrix products, arithmetic and copies ran while one was open for 1% of the time, Pallas kernels for 3%

profile of v3, /device:TPU:0, one launch (start us, length us, event | category | flops | bytes accessed | tf_op | source)
XLA Modules:
  0.0 50.8 jit_solution(3393200171344526160)
XLA Ops:
  0.6 1.1 %fusion = (f32[320,128]{1,0:T(8,128)S(1)}, f32[320,128]{1,0:T(8,128)S(1)}) fusion(f32[640,128]{1,0:T(8,128)} %bitcast.6), kind=kLoop, calls=%fused_computation.1 | loop fusion | bytes 655360 | tf_op jit(solution)/shard_map/slice | solution.py:282
  1.7 3.0 %collective-permute-start = (f32[320,128]{1,0:T(8,128)S(1)}, f32[320,128]{1,0:T(8,128)S(1)}, u32[]{:S(2)}, u32[]{:S(2)}) collective-permute-start(f32[320,128]{1,0:T(8,128)S(1)} %get-tuple-element.35), channel_id=1, source_target_pairs={{8,0},{16,8},{24,16},{28,24},{20,28},{12,20},{4,12},{0,4},{9,1},{1... | collective-permute-start | bytes 491528 | tf_op jit(solution)/shard_map/ppermute | solution.py:290
  4.7 0.2 collective-permute-start.2
  4.8 1.9 %collective-permute-start.4 = (f32[320,128]{1,0:T(8,128)S(1)}, f32[320,128]{1,0:T(8,128)S(1)}, u32[]{:S(2)}, u32[]{:S(2)}) collective-permute-start(f32[320,128]{1,0:T(8,128)S(1)} %get-tuple-element.34), channel_id=1, source_target_pairs={{8,0},{16,8},{24,16},{28,24},{20,28},{12,20},{4,12},{0,4},{9,1},{1... | collective-permute-start | bytes 491528 | tf_op jit(solution)/shard_map/ppermute | solution.py:290
  6.7 0.2 collective-permute-start.3
  6.9 2.9 %collective-permute-done.refs_3_ = f32[320,128]{1,0:T(8,128)S(1)} collective-permute-done((f32[320,128]{1,0:T(8,128)S(1)}, f32[320,128]{1,0:T(8,128)S(1)}, u32[]{:S(2)}, u32[]{:S(2)}) %collective-permute-start) | collective-permute-done | bytes 163872 | tf_op jit(solution)/shard_map/ppermute | solution.py:290
  9.8 2.0 %collective-permute-start.1 = (f32[320,128]{1,0:T(8,128)S(1)}, f32[320,128]{1,0:T(8,128)S(1)}, u32[]{:S(2)}, u32[]{:S(2)}) collective-permute-start(f32[320,128]{1,0:T(8,128)S(1)} %collective-permute-done.refs_3_), channel_id=1, source_target_pairs={{8,0},{16,8},{24,16},{28,24},{20,28},{12,20},{4,12},{0,4},{9,1},{1... | collective-permute-start | bytes 491528 | tf_op jit(solution)/shard_map/ppermute | solution.py:290
  12.6 0.6 %copy-done.4 = s32[1,1,256]{2,1,0:T(1,128)S(1)} copy-done((s32[1,1,256]{2,1,0:T(1,128)S(1)}, s32[1,1,256]{2,1,0:T(1,128)}, u32[]{:S(2)}) %copy-start.4) | copy-done | bytes 1048
  13.3 0.7 %constant_dynamic-slice_fusion.weights = f32[1,16]{1,0:T(1,128)S(1)} fusion(f32[8,16]{1,0:T(8,128)} %constant.17.clone, s32[]{:T(128)S(6)} %select_n.3), kind=kLoop, calls=%fused_computation | loop fusion | bytes 132 | tf_op jit(solution)/shard_map/dynamic_slice | solution.py:293
  14.1 1.9 %collective-permute-start.7 = (f32[320,128]{1,0:T(8,128)S(1)}, f32[320,128]{1,0:T(8,128)S(1)}, u32[]{:S(2)}, u32[]{:S(2)}) collective-permute-start(f32[320,128]{1,0:T(8,128)S(1)} %collective-permute-done.4.refs_2_), channel_id=1, source_target_pairs={{8,0},{16,8},{24,16},{28,24},{20,28},{12,20},{4,12},{0,4},{9,1},{1... | collective-permute-start | bytes 491528 | tf_op jit(solution)/shard_map/ppermute | solution.py:290
  16.0 0.1 collective-permute-start.6
  16.1 0.9 %collective-permute-done.1.refs_7_ = f32[320,128]{1,0:T(8,128)S(1)} collective-permute-done((f32[320,128]{1,0:T(8,128)S(1)}, f32[320,128]{1,0:T(8,128)S(1)}, u32[]{:S(2)}, u32[]{:S(2)}) %collective-permute-start.1) | collective-permute-done | bytes 163872 | tf_op jit(solution)/shard_map/ppermute | solution.py:290
  17.0 1.9 %collective-permute-start.11 = (f32[320,128]{1,0:T(8,128)S(1)}, f32[320,128]{1,0:T(8,128)S(1)}, u32[]{:S(2)}, u32[]{:S(2)}) collective-permute-start(f32[320,128]{1,0:T(8,128)S(1)} %collective-permute-done.1.refs_7_), channel_id=1, source_target_pairs={{8,0},{16,8},{24,16},{28,24},{20,28},{12,20},{4,12},{0,4},{9,1},{1... | collective-permute-start | bytes 491528 | tf_op jit(solution)/shard_map/ppermute | solution.py:290
  19.0 0.1 collective-permute-start.8
  19.1 2.1 %collective-permute-done.7.refs_6_ = f32[320,128]{1,0:T(8,128)S(1)} collective-permute-done((f32[320,128]{1,0:T(8,128)S(1)}, f32[320,128]{1,0:T(8,128)S(1)}, u32[]{:S(2)}, u32[]{:S(2)}) %collective-permute-start.7) | collective-permute-done | bytes 163872 | tf_op jit(solution)/shard_map/ppermute | solution.py:290
  21.2 1.9 %collective-permute-start.10 = (f32[320,128]{1,0:T(8,128)S(1)}, f32[320,128]{1,0:T(8,128)S(1)}, u32[]{:S(2)}, u32[]{:S(2)}) collective-permute-start(f32[320,128]{1,0:T(8,128)S(1)} %collective-permute-done.7.refs_6_), channel_id=1, source_target_pairs={{8,0},{16,8},{24,16},{28,24},{20,28},{12,20},{4,12},{0,4},{9,1},{1... | collective-permute-start | bytes 491528 | tf_op jit(solution)/shard_map/ppermute | solution.py:290
  23.1 0.1 collective-permute-start.9
  23.3 1.4 %collective-permute-done.11.refs_11_ = f32[320,128]{1,0:T(8,128)S(1)} collective-permute-done((f32[320,128]{1,0:T(8,128)S(1)}, f32[320,128]{1,0:T(8,128)S(1)}, u32[]{:S(2)}, u32[]{:S(2)}) %collective-permute-start.11) | collective-permute-done | bytes 163872 | tf_op jit(solution)/shard_map/ppermute | solution.py:290
  24.7 1.9 %collective-permute-start.13 = (f32[320,128]{1,0:T(8,128)S(1)}, f32[320,128]{1,0:T(8,128)S(1)}, u32[]{:S(2)}, u32[]{:S(2)}) collective-permute-start(f32[320,128]{1,0:T(8,128)S(1)} %collective-permute-done.11.refs_11_), channel_id=1, source_target_pairs={{8,0},{16,8},{24,16},{28,24},{20,28},{12,20},{4,12},{0,4},{9,1},{1... | collective-permute-start | bytes 491528 | tf_op jit(solution)/shard_map/ppermute | solution.py:315
  26.6 0.1 collective-permute-start.12
  26.8 1.5 %collective-permute-done.10.refs_10_ = f32[320,128]{1,0:T(8,128)S(1)} collective-permute-done((f32[320,128]{1,0:T(8,128)S(1)}, f32[320,128]{1,0:T(8,128)S(1)}, u32[]{:S(2)}, u32[]{:S(2)}) %collective-permute-start.10) | collective-permute-done | bytes 163872 | tf_op jit(solution)/shard_map/ppermute | solution.py:290
  28.3 1.4 %collective-permute-done.9.refs_9_ = f32[320,128]{1,0:T(8,128)S(1)} collective-permute-done((f32[320,128]{1,0:T(8,128)S(1)}, f32[320,128]{1,0:T(8,128)S(1)}, u32[]{:S(2)}, u32[]{:S(2)}) %collective-permute-start.9) | collective-permute-done | bytes 163872 | tf_op jit(solution)/shard_map/ppermute | solution.py:289
  29.7 0.9 %partial.1 = (f32[640,128]{1,0:T(8,128)S(1)}, f32[640,128]{1,0:T(8,128)S(1)}) custom-call(f32[1,16]{1,0:T(1,128)S(1)} %constant_dynamic-slice_fusion.weights, f32[5,1,128,128]{3,2,1,0:T(8,128)S(1)} %copy-done, f32[320,128]{1,0:T(8,128)S(1)} %collective-permute-done.2.refs_0_, f32[320,128]{1,0:T(8,128)S(1)} %collective-permute-done.3.refs_1_, ...), custom_call_target="tpu_custom_call" | custom-call | tf_op jit(solution)/shard_map/partial/pallas_call | solution.py:318
  30.5 1.4 %collective-permute-done.12.last_first = f32[320,128]{1,0:T(8,128)S(1)} collective-permute-done((f32[320,128]{1,0:T(8,128)S(1)}, f32[320,128]{1,0:T(8,128)S(1)}, u32[]{:S(2)}, u32[]{:S(2)}) %collective-permute-start.12) | collective-permute-done | bytes 163872 | tf_op jit(solution)/shard_map/ppermute | solution.py:314
  31.9 0.7 %finish.1 = (f32[640,128]{1,0:T(8,128)S(1)}, f32[5,8,128]{2,1,0:T(8,128)S(1)}) custom-call(f32[1,16]{1,0:T(1,128)S(1)} %constant_dynamic-slice_fusion.weights, f32[640,128]{1,0:T(8,128)S(1)} %get-tuple-element.24.smooth, f32[320,128]{1,0:T(8,128)S(1)} %collective-permute-done.12.last_first, f32[320,128]{1,0:T(8,128)S(1)} %collective-permute-done.13.last_second), custom_call_target="tpu_custom_call" | custom-call | tf_op jit(solution)/shard_map/finish/pallas_call | solution.py:329
  32.7 1.6 %collective-permute-start.15 = (f32[5,8,128]{2,1,0:T(8,128)S(1)}, f32[5,8,128]{2,1,0:T(8,128)S(1)}, u32[]{:S(2)}, u32[]{:S(2)}) collective-permute-start(f32[5,8,128]{2,1,0:T(8,128)S(1)} %get-tuple-element.27), channel_id=1, source_target_pairs={{0,3},{1,2},{2,1},{3,0},{4,7},{5,6},{6,5},{7,4},{8,11},{9,10},{10,... | collective-permute-start | bytes 61448 | tf_op jit(solution)/shard_map/ppermute | solution.py:339
  34.4 1.6 %collective-permute-done.15.edges_next = f32[5,8,128]{2,1,0:T(8,128)S(1)} collective-permute-done((f32[5,8,128]{2,1,0:T(8,128)S(1)}, f32[5,8,128]{2,1,0:T(8,128)S(1)}, u32[]{:S(2)}, u32[]{:S(2)}) %collective-permute-start.15) | collective-permute-done | bytes 20512 | tf_op jit(solution)/shard_map/ppermute | solution.py:339
  36.0 2.0 %section.1 = (f32[5,1,128,128]{3,2,1,0:T(8,128)S(1)}, f32[32,128]{1,0:T(8,128)}) custom-call(f32[1,16]{1,0:T(1,128)S(1)} %constant_dynamic-slice_fusion.weights, s32[1,1]{1,0:T(1,128)} %bitcast.1.place_x, f32[640,128]{1,0:T(8,128)S(1)} %get-tuple-element.25.smooth, f32[640,128]{1,0:T(8,128)S(1)} %get-tuple-element.26.slope, ...), custom_call_target="tpu_custom_call" | custom-call | tf_op jit(solution)/shard_map/section/pallas_call | solution.py:342
  38.1 5.0 %all-to-all-start = ((f32[32,1,128]{2,1,0:T(1,128)}), f32[32,1,128]{2,1,0:T(1,128)S(1)}, u32[]{:S(2)}, u32[]{:S(2)}) async-start(f32[32,1,128]{2,1,0:T(1,128)} %bitcast.3), calls=%async_computation | async-start | bytes 32768 | tf_op jit(solution)/shard_map/all_to_all | solution.py:371
  43.0 0.7 %store.1 = f32[5,1,128,128]{3,2,1,0:T(8,128)} custom-call(f32[5,1,128,128]{3,2,1,0:T(8,128)S(1)} %get-tuple-element.32.source), custom_call_target="tpu_custom_call" | custom-call | tf_op jit(solution)/shard_map/store/pallas_call | solution.py:372
  43.8 6.4 %all-to-all-done = f32[32,1,128]{2,1,0:T(1,128)S(1)} async-done(((f32[32,1,128]{2,1,0:T(1,128)}), f32[32,1,128]{2,1,0:T(1,128)S(1)}, u32[]{:S(2)}, u32[]{:S(2)}) %all-to-all-start) | async-done | bytes 16416 | tf_op jit(solution)/shard_map/all_to_all | solution.py:371
  50.2 0.6 %reduce_sum.9 = f32[128]{0:T(128)} reduce(f32[32,1,128]{2,1,0:T(1,128)S(1)} %all-to-all-done, f32[]{:T(128)} %constant.16.clone.1), dimensions={0,1}, to_apply=%region_0.0 | reduce | flops 3968 | bytes 16900 | tf_op jit(solution)/shard_map/reduce_sum | solution.py:381
  (24 shorter events, 0.4 us)
Async XLA Ops:
  0.6 29.0 %copy-start = (f32[5,1,128,128]{3,2,1,0:T(8,128)S(1)}, f32[5,1,128,128]{3,2,1,0:T(8,128)}, u32[]{:S(2)}) copy-start(f32[5,1,128,128]{3,2,1,0:T(8,128)} %source.1) | copy-start | bytes 983044
  1.7 8.1 %collective-permute-start = (f32[320,128]{1,0:T(8,128)S(1)}, f32[320,128]{1,0:T(8,128)S(1)}, u32[]{:S(2)}, u32[]{:S(2)}) collective-permute-start(f32[320,128]{1,0:T(8,128)S(1)} %get-tuple-element.35), channel_id=1, source_target_pairs={{8,0},{16,8},{24,16},{28,24},{20,28},{12,20},{4,12},{0,4},{9,1},{1... | collective-permute-start | bytes 491528 | tf_op jit(solution)/shard_map/ppermute | solution.py:290
  4.7 7.1 %collective-permute-start.2 = (f32[320,128]{1,0:T(8,128)S(1)}, f32[320,128]{1,0:T(8,128)S(1)}, u32[]{:S(2)}, u32[]{:S(2)}) collective-permute-start(f32[320,128]{1,0:T(8,128)S(1)} %get-tuple-element.34), channel_id=1, source_target_pairs={{0,8},{8,16},{16,24},{24,28},{28,20},{20,12},{12,4},{4,0},{1,9},{9... | collective-permute-start | bytes 491528 | tf_op jit(solution)/shard_map/ppermute | solution.py:289
  4.8 9.2 %collective-permute-start.4 = (f32[320,128]{1,0:T(8,128)S(1)}, f32[320,128]{1,0:T(8,128)S(1)}, u32[]{:S(2)}, u32[]{:S(2)}) collective-permute-start(f32[320,128]{1,0:T(8,128)S(1)} %get-tuple-element.34), channel_id=1, source_target_pairs={{8,0},{16,8},{24,16},{28,24},{20,28},{12,20},{4,12},{0,4},{9,1},{1... | collective-permute-start | bytes 491528 | tf_op jit(solution)/shard_map/ppermute | solution.py:290
  6.7 9.2 %collective-permute-start.3 = (f32[320,128]{1,0:T(8,128)S(1)}, f32[320,128]{1,0:T(8,128)S(1)}, u32[]{:S(2)}, u32[]{:S(2)}) collective-permute-start(f32[320,128]{1,0:T(8,128)S(1)} %get-tuple-element.35), channel_id=1, source_target_pairs={{0,8},{8,16},{16,24},{24,28},{28,20},{20,12},{12,4},{4,0},{1,9},{9... | collective-permute-start | bytes 491528 | tf_op jit(solution)/shard_map/ppermute | solution.py:289
  9.8 7.2 %collective-permute-start.1 = (f32[320,128]{1,0:T(8,128)S(1)}, f32[320,128]{1,0:T(8,128)S(1)}, u32[]{:S(2)}, u32[]{:S(2)}) collective-permute-start(f32[320,128]{1,0:T(8,128)S(1)} %collective-permute-done.refs_3_), channel_id=1, source_target_pairs={{8,0},{16,8},{24,16},{28,24},{20,28},{12,20},{4,12},{0,4},{9,1},{1... | collective-permute-start | bytes 491528 | tf_op jit(solution)/shard_map/ppermute | solution.py:290
  11.8 7.1 %collective-permute-start.5 = (f32[320,128]{1,0:T(8,128)S(1)}, f32[320,128]{1,0:T(8,128)S(1)}, u32[]{:S(2)}, u32[]{:S(2)}) collective-permute-start(f32[320,128]{1,0:T(8,128)S(1)} %collective-permute-done.2.refs_0_), channel_id=1, source_target_pairs={{0,8},{8,16},{16,24},{24,28},{28,20},{20,12},{12,4},{4,0},{1,9},{9... | collective-permute-start | bytes 491528 | tf_op jit(solution)/shard_map/ppermute | solution.py:289
  11.9 0.7 %copy-start.6 = (f32[1,1,256]{2,1,0:T(1,128)S(1)}, f32[1,1,256]{2,1,0:T(1,128)}, u32[]{:S(2)}) copy-start(f32[1,1,256]{2,1,0:T(1,128)} %slot_weights.1) | copy-start | bytes 3076
  12.6 0.7 %copy-start.4 = (s32[1,1,256]{2,1,0:T(1,128)S(1)}, s32[1,1,256]{2,1,0:T(1,128)}, u32[]{:S(2)}) copy-start(s32[1,1,256]{2,1,0:T(1,128)} %cells.1) | copy-start | bytes 3076
  12.6 0.7 %copy-start.5 = (s32[1,1,256]{2,1,0:T(1,128)S(1)}, s32[1,1,256]{2,1,0:T(1,128)}, u32[]{:S(2)}) copy-start(s32[1,1,256]{2,1,0:T(1,128)} %bins.1) | copy-start | bytes 3076
  14.1 7.1 %collective-permute-start.7 = (f32[320,128]{1,0:T(8,128)S(1)}, f32[320,128]{1,0:T(8,128)S(1)}, u32[]{:S(2)}, u32[]{:S(2)}) collective-permute-start(f32[320,128]{1,0:T(8,128)S(1)} %collective-permute-done.4.refs_2_), channel_id=1, source_target_pairs={{8,0},{16,8},{24,16},{28,24},{20,28},{12,20},{4,12},{0,4},{9,1},{1... | collective-permute-start | bytes 491528 | tf_op jit(solution)/shard_map/ppermute | solution.py:290
  16.0 7.1 %collective-permute-start.6 = (f32[320,128]{1,0:T(8,128)S(1)}, f32[320,128]{1,0:T(8,128)S(1)}, u32[]{:S(2)}, u32[]{:S(2)}) collective-permute-start(f32[320,128]{1,0:T(8,128)S(1)} %collective-permute-done.3.refs_1_), channel_id=1, source_target_pairs={{0,8},{8,16},{16,24},{24,28},{28,20},{20,12},{12,4},{4,0},{1,9},{9... | collective-permute-start | bytes 491528 | tf_op jit(solution)/shard_map/ppermute | solution.py:289
  17.0 7.7 %collective-permute-start.11 = (f32[320,128]{1,0:T(8,128)S(1)}, f32[320,128]{1,0:T(8,128)S(1)}, u32[]{:S(2)}, u32[]{:S(2)}) collective-permute-start(f32[320,128]{1,0:T(8,128)S(1)} %collective-permute-done.1.refs_7_), channel_id=1, source_target_pairs={{8,0},{16,8},{24,16},{28,24},{20,28},{12,20},{4,12},{0,4},{9,1},{1... | collective-permute-start | bytes 491528 | tf_op jit(solution)/shard_map/ppermute | solution.py:290
  19.0 7.7 %collective-permute-start.8 = (f32[320,128]{1,0:T(8,128)S(1)}, f32[320,128]{1,0:T(8,128)S(1)}, u32[]{:S(2)}, u32[]{:S(2)}) collective-permute-start(f32[320,128]{1,0:T(8,128)S(1)} %collective-permute-done.5.refs_4_), channel_id=1, source_target_pairs={{0,8},{8,16},{16,24},{24,28},{28,20},{20,12},{12,4},{4,0},{1,9},{9... | collective-permute-start | bytes 491528 | tf_op jit(solution)/shard_map/ppermute | solution.py:289
  21.2 7.1 %collective-permute-start.10 = (f32[320,128]{1,0:T(8,128)S(1)}, f32[320,128]{1,0:T(8,128)S(1)}, u32[]{:S(2)}, u32[]{:S(2)}) collective-permute-start(f32[320,128]{1,0:T(8,128)S(1)} %collective-permute-done.7.refs_6_), channel_id=1, source_target_pairs={{8,0},{16,8},{24,16},{28,24},{20,28},{12,20},{4,12},{0,4},{9,1},{1... | collective-permute-start | bytes 491528 | tf_op jit(solution)/shard_map/ppermute | solution.py:290
  23.1 6.6 %collective-permute-start.9 = (f32[320,128]{1,0:T(8,128)S(1)}, f32[320,128]{1,0:T(8,128)S(1)}, u32[]{:S(2)}, u32[]{:S(2)}) collective-permute-start(f32[320,128]{1,0:T(8,128)S(1)} %collective-permute-done.6.refs_5_), channel_id=1, source_target_pairs={{0,8},{8,16},{16,24},{24,28},{28,20},{20,12},{12,4},{4,0},{1,9},{9... | collective-permute-start | bytes 491528 | tf_op jit(solution)/shard_map/ppermute | solution.py:289
  24.7 5.8 %collective-permute-start.13 = (f32[320,128]{1,0:T(8,128)S(1)}, f32[320,128]{1,0:T(8,128)S(1)}, u32[]{:S(2)}, u32[]{:S(2)}) collective-permute-start(f32[320,128]{1,0:T(8,128)S(1)} %collective-permute-done.11.refs_11_), channel_id=1, source_target_pairs={{8,0},{16,8},{24,16},{28,24},{20,28},{12,20},{4,12},{0,4},{9,1},{1... | collective-permute-start | bytes 491528 | tf_op jit(solution)/shard_map/ppermute | solution.py:315
  26.6 5.3 %collective-permute-start.12 = (f32[320,128]{1,0:T(8,128)S(1)}, f32[320,128]{1,0:T(8,128)S(1)}, u32[]{:S(2)}, u32[]{:S(2)}) collective-permute-start(f32[320,128]{1,0:T(8,128)S(1)} %collective-permute-done.8.refs_8_), channel_id=1, source_target_pairs={{0,8},{8,16},{16,24},{24,28},{28,20},{20,12},{12,4},{4,0},{1,9},{9... | collective-permute-start | bytes 491528 | tf_op jit(solution)/shard_map/ppermute | solution.py:314
  31.9 4.1 %copy-start.1 = (f32[3,1,128,128]{3,2,1,0:T(8,128)S(1)}, f32[3,1,128,128]{3,2,1,0:T(8,128)}, u32[]{:S(2)}) copy-start(f32[3,1,128,128]{3,2,1,0:T(8,128)} %velocity.1) | copy-start | bytes 589828
  31.9 4.1 %copy-start.2 = (f32[1,128,128]{2,1,0:T(8,128)S(1)}, f32[1,128,128]{2,1,0:T(8,128)}, u32[]{:S(2)}) copy-start(f32[1,128,128]{2,1,0:T(8,128)} %density.1) | copy-start | bytes 196612
  31.9 4.1 %copy-start.3 = (f32[1,128,128]{2,1,0:T(8,128)S(1)}, f32[1,128,128]{2,1,0:T(8,128)}, u32[]{:S(2)}) copy-start(f32[1,128,128]{2,1,0:T(8,128)} %pressure.1) | copy-start | bytes 196612
  32.7 1.7 %collective-permute-start.14 = (f32[5,8,128]{2,1,0:T(8,128)S(1)}, f32[5,8,128]{2,1,0:T(8,128)S(1)}, u32[]{:S(2)}, u32[]{:S(2)}) collective-permute-start(f32[5,8,128]{2,1,0:T(8,128)S(1)} %get-tuple-element.27), channel_id=1, source_target_pairs={{0,1},{1,0},{2,3},{3,2},{4,5},{5,4},{6,7},{7,6},{8,9},{9,8},{10,11... | collective-permute-start | bytes 61448 | tf_op jit(solution)/shard_map/ppermute | solution.py:339
  32.7 3.3 %collective-permute-start.15 = (f32[5,8,128]{2,1,0:T(8,128)S(1)}, f32[5,8,128]{2,1,0:T(8,128)S(1)}, u32[]{:S(2)}, u32[]{:S(2)}) collective-permute-start(f32[5,8,128]{2,1,0:T(8,128)S(1)} %get-tuple-element.27), channel_id=1, source_target_pairs={{0,3},{1,2},{2,1},{3,0},{4,7},{5,6},{6,5},{7,4},{8,11},{9,10},{10,... | collective-permute-start | bytes 61448 | tf_op jit(solution)/shard_map/ppermute | solution.py:339
  38.1 12.1 %all-to-all-start = ((f32[32,1,128]{2,1,0:T(1,128)}), f32[32,1,128]{2,1,0:T(1,128)S(1)}, u32[]{:S(2)}, u32[]{:S(2)}) async-start(f32[32,1,128]{2,1,0:T(1,128)} %bitcast.3), calls=%async_computation | async-start | bytes 32768 | tf_op jit(solution)/shard_map/all_to_all | solution.py:371

commit v4 on v3

--- a/solution.py
+++ b/solution.py
@@ -80,12 +80,20 @@
     return packed
 
 
-def partial_body(blocks, weights, source, *refs):
+def edges_body(source, edges):
+    fields, radial = source.shape[0], source.shape[2]
+    for field in range(fields):
+        tiles = [source[field, 0, pl.ds(row, TILE), :] for row in range(0, radial, TILE)]
+        edges[field] = packed_edges(tiles)
+
+
+def partial_body(blocks, weights, source, last_edges, *refs):
     count = weights.shape[1] // 2
-    halves, (smooth, slope) = refs[: 2 * blocks], refs[2 * blocks :]
+    halves, (smooth, slope, edges) = refs[: 2 * blocks], refs[2 * blocks :]
     fields, radial = source.shape[0], source.shape[2]
     half = halves[0].shape[0]
     for field in range(fields):
+        tiles = []
         for row in range(0, radial, TILE):
             at = field * radial + row
             value = source[field, 0, pl.ds(row, TILE), :]
@@ -96,22 +104,8 @@
                 second = second + weights[0, count + 1 + k] * value
             smooth[pl.ds(at, TILE), :] = first
             slope[pl.ds(at, TILE), :] = second
-
-
-def finish_body(weights, smooth, last_first, last_second, filtered, edges):
-    fields, count = edges.shape[0], weights.shape[1] // 2
-    half = last_first.shape[0]
-    radial = smooth.shape[0] // fields
-    last_weight = weights[0, count - 1]
-    for field in range(fields):
-        tiles = []
-        for row in range(0, radial, TILE):
-            at = field * radial + row
-            source = last_first if at < half else last_second
-            value = smooth[pl.ds(at, TILE), :] + last_weight * source[pl.ds(at % half, TILE), :]
-            filtered[pl.ds(at, TILE), :] = value
-            tiles.append(value)
-        edges[field] = packed_edges(tiles)
+            tiles.append(first)
+        edges[field] = packed_edges(tiles) + weights[0, count - 1] * last_edges[field]
 
 
 def slots_body(live_count, cells, bins, slot_weights, column, line, owner, place):
@@ -170,7 +164,7 @@
     fields, radial = section.shape[0], section.shape[2]
     count = weights.shape[1] // 2
     half = last_first.shape[0]
-    last_slope = weights[0, 2 * count - 1]
+    last_weight, last_slope = weights[0, count - 1], weights[0, 2 * count - 1]
 
     def last(at):
         source = last_first if at < half else last_second
@@ -188,7 +182,8 @@
         packed = jnp.where(paired, edges_pair[field], inner * edges_next[field])
         for row in range(0, radial, TILE):
             at = field * radial + row
-            filtered[field, pl.ds(TILE + row, TILE), :] = smooth[pl.ds(at, TILE), :]
+            value = smooth[pl.ds(at, TILE), :] + last_weight * last(at)
+            filtered[field, pl.ds(TILE + row, TILE), :] = value
             edge = pltpu.roll(packed, LANES - (SLOT * (row // TILE) + EDGE), 1)
             halos[field, pl.ds(row, TILE), :] = edge
 
@@ -278,6 +273,7 @@
     onward = [(order[i], order[(i + 1) % thetas]) for i in range(thetas)]
     back = [(b, a) for a, b in onward]
 
+    across = [(order[i], order[(i + thetas // 2) % thetas]) for i in range(thetas)]
     flat = adjoint.reshape(rows, LANES)
     own = [flat[:half], flat[half:]]
     steps = thetas // 2 - 1
@@ -289,6 +285,19 @@
             left.append(lax.ppermute(from_left[part], "az", onward))
             right.append(lax.ppermute(from_right[part], "az", back))
         from_left, from_right = left, right
+        if step == 0:
+            source, from_left[0] = lax.optimization_barrier((adjoint, from_left[0]))
+            last_edges = pl.pallas_call(
+                edges_body,
+                out_shape=edge_shape,
+                in_specs=in_vmem(1),
+                out_specs=in_vmem(1)[0],
+                compiler_params=params,
+                name="edges",
+            )(source)
+            last_edges = lax.ppermute(last_edges, "az", across)
+        if step == 0 + 1:
+            last_edges, from_right[1] = lax.optimization_barrier((last_edges, from_right[1]))
         if step == 0:
             weights = lax.dynamic_slice_in_dim(
                 jnp.asarray(ring_weights(thetas)), lax.axis_index("az"), 1, axis=0
@@ -315,25 +324,18 @@
     last_second = lax.ppermute(from_right[1], "az", back)
 
     blocks = len(halves) // 2
-    smooth, slope = pl.pallas_call(
+    smooth, slope, edges = pl.pallas_call(
         functools.partial(partial_body, blocks),
         out_shape=(
             jax.ShapeDtypeStruct((rows, LANES), f32),
             jax.ShapeDtypeStruct((rows, LANES), f32),
+            edge_shape,
         ),
-        in_specs=in_smem(1) + in_vmem(1 + 2 * blocks),
-        out_specs=tuple(in_vmem(2)),
+        in_specs=in_smem(1) + in_vmem(2 + 2 * blocks),
+        out_specs=tuple(in_vmem(3)),
         compiler_params=params,
         name="partial",
-    )(weights, adjoint, *halves)
-    filtered, edges = pl.pallas_call(
-        finish_body,
-        out_shape=(jax.ShapeDtypeStruct((rows, LANES), f32), edge_shape),
-        in_specs=in_smem(1) + in_vmem(3),
-        out_specs=tuple(in_vmem(2)),
-        compiler_params=params,
-        name="finish",
-    )(weights, smooth, last_first, last_second)
+    )(weights, adjoint, last_edges, *halves)
     pairs = [(b, b ^ 1) for b in range(blocks_x)]
     nexts = [(b, (b + (1 if b % 2 else -1)) % blocks_x) for b in range(blocks_x)]
     edges_next, edges_pair = lax.ppermute(edges, "rx", nexts), lax.ppermute(edges, "rx", pairs)
@@ -357,7 +359,7 @@
     )(
         weights,
         place_x,
-        filtered,
+        smooth,
         slope,
         last_first,
         last_second,

time: 51 us -> 49.9 us (0.978)
  starting transfers between devices: 22.2 us -> 26.8 us
  waiting for transfers between devices: 19.8 us -> 15.2 us
  local copies, waits for them, and re-layouts: 2.45 us -> 1.78 us
    ppermute x0 -> x1, starting transfers between devices: none -> 5.02 us  [local(): last_edges = lax.ppermute(last_edges, 'az', across)]
    ppermute x6, waiting for transfers between devices: 8.89 us -> 5.11 us  [local(): right.append(lax.ppermute(from_right[part], 'az', back))]
    ppermute x6, starting transfers between devices: 0.82 us -> 4.29 us  [local(): left.append(lax.ppermute(from_left[part], 'az', onward))]
    ppermute x6, starting transfers between devices: 12.6 us -> 9.39 us  [local(): right.append(lax.ppermute(from_right[part], 'az', back))]
    ppermute x0 -> x1, waiting for transfers between devices: none -> 1.86 us  [local(): last_edges = lax.ppermute(last_edges, 'az', across)]
    ppermute x1, starting transfers between devices: 0.15 us -> 1.7 us  [local(): last_first = lax.ppermute(from_left[0], 'az', onward)]
    ppermute x1, waiting for transfers between devices: 1.4 us -> 0.01 us  [local(): last_first = lax.ppermute(from_left[0], 'az', onward)]
    ppermute x1, starting transfers between devices: 1.91 us -> 0.55 us  [local(): last_second = lax.ppermute(from_right[1], 'az', back)]
  transfers between devices with their start and end apart: 17 -> 18, of which waited for: 9 -> 6; matrix products, arithmetic and copies ran while one was open for 1% -> 1% of each run, Pallas kernels for 3% -> 4%
where the time goes in v4:
time: 49.9 us; the launch traced here: 49.7 us
  starting transfers between devices  26.8 us (54%)
  waiting for transfers between devices  15.2 us (30%)
  Pallas kernels  3.89 us (8%)
  local copies, waits for them, and re-layouts  1.78 us (4%)
  between operations  1.43 us (3%)
  other arithmetic  0.56 us (1%)
    ppermute x6, starting transfers between devices, local(): right.append(lax.ppermute(from_right[part], 'az', back))  9.39 us
    all_to_all x1, waiting for transfers between devices, local(): totals = lax.all_to_all(totals, ('az', 'rx'), 0, 0, tiled=True)  6.41 us
    ppermute x6, waiting for transfers between devices, local(): right.append(lax.ppermute(from_right[part], 'az', back))  5.11 us
    ppermute x1, starting transfers between devices, local(): last_edges = lax.ppermute(last_edges, 'az', across)  5.02 us
    ppermute x6, starting transfers between devices, local(): left.append(lax.ppermute(from_left[part], 'az', onward))  4.29 us
    all_to_all x1, starting transfers between devices, local(): totals = lax.all_to_all(totals, ('az', 'rx'), 0, 0, tiled=True)  4.2 us
    pallas_call x1, Pallas kernels, local(): pl.pallas_call(functools.partial(final_body, blocks_x), out_shape=(jax.Sh...  2.03 us
    ppermute x1, waiting for transfers between devices, local(): last_edges = lax.ppermute(last_edges, 'az', across)  1.86 us
  transfers between devices with their start and end apart: 18, of which 6 were waited for; matrix products, arithmetic and copies ran while one was open for 1% of the time, Pallas kernels for 4%

profile of v4, /device:TPU:0, one launch (start us, length us, event | category | flops | bytes accessed | tf_op | source)
XLA Modules:
  0.0 49.7 jit_solution(13506950548011487660)
XLA Ops:
  0.6 1.1 %fusion = (f32[320,128]{1,0:T(8,128)S(1)}, f32[320,128]{1,0:T(8,128)S(1)}) fusion(f32[640,128]{1,0:T(8,128)} %bitcast.6), kind=kLoop, calls=%fused_computation.1 | loop fusion | bytes 655360 | tf_op jit(solution)/shard_map/slice | solution.py:278
  1.7 3.0 %collective-permute-start.2 = (f32[320,128]{1,0:T(8,128)S(1)}, f32[320,128]{1,0:T(8,128)S(1)}, u32[]{:S(2)}, u32[]{:S(2)}) collective-permute-start(f32[320,128]{1,0:T(8,128)S(1)} %get-tuple-element.40), channel_id=1, source_target_pairs={{8,0},{16,8},{24,16},{28,24},{20,28},{12,20},{4,12},{0,4},{9,1},{1... | collective-permute-start | bytes 491528 | tf_op jit(solution)/shard_map/ppermute | solution.py:286
  4.7 0.2 collective-permute-start
  4.8 2.0 %collective-permute-start.4 = (f32[320,128]{1,0:T(8,128)S(1)}, f32[320,128]{1,0:T(8,128)S(1)}, u32[]{:S(2)}, u32[]{:S(2)}) collective-permute-start(f32[320,128]{1,0:T(8,128)S(1)} %get-tuple-element.40), channel_id=1, source_target_pairs={{0,8},{8,16},{16,24},{24,28},{28,20},{20,12},{12,4},{4,0},{1,9},{9... | collective-permute-start | bytes 491528 | tf_op jit(solution)/shard_map/ppermute | solution.py:285
  6.8 0.1 collective-permute-start.5
  6.9 2.6 %collective-permute-done.2.refs_3_ = f32[320,128]{1,0:T(8,128)S(1)} collective-permute-done((f32[320,128]{1,0:T(8,128)S(1)}, f32[320,128]{1,0:T(8,128)S(1)}, u32[]{:S(2)}, u32[]{:S(2)}) %collective-permute-start.2) | collective-permute-done | bytes 163872 | tf_op jit(solution)/shard_map/ppermute | solution.py:286
  9.5 2.3 %collective-permute-start.3 = (f32[320,128]{1,0:T(8,128)S(1)}, f32[320,128]{1,0:T(8,128)S(1)}, u32[]{:S(2)}, u32[]{:S(2)}) collective-permute-start(f32[320,128]{1,0:T(8,128)S(1)} %collective-permute-done.2.refs_3_), channel_id=1, source_target_pairs={{8,0},{16,8},{24,16},{28,24},{20,28},{12,20},{4,12},{0,4},{9,1},{1... | collective-permute-start | bytes 491528 | tf_op jit(solution)/shard_map/ppermute | solution.py:286
  11.8 0.0 collective-permute-done.refs_0_
  11.8 0.1 collective-permute-start.6
  11.9 0.1 edges.1
  12.1 5.0 %collective-permute-start.1 = (f32[5,8,128]{2,1,0:T(8,128)S(1)}, f32[5,8,128]{2,1,0:T(8,128)S(1)}, u32[]{:S(2)}, u32[]{:S(2)}) collective-permute-start(f32[5,8,128]{2,1,0:T(8,128)S(1)} %edges.1), channel_id=1, source_target_pairs={{0,28},{8,20},{16,12},{24,4},{28,0},{20,8},{12,16},{4,24},{1,29},{... | collective-permute-start | bytes 61448 | tf_op jit(solution)/shard_map/ppermute | solution.py:298
  17.1 0.0 collective-permute-done.4.refs_1_
  17.1 2.0 %collective-permute-start.8 = (f32[320,128]{1,0:T(8,128)S(1)}, f32[320,128]{1,0:T(8,128)S(1)}, u32[]{:S(2)}, u32[]{:S(2)}) collective-permute-start(f32[320,128]{1,0:T(8,128)S(1)} %collective-permute-done.5.refs_2_), channel_id=1, source_target_pairs={{8,0},{16,8},{24,16},{28,24},{20,28},{12,20},{4,12},{0,4},{9,1},{1... | collective-permute-start | bytes 491528 | tf_op jit(solution)/shard_map/ppermute | solution.py:286
  19.1 0.7 %constant_dynamic-slice_fusion.weights = f32[1,16]{1,0:T(1,128)S(1)} fusion(f32[8,16]{1,0:T(8,128)} %constant.17.clone, s32[]{:T(128)S(6)} %select_n.3), kind=kLoop, calls=%fused_computation | loop fusion | bytes 132 | tf_op jit(solution)/shard_map/dynamic_slice | solution.py:302
  20.6 1.9 %collective-permute-done.1.last_edges = f32[5,8,128]{2,1,0:T(8,128)S(1)} collective-permute-done((f32[5,8,128]{2,1,0:T(8,128)S(1)}, f32[5,8,128]{2,1,0:T(8,128)S(1)}, u32[]{:S(2)}, u32[]{:S(2)}) %collective-permute-start.1) | collective-permute-done | bytes 20512 | tf_op jit(solution)/shard_map/ppermute | solution.py:298
  22.5 0.1 collective-permute-start.12
  22.5 2.0 %collective-permute-start.9 = (f32[320,128]{1,0:T(8,128)S(1)}, f32[320,128]{1,0:T(8,128)S(1)}, u32[]{:S(2)}, u32[]{:S(2)}) collective-permute-start(f32[320,128]{1,0:T(8,128)S(1)} %collective-permute-done.6.refs_4_), channel_id=1, source_target_pairs={{0,8},{8,16},{16,24},{24,28},{28,20},{20,12},{12,4},{4,0},{1,9},{9... | collective-permute-start | bytes 491528 | tf_op jit(solution)/shard_map/ppermute | solution.py:285
  24.5 0.1 collective-permute-start.10
  24.6 2.0 %collective-permute-start.11 = (f32[320,128]{1,0:T(8,128)S(1)}, f32[320,128]{1,0:T(8,128)S(1)}, u32[]{:S(2)}, u32[]{:S(2)}) collective-permute-start(f32[320,128]{1,0:T(8,128)S(1)} %collective-permute-done.8.refs_6_), channel_id=1, source_target_pairs={{8,0},{16,8},{24,16},{28,24},{20,28},{12,20},{4,12},{0,4},{9,1},{1... | collective-permute-start | bytes 491528 | tf_op jit(solution)/shard_map/ppermute | solution.py:286
  26.6 2.5 %collective-permute-done.12.refs_11_ = f32[320,128]{1,0:T(8,128)S(1)} collective-permute-done((f32[320,128]{1,0:T(8,128)S(1)}, f32[320,128]{1,0:T(8,128)S(1)}, u32[]{:S(2)}, u32[]{:S(2)}) %collective-permute-start.12) | collective-permute-done | bytes 163872 | tf_op jit(solution)/shard_map/ppermute | solution.py:286
  29.1 0.5 %collective-permute-start.14 = (f32[320,128]{1,0:T(8,128)S(1)}, f32[320,128]{1,0:T(8,128)S(1)}, u32[]{:S(2)}, u32[]{:S(2)}) collective-permute-start(f32[320,128]{1,0:T(8,128)S(1)} %collective-permute-done.12.refs_11_), channel_id=1, source_target_pairs={{8,0},{16,8},{24,16},{28,24},{20,28},{12,20},{4,12},{0,4},{9,1},{1... | collective-permute-start | bytes 491528 | tf_op jit(solution)/shard_map/ppermute | solution.py:324
  29.6 1.7 %collective-permute-start.13 = (f32[320,128]{1,0:T(8,128)S(1)}, f32[320,128]{1,0:T(8,128)S(1)}, u32[]{:S(2)}, u32[]{:S(2)}) collective-permute-start(f32[320,128]{1,0:T(8,128)S(1)} %collective-permute-done.9.refs_8_), channel_id=1, source_target_pairs={{0,8},{8,16},{16,24},{24,28},{28,20},{20,12},{12,4},{4,0},{1,9},{9... | collective-permute-start | bytes 491528 | tf_op jit(solution)/shard_map/ppermute | solution.py:323
  31.3 0.1 collective-permute-done.10.refs_9_
  31.4 0.9 %partial.1 = (f32[640,128]{1,0:T(8,128)S(1)}, f32[640,128]{1,0:T(8,128)S(1)}, f32[5,8,128]{2,1,0:T(8,128)S(1)}) custom-call(f32[1,16]{1,0:T(1,128)S(1)} %constant_dynamic-slice_fusion.weights, f32[5,1,128,128]{3,2,1,0:T(8,128)S(1)} %copy-done, f32[5,8,128]{2,1,0:T(8,128)S(1)} %collective-permute-done.1.last_edges, ...), custom_call_target="tpu_custom_call" | custom-call | tf_op jit(solution)/shard_map/partial/pallas_call | solution.py:327
  32.4 0.1 collective-permute-start.15
  32.4 1.6 %collective-permute-start.16 = (f32[5,8,128]{2,1,0:T(8,128)S(1)}, f32[5,8,128]{2,1,0:T(8,128)S(1)}, u32[]{:S(2)}, u32[]{:S(2)}) collective-permute-start(f32[5,8,128]{2,1,0:T(8,128)S(1)} %get-tuple-element.33), channel_id=1, source_target_pairs={{0,3},{1,2},{2,1},{3,0},{4,7},{5,6},{6,5},{7,4},{8,11},{9,10},{10,... | collective-permute-start | bytes 61448 | tf_op jit(solution)/shard_map/ppermute | solution.py:341
  34.1 1.6 %collective-permute-done.16.edges_next = f32[5,8,128]{2,1,0:T(8,128)S(1)} collective-permute-done((f32[5,8,128]{2,1,0:T(8,128)S(1)}, f32[5,8,128]{2,1,0:T(8,128)S(1)}, u32[]{:S(2)}, u32[]{:S(2)}) %collective-permute-start.16) | collective-permute-done | bytes 20512 | tf_op jit(solution)/shard_map/ppermute | solution.py:341
  35.7 2.0 %section.1 = (f32[5,1,128,128]{3,2,1,0:T(8,128)S(1)}, f32[32,128]{1,0:T(8,128)}) custom-call(f32[1,16]{1,0:T(1,128)S(1)} %constant_dynamic-slice_fusion.weights, s32[1,1]{1,0:T(1,128)} %bitcast.1.place_x, f32[640,128]{1,0:T(8,128)S(1)} %get-tuple-element.31.smooth, f32[640,128]{1,0:T(8,128)S(1)} %get-tuple-element.32.slope, ...), custom_call_target="tpu_custom_call" | custom-call | tf_op jit(solution)/shard_map/section/pallas_call | solution.py:344
  37.8 4.2 %all-to-all-start = ((f32[32,1,128]{2,1,0:T(1,128)}), f32[32,1,128]{2,1,0:T(1,128)S(1)}, u32[]{:S(2)}, u32[]{:S(2)}) async-start(f32[32,1,128]{2,1,0:T(1,128)} %bitcast.3), calls=%async_computation | async-start | bytes 32768 | tf_op jit(solution)/shard_map/all_to_all | solution.py:373
  42.0 0.7 %store.1 = f32[5,1,128,128]{3,2,1,0:T(8,128)} custom-call(f32[5,1,128,128]{3,2,1,0:T(8,128)S(1)} %get-tuple-element.38.source), custom_call_target="tpu_custom_call" | custom-call | tf_op jit(solution)/shard_map/store/pallas_call | solution.py:374
  42.7 6.4 %all-to-all-done = f32[32,1,128]{2,1,0:T(1,128)S(1)} async-done(((f32[32,1,128]{2,1,0:T(1,128)}), f32[32,1,128]{2,1,0:T(1,128)S(1)}, u32[]{:S(2)}, u32[]{:S(2)}) %all-to-all-start) | async-done | bytes 16416 | tf_op jit(solution)/shard_map/all_to_all | solution.py:373
  49.1 0.6 %reduce_sum.9 = f32[128]{0:T(128)} reduce(f32[32,1,128]{2,1,0:T(1,128)S(1)} %all-to-all-done, f32[]{:T(128)} %constant.16.clone.1), dimensions={0,1}, to_apply=%region_0.0 | reduce | flops 3968 | bytes 16900 | tf_op jit(solution)/shard_map/reduce_sum | solution.py:383
  (26 shorter events, 0.1 us)
Async XLA Ops:
  0.6 11.3 %copy-start = (f32[5,1,128,128]{3,2,1,0:T(8,128)S(1)}, f32[5,1,128,128]{3,2,1,0:T(8,128)}, u32[]{:S(2)}) copy-start(f32[5,1,128,128]{3,2,1,0:T(8,128)} %source.2) | copy-start | bytes 983044
  1.7 7.8 %collective-permute-start.2 = (f32[320,128]{1,0:T(8,128)S(1)}, f32[320,128]{1,0:T(8,128)S(1)}, u32[]{:S(2)}, u32[]{:S(2)}) collective-permute-start(f32[320,128]{1,0:T(8,128)S(1)} %get-tuple-element.40), channel_id=1, source_target_pairs={{8,0},{16,8},{24,16},{28,24},{20,28},{12,20},{4,12},{0,4},{9,1},{1... | collective-permute-start | bytes 491528 | tf_op jit(solution)/shard_map/ppermute | solution.py:286
  4.7 7.1 %collective-permute-start = (f32[320,128]{1,0:T(8,128)S(1)}, f32[320,128]{1,0:T(8,128)S(1)}, u32[]{:S(2)}, u32[]{:S(2)}) collective-permute-start(f32[320,128]{1,0:T(8,128)S(1)} %get-tuple-element.41), channel_id=1, source_target_pairs={{0,8},{8,16},{16,24},{24,28},{28,20},{20,12},{12,4},{4,0},{1,9},{9... | collective-permute-start | bytes 491528 | tf_op jit(solution)/shard_map/ppermute | solution.py:285
  4.8 12.3 %collective-permute-start.4 = (f32[320,128]{1,0:T(8,128)S(1)}, f32[320,128]{1,0:T(8,128)S(1)}, u32[]{:S(2)}, u32[]{:S(2)}) collective-permute-start(f32[320,128]{1,0:T(8,128)S(1)} %get-tuple-element.40), channel_id=1, source_target_pairs={{0,8},{8,16},{16,24},{24,28},{28,20},{20,12},{12,4},{4,0},{1,9},{9... | collective-permute-start | bytes 491528 | tf_op jit(solution)/shard_map/ppermute | solution.py:285
  6.8 10.3 %collective-permute-start.5 = (f32[320,128]{1,0:T(8,128)S(1)}, f32[320,128]{1,0:T(8,128)S(1)}, u32[]{:S(2)}, u32[]{:S(2)}) collective-permute-start(f32[320,128]{1,0:T(8,128)S(1)} %get-tuple-element.41), channel_id=1, source_target_pairs={{8,0},{16,8},{24,16},{28,24},{20,28},{12,20},{4,12},{0,4},{9,1},{1... | collective-permute-start | bytes 491528 | tf_op jit(solution)/shard_map/ppermute | solution.py:286
  9.5 12.9 %collective-permute-start.3 = (f32[320,128]{1,0:T(8,128)S(1)}, f32[320,128]{1,0:T(8,128)S(1)}, u32[]{:S(2)}, u32[]{:S(2)}) collective-permute-start(f32[320,128]{1,0:T(8,128)S(1)} %collective-permute-done.2.refs_3_), channel_id=1, source_target_pairs={{8,0},{16,8},{24,16},{28,24},{20,28},{12,20},{4,12},{0,4},{9,1},{1... | collective-permute-start | bytes 491528 | tf_op jit(solution)/shard_map/ppermute | solution.py:286
  11.8 10.7 %collective-permute-start.6 = (f32[320,128]{1,0:T(8,128)S(1)}, f32[320,128]{1,0:T(8,128)S(1)}, u32[]{:S(2)}, u32[]{:S(2)}) collective-permute-start(f32[320,128]{1,0:T(8,128)S(1)} %collective-permute-done.refs_0_), channel_id=1, source_target_pairs={{0,8},{8,16},{16,24},{24,28},{28,20},{20,12},{12,4},{4,0},{1,9},{9... | collective-permute-start | bytes 491528 | tf_op jit(solution)/shard_map/ppermute | solution.py:285
  11.9 8.6 %copy-start.5 = (s32[1,1,256]{2,1,0:T(1,128)S(1)}, s32[1,1,256]{2,1,0:T(1,128)}, u32[]{:S(2)}) copy-start(s32[1,1,256]{2,1,0:T(1,128)} %bins.1) | copy-start | bytes 3076
  11.9 8.6 %copy-start.6 = (f32[1,1,256]{2,1,0:T(1,128)S(1)}, f32[1,1,256]{2,1,0:T(1,128)}, u32[]{:S(2)}) copy-start(f32[1,1,256]{2,1,0:T(1,128)} %slot_weights.1) | copy-start | bytes 3076
  12.1 10.4 %collective-permute-start.1 = (f32[5,8,128]{2,1,0:T(8,128)S(1)}, f32[5,8,128]{2,1,0:T(8,128)S(1)}, u32[]{:S(2)}, u32[]{:S(2)}) collective-permute-start(f32[5,8,128]{2,1,0:T(8,128)S(1)} %edges.1), channel_id=1, source_target_pairs={{0,28},{8,20},{16,12},{24,4},{28,0},{20,8},{12,16},{4,24},{1,29},{... | collective-permute-start | bytes 61448 | tf_op jit(solution)/shard_map/ppermute | solution.py:298
  17.1 7.4 %collective-permute-start.7 = (f32[320,128]{1,0:T(8,128)S(1)}, f32[320,128]{1,0:T(8,128)S(1)}, u32[]{:S(2)}, u32[]{:S(2)}) collective-permute-start(f32[320,128]{1,0:T(8,128)S(1)} %collective-permute-done.4.refs_1_), channel_id=1, source_target_pairs={{0,8},{8,16},{16,24},{24,28},{28,20},{20,12},{12,4},{4,0},{1,9},{9... | collective-permute-start | bytes 491528 | tf_op jit(solution)/shard_map/ppermute | solution.py:285
  17.1 7.5 %collective-permute-start.8 = (f32[320,128]{1,0:T(8,128)S(1)}, f32[320,128]{1,0:T(8,128)S(1)}, u32[]{:S(2)}, u32[]{:S(2)}) collective-permute-start(f32[320,128]{1,0:T(8,128)S(1)} %collective-permute-done.5.refs_2_), channel_id=1, source_target_pairs={{8,0},{16,8},{24,16},{28,24},{20,28},{12,20},{4,12},{0,4},{9,1},{1... | collective-permute-start | bytes 491528 | tf_op jit(solution)/shard_map/ppermute | solution.py:286
  19.8 0.7 %copy-start.4 = (s32[1,1,256]{2,1,0:T(1,128)S(1)}, s32[1,1,256]{2,1,0:T(1,128)}, u32[]{:S(2)}) copy-start(s32[1,1,256]{2,1,0:T(1,128)} %cells.1) | copy-start | bytes 3076
  22.4 13.3 %copy-start.1 = (f32[3,1,128,128]{3,2,1,0:T(8,128)S(1)}, f32[3,1,128,128]{3,2,1,0:T(8,128)}, u32[]{:S(2)}) copy-start(f32[3,1,128,128]{3,2,1,0:T(8,128)} %velocity.1) | copy-start | bytes 589828
  22.4 13.3 %copy-start.2 = (f32[1,128,128]{2,1,0:T(8,128)S(1)}, f32[1,128,128]{2,1,0:T(8,128)}, u32[]{:S(2)}) copy-start(f32[1,128,128]{2,1,0:T(8,128)} %density.1) | copy-start | bytes 196612
  22.4 13.3 %copy-start.3 = (f32[1,128,128]{2,1,0:T(8,128)S(1)}, f32[1,128,128]{2,1,0:T(8,128)}, u32[]{:S(2)}) copy-start(f32[1,128,128]{2,1,0:T(8,128)} %pressure.1) | copy-start | bytes 196612
  22.5 6.6 %collective-permute-start.12 = (f32[320,128]{1,0:T(8,128)S(1)}, f32[320,128]{1,0:T(8,128)S(1)}, u32[]{:S(2)}, u32[]{:S(2)}) collective-permute-start(f32[320,128]{1,0:T(8,128)S(1)} %collective-permute-done.3.refs_7_), channel_id=1, source_target_pairs={{8,0},{16,8},{24,16},{28,24},{20,28},{12,20},{4,12},{0,4},{9,1},{1... | collective-permute-start | bytes 491528 | tf_op jit(solution)/shard_map/ppermute | solution.py:286
  22.5 7.1 %collective-permute-start.9 = (f32[320,128]{1,0:T(8,128)S(1)}, f32[320,128]{1,0:T(8,128)S(1)}, u32[]{:S(2)}, u32[]{:S(2)}) collective-permute-start(f32[320,128]{1,0:T(8,128)S(1)} %collective-permute-done.6.refs_4_), channel_id=1, source_target_pairs={{0,8},{8,16},{16,24},{24,28},{28,20},{20,12},{12,4},{4,0},{1,9},{9... | collective-permute-start | bytes 491528 | tf_op jit(solution)/shard_map/ppermute | solution.py:285
  24.5 6.9 %collective-permute-start.10 = (f32[320,128]{1,0:T(8,128)S(1)}, f32[320,128]{1,0:T(8,128)S(1)}, u32[]{:S(2)}, u32[]{:S(2)}) collective-permute-start(f32[320,128]{1,0:T(8,128)S(1)} %collective-permute-done.7.refs_5_), channel_id=1, source_target_pairs={{0,8},{8,16},{16,24},{24,28},{28,20},{20,12},{12,4},{4,0},{1,9},{9... | collective-permute-start | bytes 491528 | tf_op jit(solution)/shard_map/ppermute | solution.py:285
  24.6 6.8 %collective-permute-start.11 = (f32[320,128]{1,0:T(8,128)S(1)}, f32[320,128]{1,0:T(8,128)S(1)}, u32[]{:S(2)}, u32[]{:S(2)}) collective-permute-start(f32[320,128]{1,0:T(8,128)S(1)} %collective-permute-done.8.refs_6_), channel_id=1, source_target_pairs={{8,0},{16,8},{24,16},{28,24},{20,28},{12,20},{4,12},{0,4},{9,1},{1... | collective-permute-start | bytes 491528 | tf_op jit(solution)/shard_map/ppermute | solution.py:286
  29.1 6.6 %collective-permute-start.14 = (f32[320,128]{1,0:T(8,128)S(1)}, f32[320,128]{1,0:T(8,128)S(1)}, u32[]{:S(2)}, u32[]{:S(2)}) collective-permute-start(f32[320,128]{1,0:T(8,128)S(1)} %collective-permute-done.12.refs_11_), channel_id=1, source_target_pairs={{8,0},{16,8},{24,16},{28,24},{20,28},{12,20},{4,12},{0,4},{9,1},{1... | collective-permute-start | bytes 491528 | tf_op jit(solution)/shard_map/ppermute | solution.py:324
  29.6 6.1 %collective-permute-start.13 = (f32[320,128]{1,0:T(8,128)S(1)}, f32[320,128]{1,0:T(8,128)S(1)}, u32[]{:S(2)}, u32[]{:S(2)}) collective-permute-start(f32[320,128]{1,0:T(8,128)S(1)} %collective-permute-done.9.refs_8_), channel_id=1, source_target_pairs={{0,8},{8,16},{16,24},{24,28},{28,20},{20,12},{12,4},{4,0},{1,9},{9... | collective-permute-start | bytes 491528 | tf_op jit(solution)/shard_map/ppermute | solution.py:323
  32.4 1.7 %collective-permute-start.15 = (f32[5,8,128]{2,1,0:T(8,128)S(1)}, f32[5,8,128]{2,1,0:T(8,128)S(1)}, u32[]{:S(2)}, u32[]{:S(2)}) collective-permute-start(f32[5,8,128]{2,1,0:T(8,128)S(1)} %get-tuple-element.33), channel_id=1, source_target_pairs={{0,1},{1,0},{2,3},{3,2},{4,5},{5,4},{6,7},{7,6},{8,9},{9,8},{10,11... | collective-permute-start | bytes 61448 | tf_op jit(solution)/shard_map/ppermute | solution.py:341
  32.4 3.3 %collective-permute-start.16 = (f32[5,8,128]{2,1,0:T(8,128)S(1)}, f32[5,8,128]{2,1,0:T(8,128)S(1)}, u32[]{:S(2)}, u32[]{:S(2)}) collective-permute-start(f32[5,8,128]{2,1,0:T(8,128)S(1)} %get-tuple-element.33), channel_id=1, source_target_pairs={{0,3},{1,2},{2,1},{3,0},{4,7},{5,6},{6,5},{7,4},{8,11},{9,10},{10,... | collective-permute-start | bytes 61448 | tf_op jit(solution)/shard_map/ppermute | solution.py:341
  37.8 11.4 %all-to-all-start = ((f32[32,1,128]{2,1,0:T(1,128)}), f32[32,1,128]{2,1,0:T(1,128)S(1)}, u32[]{:S(2)}, u32[]{:S(2)}) async-start(f32[32,1,128]{2,1,0:T(1,128)} %bitcast.3), calls=%async_computation | async-start | bytes 32768 | tf_op jit(solution)/shard_map/all_to_all | solution.py:373

commit v5 on v4

--- a/solution.py
+++ b/solution.py
@@ -108,20 +108,51 @@
         edges[field] = packed_edges(tiles) + weights[0, count - 1] * last_edges[field]
 
 
-def slots_body(live_count, cells, bins, slot_weights, column, line, owner, place):
-    slots = cells.shape[2]
+def slots_body(
+    live_count,
+    cells,
+    bins,
+    slot_weights,
+    density,
+    velocity,
+    pressure,
+    column,
+    line,
+    owner,
+    place,
+    edge_column,
+    edge_line,
+    flow_edges,
+):
+    slots, radial = cells.shape[2], density.shape[1]
     cell, own_bin = cells[0], bins[0]
     order = lax.broadcasted_iota(jnp.int32, (1, slots), 1)
     weight = jnp.where(order < live_count[0, 0], slot_weights[0], 0.0)
+    x = cell & (LANES - 1)
+    row = lax.shift_right_logical(cell, LANES.bit_length() - 1)
 
     def table(target, index, value):
         rows = lax.broadcasted_iota(jnp.int32, target.shape, 0)
         target[...] = jnp.where(rows == index, value, 0.0).astype(target.dtype)
 
-    table(column, cell & (LANES - 1), 1.0)
-    table(line, lax.shift_right_logical(cell, LANES.bit_length() - 1), weight)
+    table(column, x, 1.0)
+    table(line, row, weight)
     table(owner, own_bin // BIN_DEV, 1.0)
     table(place, own_bin % BIN_DEV, 1.0)
+    base = SLOT * lax.shift_right_logical(row, TILE.bit_length() - 1)
+    outer = jnp.where(x >= LANES - EDGE, base + (x - (LANES - EDGE)), -1)
+    table(edge_column, jnp.where(x < EDGE, base + EDGE + x, outer), 1.0)
+    table(edge_line, row & (TILE - 1), weight)
+    for which, make in enumerate(
+        (
+            lambda rows: velocity[0, 0, rows, :],
+            lambda rows: density[0, rows, :],
+            lambda rows: GAMMA_GAS * pressure[0, rows, :],
+            lambda rows: 1.0 / density[0, rows, :],
+        )
+    ):
+        tiles = [make(pl.ds(at, TILE)) for at in range(0, radial, TILE)]
+        flow_edges[which] = packed_edges(tiles)
 
 
 def three_parts(value):
@@ -138,27 +169,25 @@
     return stacked[:rows] + (stacked[rows : 2 * rows] + stacked[2 * rows :])
 
 
-def final_body(
-    blocks_x,
+def axial_coefs():
+    unit = SECTION_STEP / (60.0 * AXIAL_STEP)
+    return [np.float32(c * unit) for c in (45.0, -9.0, 1.0)]
+
+
+def bulk_body(
     weights,
-    place_x,
     smooth,
     slope,
     last_first,
     last_second,
-    edges_pair,
-    edges_next,
     density,
     velocity,
     pressure,
     column,
     line,
-    owner,
-    place,
     section,
-    totals,
+    values,
     filtered,
-    halos,
     picked,
 ):
     fields, radial = section.shape[0], section.shape[2]
@@ -172,23 +201,16 @@
 
     lane = lax.broadcasted_iota(jnp.int32, (TILE, LANES), 1)
     sub = lax.broadcasted_iota(jnp.int32, (TILE, LANES), 0)
-    odd = (place_x[0, 0] & 1) == 1
-    paired = ((lane & (SLOT - 1)) < EDGE) == odd
-    inner = jnp.where((place_x[0, 0] == 0) | (place_x[0, 0] == blocks_x - 1), 0.0, 1.0)
     pad = jnp.zeros((TILE, LANES), jnp.float32)
     for field in range(fields):
         filtered[field, pl.ds(0, TILE), :] = pad
         filtered[field, pl.ds(TILE + radial, TILE), :] = pad
-        packed = jnp.where(paired, edges_pair[field], inner * edges_next[field])
         for row in range(0, radial, TILE):
             at = field * radial + row
             value = smooth[pl.ds(at, TILE), :] + last_weight * last(at)
             filtered[field, pl.ds(TILE + row, TILE), :] = value
-            edge = pltpu.roll(packed, LANES - (SLOT * (row // TILE) + EDGE), 1)
-            halos[field, pl.ds(row, TILE), :] = edge
-
-    unit = SECTION_STEP / (60.0 * AXIAL_STEP)
-    axial = [np.float32(c * unit) for c in (45.0, -9.0, 1.0)]
+
+    axial = axial_coefs()
     unit = SECTION_STEP / (60.0 * RADIAL_STEP)
     radially = [np.float32(c * unit) for c in (45.0, -9.0, 1.0)]
 
@@ -199,11 +221,10 @@
         stretch = SECTION_STEP / cell_radius
         for field in range(fields):
             here = filtered[field, pl.ds(TILE + row, TILE), :]
-            edge = halos[field, rows, :]
             total = None
             for k in range(1, EDGE + 1):
-                ahead = pltpu.roll(jnp.where(lane < k, edge, here), LANES - k, 1)
-                behind = pltpu.roll(jnp.where(lane >= LANES - k, edge, here), k, 1)
+                ahead = pltpu.roll(jnp.where(lane < k, 0.0, here), LANES - k, 1)
+                behind = pltpu.roll(jnp.where(lane >= LANES - k, 0.0, here), k, 1)
                 term = axial[k - 1] * (ahead - behind)
                 total = term if total is None else total + term
             g.append(total)
@@ -234,8 +255,53 @@
         picked[rows, :] = out[4] + out[1]
 
     lines = jnp.dot(three_parts(picked[...]), column[...], preferred_element_type=jnp.float32)
-    values = jnp.sum(line[...] * add_parts(lines), axis=0, keepdims=True)
-    spread = three_parts(owner[...] * values)
+    values[...] = jnp.sum(line[...] * add_parts(lines), axis=0, keepdims=True)
+
+
+def close_body(
+    blocks_x,
+    place_x,
+    edges_pair,
+    edges_next,
+    flow_edges,
+    values,
+    edge_column,
+    edge_line,
+    owner,
+    place,
+    fixes,
+    totals,
+):
+    fields = fixes.shape[0]
+    lane = lax.broadcasted_iota(jnp.int32, (TILE, LANES), 1)
+    slot = lane & (SLOT - 1)
+    odd = (place_x[0, 0] & 1) == 1
+    paired = (slot < EDGE) == odd
+    inner = jnp.where((place_x[0, 0] == 0) | (place_x[0, 0] == blocks_x - 1), 0.0, 1.0)
+    g = []
+    for field in range(fields):
+        halo = jnp.where(paired, edges_pair[field], inner * edges_next[field])
+        total = None
+        for k, coef in enumerate(axial_coefs(), 1):
+            after = jnp.where(slot + k >= EDGE, pltpu.roll(halo, LANES - k, 1), 0.0)
+            before = jnp.where(slot - k < EDGE, pltpu.roll(halo, k, 1), 0.0)
+            term = coef * jnp.where(slot < EDGE, after, -before)
+            total = term if total is None else total + term
+        g.append(total)
+    u, rho, stiff, inverse = (flow_edges[i] for i in range(4))
+    out = [
+        u * g[0],
+        u * g[1] + rho * g[0] + stiff * g[4],
+        u * g[2],
+        u * g[3],
+        u * g[4] + inverse * g[1],
+    ]
+    for field in range(fields):
+        fixes[field] = out[field]
+    seen = jnp.concatenate([out[4] + out[1], jnp.zeros((TILE, LANES), jnp.float32)], axis=0)
+    lines = jnp.dot(three_parts(seen), edge_column[...], preferred_element_type=jnp.float32)
+    share = jnp.sum(edge_line[...] * add_parts(lines)[:TILE], axis=0, keepdims=True)
+    spread = three_parts(owner[...] * (values[...] + share))
     totals[...] = add_parts(
         lax.dot_general(
             spread, place[...], (((1,), (1,)), ((), ())), preferred_element_type=jnp.float32
@@ -243,10 +309,15 @@
     )
 
 
-def store_body(source, target, semaphore):
-    copy = pltpu.make_async_copy(source, target, semaphore)
-    copy.start()
-    copy.wait()
+def store_body(held, fixes, section):
+    fields, radial = section.shape[0], section.shape[2]
+    lane = lax.broadcasted_iota(jnp.int32, (TILE, LANES), 1)
+    outer = (lane < EDGE) | (lane >= LANES - EDGE)
+    for field in range(fields):
+        for row in range(0, radial, TILE):
+            rows = pl.ds(row, TILE)
+            fix = pltpu.roll(fixes[field], LANES - (SLOT * (row // TILE) + EDGE), 1)
+            section[field, 0, rows, :] = held[field, 0, rows, :] + jnp.where(outer, fix, 0.0)
 
 
 def in_vmem(count):
@@ -309,12 +380,15 @@
                     jax.ShapeDtypeStruct((radial, slots), f32),
                     jax.ShapeDtypeStruct((devices, slots), f32),
                     jax.ShapeDtypeStruct((LANES, slots), jnp.bfloat16),
+                    jax.ShapeDtypeStruct((LANES, slots), jnp.bfloat16),
+                    jax.ShapeDtypeStruct((TILE, slots), f32),
+                    jax.ShapeDtypeStruct((4, TILE, LANES), f32),
                 ),
-                in_specs=in_smem(1) + in_vmem(3),
-                out_specs=tuple(in_vmem(4)),
+                in_specs=in_smem(1) + in_vmem(6),
+                out_specs=tuple(in_vmem(7)),
                 compiler_params=params,
                 name="slots",
-            )(fwh_count, fwh_cell, fwh_bin, fwh_weight)
+            )(fwh_count, fwh_cell, fwh_bin, fwh_weight, density, velocity, pressure)
         if step == 1:
             weights, tables, from_right[1] = lax.optimization_barrier(
                 (weights, tables, from_right[1])
@@ -341,45 +415,60 @@
     edges_next, edges_pair = lax.ppermute(edges, "rx", nexts), lax.ppermute(edges, "rx", pairs)
     place_x = jnp.reshape(lax.axis_index("rx"), (1, 1))
 
-    held, totals = pl.pallas_call(
-        functools.partial(final_body, blocks_x),
+    column, line, owner, place, edge_column, edge_line, flow_edges = tables
+    held, values = pl.pallas_call(
+        bulk_body,
         out_shape=(
             jax.ShapeDtypeStruct(adjoint.shape, f32),
-            jax.ShapeDtypeStruct((devices, LANES), f32),
+            jax.ShapeDtypeStruct((1, slots), f32),
         ),
-        in_specs=in_smem(2) + in_vmem(13),
+        in_specs=in_smem(1) + in_vmem(9),
         out_specs=tuple(in_vmem(2)),
         scratch_shapes=[
             pltpu.VMEM((fields, radial + 2 * TILE, LANES), f32),
-            pltpu.VMEM((fields, radial, LANES), f32),
             pltpu.VMEM((radial, LANES), f32),
         ],
         compiler_params=params,
-        name="section",
+        name="bulk",
     )(
         weights,
-        place_x,
         smooth,
         slope,
         last_first,
         last_second,
-        edges_pair,
-        edges_next,
         density,
         velocity,
         pressure,
-        *tables,
+        column,
+        line,
+    )
+    fixes, totals = pl.pallas_call(
+        functools.partial(close_body, blocks_x),
+        out_shape=(edge_shape, jax.ShapeDtypeStruct((devices, LANES), f32)),
+        in_specs=in_smem(1) + in_vmem(8),
+        out_specs=tuple(in_vmem(2)),
+        compiler_params=params,
+        name="close",
+    )(
+        place_x,
+        edges_pair,
+        edges_next,
+        flow_edges,
+        values,
+        edge_column,
+        edge_line,
+        owner,
+        place,
     )
     totals = lax.all_to_all(totals, ("az", "rx"), 0, 0, tiled=True)
     section = pl.pallas_call(
         store_body,
         out_shape=jax.ShapeDtypeStruct(adjoint.shape, f32),
-        in_specs=[pl.BlockSpec(memory_space=pl.ANY)],
-        out_specs=pl.BlockSpec(memory_space=pl.ANY),
-        scratch_shapes=[pltpu.SemaphoreType.DMA],
+        in_specs=in_vmem(2),
+        out_specs=in_vmem(1)[0],
         compiler_params=params,
         name="store",
-    )(held)
+    )(held, fixes)
     return section, jnp.sum(totals, axis=0)[:BIN_DEV]
 
 

time: 49.9 us -> 48.8 us (0.978)
  waiting for transfers between devices: 15.2 us -> 14 us
    ppermute x1, waiting for transfers between devices: 1.63 us -> 0.01 us  [local(): lax.ppermute(edges, 'rx', nexts)]
    ppermute x1, waiting for transfers between devices: 0.01 us -> 0.62 us  [local(): last_first = lax.ppermute(from_left[0], 'az', onward)]
    pallas_call x1 -> x2, Pallas kernels: 2.03 us -> 2.2 us  [the longest x1 1.21 us: local(): pl.pallas_call(bulk_body, out_shape=(jax.ShapeDtypeStruct(adjoint.shape,...]
  transfers between devices with their start and end apart: 18 -> 18, of which waited for: 6 -> 7; matrix products, arithmetic and copies ran while one was open for 1% -> 1% of each run, Pallas kernels for 4% -> 7%
where the time goes in v5:
time: 48.8 us; the launch traced here: 48.6 us
  starting transfers between devices  26.5 us (54%)
  waiting for transfers between devices  14 us (29%)
  Pallas kernels  4.32 us (9%)
  local copies, waits for them, and re-layouts  1.79 us (4%)
  between operations  1.44 us (3%)
  other arithmetic  0.56 us (1%)
    ppermute x6, starting transfers between devices, local(): right.append(lax.ppermute(from_right[part], 'az', back))  9.34 us
    all_to_all x1, waiting for transfers between devices, local(): totals = lax.all_to_all(totals, ('az', 'rx'), 0, 0, tiled=True)  6.27 us
    ppermute x6, waiting for transfers between devices, local(): right.append(lax.ppermute(from_right[part], 'az', back))  5.04 us
    ppermute x1, starting transfers between devices, local(): last_edges = lax.ppermute(last_edges, 'az', across)  5.02 us
    ppermute x6, starting transfers between devices, local(): left.append(lax.ppermute(from_left[part], 'az', onward))  4.3 us
    all_to_all x1, starting transfers between devices, local(): totals = lax.all_to_all(totals, ('az', 'rx'), 0, 0, tiled=True)  3.8 us
    ppermute x1, starting transfers between devices, local(): last_first = lax.ppermute(from_left[0], 'az', onward)  1.71 us
    ppermute x1, waiting for transfers between devices, local(): last_edges = lax.ppermute(last_edges, 'az', across)  1.69 us
  transfers between devices with their start and end apart: 18, of which 7 were waited for; matrix products, arithmetic and copies ran while one was open for 1% of the time, Pallas kernels for 7%

profile of v5, /device:TPU:0, one launch (start us, length us, event | category | flops | bytes accessed | tf_op | source)
XLA Modules:
  0.0 48.6 jit_solution(7433690515459575775)
XLA Ops:
  0.6 1.1 %fusion = (f32[320,128]{1,0:T(8,128)S(1)}, f32[320,128]{1,0:T(8,128)S(1)}) fusion(f32[640,128]{1,0:T(8,128)} %bitcast.6), kind=kLoop, calls=%fused_computation.1 | loop fusion | bytes 655360 | tf_op jit(solution)/shard_map/slice | solution.py:349
  1.7 3.0 %collective-permute-start.2 = (f32[320,128]{1,0:T(8,128)S(1)}, f32[320,128]{1,0:T(8,128)S(1)}, u32[]{:S(2)}, u32[]{:S(2)}) collective-permute-start(f32[320,128]{1,0:T(8,128)S(1)} %get-tuple-element.56), channel_id=1, source_target_pairs={{8,0},{16,8},{24,16},{28,24},{20,28},{12,20},{4,12},{0,4},{9,1},{1... | collective-permute-start | bytes 491528 | tf_op jit(solution)/shard_map/ppermute | solution.py:357
  4.7 0.2 collective-permute-start
  4.9 2.0 %collective-permute-start.4 = (f32[320,128]{1,0:T(8,128)S(1)}, f32[320,128]{1,0:T(8,128)S(1)}, u32[]{:S(2)}, u32[]{:S(2)}) collective-permute-start(f32[320,128]{1,0:T(8,128)S(1)} %get-tuple-element.56), channel_id=1, source_target_pairs={{0,8},{8,16},{16,24},{24,28},{28,20},{20,12},{12,4},{4,0},{1,9},{9... | collective-permute-start | bytes 491528 | tf_op jit(solution)/shard_map/ppermute | solution.py:356
  6.8 0.1 collective-permute-start.5
  6.9 2.6 %collective-permute-done.2.refs_3_ = f32[320,128]{1,0:T(8,128)S(1)} collective-permute-done((f32[320,128]{1,0:T(8,128)S(1)}, f32[320,128]{1,0:T(8,128)S(1)}, u32[]{:S(2)}, u32[]{:S(2)}) %collective-permute-start.2) | collective-permute-done | bytes 163872 | tf_op jit(solution)/shard_map/ppermute | solution.py:357
  9.5 2.3 %collective-permute-start.3 = (f32[320,128]{1,0:T(8,128)S(1)}, f32[320,128]{1,0:T(8,128)S(1)}, u32[]{:S(2)}, u32[]{:S(2)}) collective-permute-start(f32[320,128]{1,0:T(8,128)S(1)} %collective-permute-done.2.refs_3_), channel_id=1, source_target_pairs={{8,0},{16,8},{24,16},{28,24},{20,28},{12,20},{4,12},{0,4},{9,1},{1... | collective-permute-start | bytes 491528 | tf_op jit(solution)/shard_map/ppermute | solution.py:357
  11.8 0.1 collective-permute-start.6
  12.0 0.1 edges.1
  12.1 5.0 %collective-permute-start.1 = (f32[5,8,128]{2,1,0:T(8,128)S(1)}, f32[5,8,128]{2,1,0:T(8,128)S(1)}, u32[]{:S(2)}, u32[]{:S(2)}) collective-permute-start(f32[5,8,128]{2,1,0:T(8,128)S(1)} %edges.1), channel_id=1, source_target_pairs={{0,28},{8,20},{16,12},{24,4},{28,0},{20,8},{12,16},{4,24},{1,29},{... | collective-permute-start | bytes 61448 | tf_op jit(solution)/shard_map/ppermute | solution.py:369
  17.1 2.0 %collective-permute-start.8 = (f32[320,128]{1,0:T(8,128)S(1)}, f32[320,128]{1,0:T(8,128)S(1)}, u32[]{:S(2)}, u32[]{:S(2)}) collective-permute-start(f32[320,128]{1,0:T(8,128)S(1)} %collective-permute-done.5.refs_2_), channel_id=1, source_target_pairs={{8,0},{16,8},{24,16},{28,24},{20,28},{12,20},{4,12},{0,4},{9,1},{1... | collective-permute-start | bytes 491528 | tf_op jit(solution)/shard_map/ppermute | solution.py:357
  19.2 0.7 %constant_dynamic-slice_fusion.weights = f32[1,16]{1,0:T(1,128)S(1)} fusion(f32[8,16]{1,0:T(8,128)} %constant.17.clone, s32[]{:T(128)S(6)} %select_n.3), kind=kLoop, calls=%fused_computation | loop fusion | bytes 132 | tf_op jit(solution)/shard_map/dynamic_slice | solution.py:373
  20.6 0.2 slots.1
  20.8 1.7 %collective-permute-done.1.last_edges = f32[5,8,128]{2,1,0:T(8,128)S(1)} collective-permute-done((f32[5,8,128]{2,1,0:T(8,128)S(1)}, f32[5,8,128]{2,1,0:T(8,128)S(1)}, u32[]{:S(2)}, u32[]{:S(2)}) %collective-permute-start.1) | collective-permute-done | bytes 20512 | tf_op jit(solution)/shard_map/ppermute | solution.py:369
  22.5 2.0 %collective-permute-start.9 = (f32[320,128]{1,0:T(8,128)S(1)}, f32[320,128]{1,0:T(8,128)S(1)}, u32[]{:S(2)}, u32[]{:S(2)}) collective-permute-start(f32[320,128]{1,0:T(8,128)S(1)} %collective-permute-done.6.refs_4_), channel_id=1, source_target_pairs={{0,8},{8,16},{16,24},{24,28},{28,20},{20,12},{12,4},{4,0},{1,9},{9... | collective-permute-start | bytes 491528 | tf_op jit(solution)/shard_map/ppermute | solution.py:356
  24.5 0.1 collective-permute-start.10
  24.6 2.0 %collective-permute-start.11 = (f32[320,128]{1,0:T(8,128)S(1)}, f32[320,128]{1,0:T(8,128)S(1)}, u32[]{:S(2)}, u32[]{:S(2)}) collective-permute-start(f32[320,128]{1,0:T(8,128)S(1)} %collective-permute-done.8.refs_6_), channel_id=1, source_target_pairs={{8,0},{16,8},{24,16},{28,24},{20,28},{12,20},{4,12},{0,4},{9,1},{1... | collective-permute-start | bytes 491528 | tf_op jit(solution)/shard_map/ppermute | solution.py:357
  26.5 2.4 %collective-permute-done.12.refs_11_ = f32[320,128]{1,0:T(8,128)S(1)} collective-permute-done((f32[320,128]{1,0:T(8,128)S(1)}, f32[320,128]{1,0:T(8,128)S(1)}, u32[]{:S(2)}, u32[]{:S(2)}) %collective-permute-start.12) | collective-permute-done | bytes 163872 | tf_op jit(solution)/shard_map/ppermute | solution.py:357
  28.9 0.6 %collective-permute-start.14 = (f32[320,128]{1,0:T(8,128)S(1)}, f32[320,128]{1,0:T(8,128)S(1)}, u32[]{:S(2)}, u32[]{:S(2)}) collective-permute-start(f32[320,128]{1,0:T(8,128)S(1)} %collective-permute-done.12.refs_11_), channel_id=1, source_target_pairs={{8,0},{16,8},{24,16},{28,24},{20,28},{12,20},{4,12},{0,4},{9,1},{1... | collective-permute-start | bytes 491528 | tf_op jit(solution)/shard_map/ppermute | solution.py:398
  29.5 1.7 %collective-permute-start.13 = (f32[320,128]{1,0:T(8,128)S(1)}, f32[320,128]{1,0:T(8,128)S(1)}, u32[]{:S(2)}, u32[]{:S(2)}) collective-permute-start(f32[320,128]{1,0:T(8,128)S(1)} %collective-permute-done.9.refs_8_), channel_id=1, source_target_pairs={{0,8},{8,16},{16,24},{24,28},{28,20},{20,12},{12,4},{4,0},{1,9},{9... | collective-permute-start | bytes 491528 | tf_op jit(solution)/shard_map/ppermute | solution.py:397
  31.3 0.2 collective-permute-done.10.refs_9_
  31.5 0.9 %partial.1 = (f32[640,128]{1,0:T(8,128)S(1)}, f32[640,128]{1,0:T(8,128)S(1)}, f32[5,8,128]{2,1,0:T(8,128)S(1)}) custom-call(f32[1,16]{1,0:T(1,128)S(1)} %constant_dynamic-slice_fusion.weights, f32[5,1,128,128]{3,2,1,0:T(8,128)S(1)} %copy-done, f32[5,8,128]{2,1,0:T(8,128)S(1)} %collective-permute-done.1.last_edges, ...), custom_call_target="tpu_custom_call" | custom-call | tf_op jit(solution)/shard_map/partial/pallas_call | solution.py:401
  32.4 0.1 collective-permute-start.15
  32.5 1.6 %collective-permute-start.16 = (f32[5,8,128]{2,1,0:T(8,128)S(1)}, f32[5,8,128]{2,1,0:T(8,128)S(1)}, u32[]{:S(2)}, u32[]{:S(2)}) collective-permute-start(f32[5,8,128]{2,1,0:T(8,128)S(1)} %get-tuple-element.47), channel_id=1, source_target_pairs={{0,3},{1,2},{2,1},{3,0},{4,7},{5,6},{6,5},{7,4},{8,11},{9,10},{10,... | collective-permute-start | bytes 61448 | tf_op jit(solution)/shard_map/ppermute | solution.py:415
  34.1 0.2 collective-permute-done.14.last_second
  34.2 0.6 %collective-permute-done.13.last_first = f32[320,128]{1,0:T(8,128)S(1)} collective-permute-done((f32[320,128]{1,0:T(8,128)S(1)}, f32[320,128]{1,0:T(8,128)S(1)}, u32[]{:S(2)}, u32[]{:S(2)}) %collective-permute-start.13) | collective-permute-done | bytes 163872 | tf_op jit(solution)/shard_map/ppermute | solution.py:397
  34.9 1.2 %bulk.1 = (f32[5,1,128,128]{3,2,1,0:T(8,128)S(1)}, f32[1,256]{1,0:T(1,128)S(1)}) custom-call(f32[1,16]{1,0:T(1,128)S(1)} %constant_dynamic-slice_fusion.weights, f32[640,128]{1,0:T(8,128)S(1)} %get-tuple-element.42.smooth, f32[640,128]{1,0:T(8,128)S(1)} %get-tuple-element.43.slope, f32[320,128]{1,0:T(8,128)S(1)} %collective-permute-done.13.last_first, ...), custom_call_target="tpu_custom_call" | custom-call | tf_op jit(solution)/shard_map/bulk/pallas_call | solution.py:419
  36.1 1.0 %close.1 = (f32[5,8,128]{2,1,0:T(8,128)S(1)}, f32[32,128]{1,0:T(8,128)}) custom-call(s32[1,1]{1,0:T(1,128)} %bitcast.1.place_x, f32[5,8,128]{2,1,0:T(8,128)S(1)} %collective-permute-done.15.edges_pair, f32[5,8,128]{2,1,0:T(8,128)S(1)} %collective-permute-done.16.edges_next, f32[4,8,128]{2,1,0:T(8,128)S(1)} %get-tuple-element.48.flow_edges, ...), custom_call_target="tpu_custom_call" | custom-call | tf_op jit(solution)/shard_map/close/pallas_call | solution.py:445
  37.1 3.8 %all-to-all-start = ((f32[32,1,128]{2,1,0:T(1,128)}), f32[32,1,128]{2,1,0:T(1,128)S(1)}, u32[]{:S(2)}, u32[]{:S(2)}) async-start(f32[32,1,128]{2,1,0:T(1,128)} %bitcast.3), calls=%async_computation | async-start | bytes 32768 | tf_op jit(solution)/shard_map/all_to_all | solution.py:463
  40.9 0.9 %store.1 = f32[5,1,128,128]{3,2,1,0:T(8,128)} custom-call(f32[5,1,128,128]{3,2,1,0:T(8,128)S(1)} %get-tuple-element.46.held, f32[5,8,128]{2,1,0:T(8,128)S(1)} %get-tuple-element.54.fixes), custom_call_target="tpu_custom_call" | custom-call | tf_op jit(solution)/shard_map/store/pallas_call | solution.py:464
  41.8 6.3 %all-to-all-done = f32[32,1,128]{2,1,0:T(1,128)S(1)} async-done(((f32[32,1,128]{2,1,0:T(1,128)}), f32[32,1,128]{2,1,0:T(1,128)S(1)}, u32[]{:S(2)}, u32[]{:S(2)}) %all-to-all-start) | async-done | bytes 16416 | tf_op jit(solution)/shard_map/all_to_all | solution.py:463
  48.0 0.6 %reduce_sum.9 = f32[128]{0:T(128)} reduce(f32[32,1,128]{2,1,0:T(1,128)S(1)} %all-to-all-done, f32[]{:T(128)} %constant.16.clone.1), dimensions={0,1}, to_apply=%region_0.0 | reduce | flops 3968 | bytes 16900 | tf_op jit(solution)/shard_map/reduce_sum | solution.py:472
  (27 shorter events, 0.1 us)
Async XLA Ops:
  0.6 11.3 %copy-start = (f32[5,1,128,128]{3,2,1,0:T(8,128)S(1)}, f32[5,1,128,128]{3,2,1,0:T(8,128)}, u32[]{:S(2)}) copy-start(f32[5,1,128,128]{3,2,1,0:T(8,128)} %source.2) | copy-start | bytes 983044
  1.7 18.8 %copy-start.1 = (f32[3,1,128,128]{3,2,1,0:T(8,128)S(1)}, f32[3,1,128,128]{3,2,1,0:T(8,128)}, u32[]{:S(2)}) copy-start(f32[3,1,128,128]{3,2,1,0:T(8,128)} %velocity.3) | copy-start | bytes 589828
  1.7 7.8 %collective-permute-start.2 = (f32[320,128]{1,0:T(8,128)S(1)}, f32[320,128]{1,0:T(8,128)S(1)}, u32[]{:S(2)}, u32[]{:S(2)}) collective-permute-start(f32[320,128]{1,0:T(8,128)S(1)} %get-tuple-element.56), channel_id=1, source_target_pairs={{8,0},{16,8},{24,16},{28,24},{20,28},{12,20},{4,12},{0,4},{9,1},{1... | collective-permute-start | bytes 491528 | tf_op jit(solution)/shard_map/ppermute | solution.py:357
  4.7 7.1 %collective-permute-start = (f32[320,128]{1,0:T(8,128)S(1)}, f32[320,128]{1,0:T(8,128)S(1)}, u32[]{:S(2)}, u32[]{:S(2)}) collective-permute-start(f32[320,128]{1,0:T(8,128)S(1)} %get-tuple-element.57), channel_id=1, source_target_pairs={{0,8},{8,16},{16,24},{24,28},{28,20},{20,12},{12,4},{4,0},{1,9},{9... | collective-permute-start | bytes 491528 | tf_op jit(solution)/shard_map/ppermute | solution.py:356
  4.9 12.3 %collective-permute-start.4 = (f32[320,128]{1,0:T(8,128)S(1)}, f32[320,128]{1,0:T(8,128)S(1)}, u32[]{:S(2)}, u32[]{:S(2)}) collective-permute-start(f32[320,128]{1,0:T(8,128)S(1)} %get-tuple-element.56), channel_id=1, source_target_pairs={{0,8},{8,16},{16,24},{24,28},{28,20},{20,12},{12,4},{4,0},{1,9},{9... | collective-permute-start | bytes 491528 | tf_op jit(solution)/shard_map/ppermute | solution.py:356
  6.8 10.3 %collective-permute-start.5 = (f32[320,128]{1,0:T(8,128)S(1)}, f32[320,128]{1,0:T(8,128)S(1)}, u32[]{:S(2)}, u32[]{:S(2)}) collective-permute-start(f32[320,128]{1,0:T(8,128)S(1)} %get-tuple-element.57), channel_id=1, source_target_pairs={{8,0},{16,8},{24,16},{28,24},{20,28},{12,20},{4,12},{0,4},{9,1},{1... | collective-permute-start | bytes 491528 | tf_op jit(solution)/shard_map/ppermute | solution.py:357
  9.5 12.9 %collective-permute-start.3 = (f32[320,128]{1,0:T(8,128)S(1)}, f32[320,128]{1,0:T(8,128)S(1)}, u32[]{:S(2)}, u32[]{:S(2)}) collective-permute-start(f32[320,128]{1,0:T(8,128)S(1)} %collective-permute-done.2.refs_3_), channel_id=1, source_target_pairs={{8,0},{16,8},{24,16},{28,24},{20,28},{12,20},{4,12},{0,4},{9,1},{1... | collective-permute-start | bytes 491528 | tf_op jit(solution)/shard_map/ppermute | solution.py:357
  11.8 10.6 %collective-permute-start.6 = (f32[320,128]{1,0:T(8,128)S(1)}, f32[320,128]{1,0:T(8,128)S(1)}, u32[]{:S(2)}, u32[]{:S(2)}) collective-permute-start(f32[320,128]{1,0:T(8,128)S(1)} %collective-permute-done.refs_0_), channel_id=1, source_target_pairs={{0,8},{8,16},{16,24},{24,28},{28,20},{20,12},{12,4},{4,0},{1,9},{9... | collective-permute-start | bytes 491528 | tf_op jit(solution)/shard_map/ppermute | solution.py:356
  11.9 8.6 %copy-start.2 = (f32[1,128,128]{2,1,0:T(8,128)S(1)}, f32[1,128,128]{2,1,0:T(8,128)}, u32[]{:S(2)}) copy-start(f32[1,128,128]{2,1,0:T(8,128)} %density.3) | copy-start | bytes 196612
  12.0 8.6 %copy-start.3 = (f32[1,128,128]{2,1,0:T(8,128)S(1)}, f32[1,128,128]{2,1,0:T(8,128)}, u32[]{:S(2)}) copy-start(f32[1,128,128]{2,1,0:T(8,128)} %pressure.3) | copy-start | bytes 196612
  12.0 8.6 %copy-start.5 = (s32[1,1,256]{2,1,0:T(1,128)S(1)}, s32[1,1,256]{2,1,0:T(1,128)}, u32[]{:S(2)}) copy-start(s32[1,1,256]{2,1,0:T(1,128)} %bins.1) | copy-start | bytes 3076
  12.0 8.6 %copy-start.6 = (f32[1,1,256]{2,1,0:T(1,128)S(1)}, f32[1,1,256]{2,1,0:T(1,128)}, u32[]{:S(2)}) copy-start(f32[1,1,256]{2,1,0:T(1,128)} %slot_weights.1) | copy-start | bytes 3076
  12.1 10.3 %collective-permute-start.1 = (f32[5,8,128]{2,1,0:T(8,128)S(1)}, f32[5,8,128]{2,1,0:T(8,128)S(1)}, u32[]{:S(2)}, u32[]{:S(2)}) collective-permute-start(f32[5,8,128]{2,1,0:T(8,128)S(1)} %edges.1), channel_id=1, source_target_pairs={{0,28},{8,20},{16,12},{24,4},{28,0},{20,8},{12,16},{4,24},{1,29},{... | collective-permute-start | bytes 61448 | tf_op jit(solution)/shard_map/ppermute | solution.py:369
  17.1 7.4 %collective-permute-start.7 = (f32[320,128]{1,0:T(8,128)S(1)}, f32[320,128]{1,0:T(8,128)S(1)}, u32[]{:S(2)}, u32[]{:S(2)}) collective-permute-start(f32[320,128]{1,0:T(8,128)S(1)} %collective-permute-done.4.refs_1_), channel_id=1, source_target_pairs={{0,8},{8,16},{16,24},{24,28},{28,20},{20,12},{12,4},{4,0},{1,9},{9... | collective-permute-start | bytes 491528 | tf_op jit(solution)/shard_map/ppermute | solution.py:356
  17.1 7.4 %collective-permute-start.8 = (f32[320,128]{1,0:T(8,128)S(1)}, f32[320,128]{1,0:T(8,128)S(1)}, u32[]{:S(2)}, u32[]{:S(2)}) collective-permute-start(f32[320,128]{1,0:T(8,128)S(1)} %collective-permute-done.5.refs_2_), channel_id=1, source_target_pairs={{8,0},{16,8},{24,16},{28,24},{20,28},{12,20},{4,12},{0,4},{9,1},{1... | collective-permute-start | bytes 491528 | tf_op jit(solution)/shard_map/ppermute | solution.py:357
  19.9 0.7 %copy-start.4 = (s32[1,1,256]{2,1,0:T(1,128)S(1)}, s32[1,1,256]{2,1,0:T(1,128)}, u32[]{:S(2)}) copy-start(s32[1,1,256]{2,1,0:T(1,128)} %cells.1) | copy-start | bytes 3076
  22.5 6.5 %collective-permute-start.12 = (f32[320,128]{1,0:T(8,128)S(1)}, f32[320,128]{1,0:T(8,128)S(1)}, u32[]{:S(2)}, u32[]{:S(2)}) collective-permute-start(f32[320,128]{1,0:T(8,128)S(1)} %collective-permute-done.3.refs_7_), channel_id=1, source_target_pairs={{8,0},{16,8},{24,16},{28,24},{20,28},{12,20},{4,12},{0,4},{9,1},{1... | collective-permute-start | bytes 491528 | tf_op jit(solution)/shard_map/ppermute | solution.py:357
  22.5 7.1 %collective-permute-start.9 = (f32[320,128]{1,0:T(8,128)S(1)}, f32[320,128]{1,0:T(8,128)S(1)}, u32[]{:S(2)}, u32[]{:S(2)}) collective-permute-start(f32[320,128]{1,0:T(8,128)S(1)} %collective-permute-done.6.refs_4_), channel_id=1, source_target_pairs={{0,8},{8,16},{16,24},{24,28},{28,20},{20,12},{12,4},{4,0},{1,9},{9... | collective-permute-start | bytes 491528 | tf_op jit(solution)/shard_map/ppermute | solution.py:356
  24.5 7.0 %collective-permute-start.10 = (f32[320,128]{1,0:T(8,128)S(1)}, f32[320,128]{1,0:T(8,128)S(1)}, u32[]{:S(2)}, u32[]{:S(2)}) collective-permute-start(f32[320,128]{1,0:T(8,128)S(1)} %collective-permute-done.7.refs_5_), channel_id=1, source_target_pairs={{0,8},{8,16},{16,24},{24,28},{28,20},{20,12},{12,4},{4,0},{1,9},{9... | collective-permute-start | bytes 491528 | tf_op jit(solution)/shard_map/ppermute | solution.py:356
  24.6 6.9 %collective-permute-start.11 = (f32[320,128]{1,0:T(8,128)S(1)}, f32[320,128]{1,0:T(8,128)S(1)}, u32[]{:S(2)}, u32[]{:S(2)}) collective-permute-start(f32[320,128]{1,0:T(8,128)S(1)} %collective-permute-done.8.refs_6_), channel_id=1, source_target_pairs={{8,0},{16,8},{24,16},{28,24},{20,28},{12,20},{4,12},{0,4},{9,1},{1... | collective-permute-start | bytes 491528 | tf_op jit(solution)/shard_map/ppermute | solution.py:357
  28.9 5.3 %collective-permute-start.14 = (f32[320,128]{1,0:T(8,128)S(1)}, f32[320,128]{1,0:T(8,128)S(1)}, u32[]{:S(2)}, u32[]{:S(2)}) collective-permute-start(f32[320,128]{1,0:T(8,128)S(1)} %collective-permute-done.12.refs_11_), channel_id=1, source_target_pairs={{8,0},{16,8},{24,16},{28,24},{20,28},{12,20},{4,12},{0,4},{9,1},{1... | collective-permute-start | bytes 491528 | tf_op jit(solution)/shard_map/ppermute | solution.py:398
  29.5 5.3 %collective-permute-start.13 = (f32[320,128]{1,0:T(8,128)S(1)}, f32[320,128]{1,0:T(8,128)S(1)}, u32[]{:S(2)}, u32[]{:S(2)}) collective-permute-start(f32[320,128]{1,0:T(8,128)S(1)} %collective-permute-done.9.refs_8_), channel_id=1, source_target_pairs={{0,8},{8,16},{16,24},{24,28},{28,20},{20,12},{12,4},{4,0},{1,9},{9... | collective-permute-start | bytes 491528 | tf_op jit(solution)/shard_map/ppermute | solution.py:397
  32.4 3.7 %collective-permute-start.15 = (f32[5,8,128]{2,1,0:T(8,128)S(1)}, f32[5,8,128]{2,1,0:T(8,128)S(1)}, u32[]{:S(2)}, u32[]{:S(2)}) collective-permute-start(f32[5,8,128]{2,1,0:T(8,128)S(1)} %get-tuple-element.47), channel_id=1, source_target_pairs={{0,1},{1,0},{2,3},{3,2},{4,5},{5,4},{6,7},{7,6},{8,9},{9,8},{10,11... | collective-permute-start | bytes 61448 | tf_op jit(solution)/shard_map/ppermute | solution.py:415
  32.5 3.6 %collective-permute-start.16 = (f32[5,8,128]{2,1,0:T(8,128)S(1)}, f32[5,8,128]{2,1,0:T(8,128)S(1)}, u32[]{:S(2)}, u32[]{:S(2)}) collective-permute-start(f32[5,8,128]{2,1,0:T(8,128)S(1)} %get-tuple-element.47), channel_id=1, source_target_pairs={{0,3},{1,2},{2,1},{3,0},{4,7},{5,6},{6,5},{7,4},{8,11},{9,10},{10,... | collective-permute-start | bytes 61448 | tf_op jit(solution)/shard_map/ppermute | solution.py:415
  37.1 11.0 %all-to-all-start = ((f32[32,1,128]{2,1,0:T(1,128)}), f32[32,1,128]{2,1,0:T(1,128)S(1)}, u32[]{:S(2)}, u32[]{:S(2)}) async-start(f32[32,1,128]{2,1,0:T(1,128)} %bitcast.3), calls=%async_computation | async-start | bytes 32768 | tf_op jit(solution)/shard_map/all_to_all | solution.py:463

commit v6 on v5

--- a/solution.py
+++ b/solution.py
@@ -87,24 +87,51 @@
         edges[field] = packed_edges(tiles)
 
 
-def partial_body(blocks, weights, source, last_edges, *refs):
+def early_body(weights, source, *refs):
     count = weights.shape[1] // 2
-    halves, (smooth, slope, edges) = refs[: 2 * blocks], refs[2 * blocks :]
+    halves, (smooth, slope) = refs[:-2], refs[-2:]
     fields, radial = source.shape[0], source.shape[2]
     half = halves[0].shape[0]
     for field in range(fields):
-        tiles = []
         for row in range(0, radial, TILE):
             at = field * radial + row
             value = source[field, 0, pl.ds(row, TILE), :]
             first, second = weights[0, 0] * value, weights[0, count] * value
-            for k in range(blocks):
+            for k in range(len(halves) // 2):
                 value = halves[2 * k + at // half][pl.ds(at % half, TILE), :]
                 first = first + weights[0, 1 + k] * value
                 second = second + weights[0, count + 1 + k] * value
             smooth[pl.ds(at, TILE), :] = first
             slope[pl.ds(at, TILE), :] = second
-            tiles.append(first)
+
+
+def partial_body(
+    weights,
+    early_smooth,
+    early_slope,
+    left_first,
+    left_second,
+    right_first,
+    right_second,
+    last_edges,
+    smooth,
+    slope,
+    edges,
+):
+    count, fields = weights.shape[1] // 2, edges.shape[0]
+    half, radial = left_first.shape[0], smooth.shape[0] // fields
+    lefts, rights = (left_first, left_second), (right_first, right_second)
+    for field in range(fields):
+        tiles = []
+        for row in range(0, radial, TILE):
+            at = field * radial + row
+            rows, part = pl.ds(at, TILE), pl.ds(at % half, TILE)
+            left, right = lefts[at // half][part, :], rights[at // half][part, :]
+            near, far = weights[0, count - 3], weights[0, count - 2]
+            tiles.append(early_smooth[rows, :] + (near * left + far * right))
+            smooth[rows, :] = tiles[-1]
+            near, far = weights[0, 2 * count - 3], weights[0, 2 * count - 2]
+            slope[rows, :] = early_slope[rows, :] + (near * left + far * right)
         edges[field] = packed_edges(tiles) + weights[0, count - 1] * last_edges[field]
 
 
@@ -261,8 +288,8 @@
 def close_body(
     blocks_x,
     place_x,
+    edges_next,
     edges_pair,
-    edges_next,
     flow_edges,
     values,
     edge_column,
@@ -332,7 +359,8 @@
     fields, local_theta, radial, axial_cells = adjoint.shape
     thetas, blocks_x = lax.axis_size("az"), lax.axis_size("rx")
     devices = thetas * blocks_x
-    assert local_theta == 1 and axial_cells == LANES and thetas % 2 == 0 and blocks_x % 2 == 0
+    assert local_theta == 1 and axial_cells == LANES and blocks_x % 2 == 0
+    assert thetas % 2 == 0 and thetas >= 6
     assert radial % TILE == 0 and radial // TILE * SLOT <= LANES
     params = pltpu.CompilerParams(vmem_limit_bytes=40 * 1024 * 1024)
     f32 = jnp.float32
@@ -393,23 +421,32 @@
             weights, tables, from_right[1] = lax.optimization_barrier(
                 (weights, tables, from_right[1])
             )
+        if step == steps - 1:
+            smooth, slope, from_right[1] = lax.optimization_barrier(
+                (smooth, slope, from_right[1])
+            )
+            continue
         halves += from_left + from_right
+        if step == steps - 2:
+            smooth, slope = pl.pallas_call(
+                early_body,
+                out_shape=(jax.ShapeDtypeStruct((rows, LANES), f32),) * 2,
+                in_specs=in_smem(1) + in_vmem(1 + len(halves)),
+                out_specs=tuple(in_vmem(2)),
+                compiler_params=params,
+                name="early",
+            )(weights, adjoint, *halves)
     last_first = lax.ppermute(from_left[0], "az", onward)
     last_second = lax.ppermute(from_right[1], "az", back)
 
-    blocks = len(halves) // 2
     smooth, slope, edges = pl.pallas_call(
-        functools.partial(partial_body, blocks),
-        out_shape=(
-            jax.ShapeDtypeStruct((rows, LANES), f32),
-            jax.ShapeDtypeStruct((rows, LANES), f32),
-            edge_shape,
-        ),
-        in_specs=in_smem(1) + in_vmem(2 + 2 * blocks),
+        partial_body,
+        out_shape=(jax.ShapeDtypeStruct((rows, LANES), f32),) * 2 + (edge_shape,),
+        in_specs=in_smem(1) + in_vmem(7),
         out_specs=tuple(in_vmem(3)),
         compiler_params=params,
         name="partial",
-    )(weights, adjoint, last_edges, *halves)
+    )(weights, smooth, slope, *from_left, *from_right, last_edges)
     pairs = [(b, b ^ 1) for b in range(blocks_x)]
     nexts = [(b, (b + (1 if b % 2 else -1)) % blocks_x) for b in range(blocks_x)]
     edges_next, edges_pair = lax.ppermute(edges, "rx", nexts), lax.ppermute(edges, "rx", pairs)
@@ -451,8 +488,8 @@
         name="close",
     )(
         place_x,
+        edges_next,
         edges_pair,
-        edges_next,
         flow_edges,
         values,
         edge_column,

time: 48.8 us -> 48.5 us (level)
  Pallas kernels: 4.32 us -> 4.88 us
  waiting for transfers between devices: 14 us -> 13.5 us
    ppermute x1, starting transfers between devices: 1.64 us -> 0.07 us  [local(): lax.ppermute(edges, 'rx', nexts)]
    ppermute x1, starting transfers between devices: 0.06 us -> 1.62 us  [local(): lax.ppermute(edges, 'rx', pairs)]
    ppermute x6, waiting for transfers between devices: 5.04 us -> 4.28 us  [local(): right.append(lax.ppermute(from_right[part], 'az', back))]
    pallas_call x1 -> x2, Pallas kernels: 0.93 us -> 1.48 us  [the longest x1 0.76 us: local(): pl.pallas_call(early_body, out_shape=(jax.ShapeDtypeStruct((rows, LANES),...]
  transfers between devices with their start and end apart: 18 -> 18, of which waited for: 7 -> 7; matrix products, arithmetic and copies ran while one was open for 1% -> 1% of each run, Pallas kernels for 7% -> 8%
where the time goes in v6:
time: 48.5 us; the launch traced here: 48.3 us
  starting transfers between devices  26.2 us (54%)
  waiting for transfers between devices  13.5 us (28%)
  Pallas kernels  4.88 us (10%)
  local copies, waits for them, and re-layouts  1.79 us (4%)
  between operations  1.44 us (3%)
  other arithmetic  0.56 us (1%)
    ppermute x6, starting transfers between devices, local(): right.append(lax.ppermute(from_right[part], 'az', back))  9.34 us
    all_to_all x1, waiting for transfers between devices, local(): totals = lax.all_to_all(totals, ('az', 'rx'), 0, 0, tiled=True)  6.27 us
    ppermute x1, starting transfers between devices, local(): last_edges = lax.ppermute(last_edges, 'az', across)  5.02 us
    ppermute x6, starting transfers between devices, local(): left.append(lax.ppermute(from_left[part], 'az', onward))  4.3 us
    ppermute x6, waiting for transfers between devices, local(): right.append(lax.ppermute(from_right[part], 'az', back))  4.28 us
    all_to_all x1, starting transfers between devices, local(): totals = lax.all_to_all(totals, ('az', 'rx'), 0, 0, tiled=True)  3.48 us
    ppermute x1, starting transfers between devices, local(): last_first = lax.ppermute(from_left[0], 'az', onward)  1.71 us
    ppermute x1, waiting for transfers between devices, local(): last_edges = lax.ppermute(last_edges, 'az', across)  1.69 us
  transfers between devices with their start and end apart: 18, of which 7 were waited for; matrix products, arithmetic and copies ran while one was open for 1% of the time, Pallas kernels for 8%

profile of v6, /device:TPU:0, one launch (start us, length us, event | category | flops | bytes accessed | tf_op | source)
XLA Modules:
  0.0 48.3 jit_solution(18027591115573033304)
XLA Ops:
  0.6 1.1 %fusion = (f32[320,128]{1,0:T(8,128)S(1)}, f32[320,128]{1,0:T(8,128)S(1)}) fusion(f32[640,128]{1,0:T(8,128)} %bitcast.6), kind=kLoop, calls=%fused_computation.1 | loop fusion | bytes 655360 | tf_op jit(solution)/shard_map/slice | solution.py:377
  1.7 3.0 %collective-permute-start.2 = (f32[320,128]{1,0:T(8,128)S(1)}, f32[320,128]{1,0:T(8,128)S(1)}, u32[]{:S(2)}, u32[]{:S(2)}) collective-permute-start(f32[320,128]{1,0:T(8,128)S(1)} %get-tuple-element.66), channel_id=1, source_target_pairs={{8,0},{16,8},{24,16},{28,24},{20,28},{12,20},{4,12},{0,4},{9,1},{1... | collective-permute-start | bytes 491528 | tf_op jit(solution)/shard_map/ppermute | solution.py:385
  4.7 0.2 collective-permute-start
  4.9 2.0 %collective-permute-start.4 = (f32[320,128]{1,0:T(8,128)S(1)}, f32[320,128]{1,0:T(8,128)S(1)}, u32[]{:S(2)}, u32[]{:S(2)}) collective-permute-start(f32[320,128]{1,0:T(8,128)S(1)} %get-tuple-element.66), channel_id=1, source_target_pairs={{0,8},{8,16},{16,24},{24,28},{28,20},{20,12},{12,4},{4,0},{1,9},{9... | collective-permute-start | bytes 491528 | tf_op jit(solution)/shard_map/ppermute | solution.py:384
  6.8 0.1 collective-permute-start.5
  6.9 2.6 %collective-permute-done.2.refs_3_ = f32[320,128]{1,0:T(8,128)S(1)} collective-permute-done((f32[320,128]{1,0:T(8,128)S(1)}, f32[320,128]{1,0:T(8,128)S(1)}, u32[]{:S(2)}, u32[]{:S(2)}) %collective-permute-start.2) | collective-permute-done | bytes 163872 | tf_op jit(solution)/shard_map/ppermute | solution.py:385
  9.5 2.3 %collective-permute-start.3 = (f32[320,128]{1,0:T(8,128)S(1)}, f32[320,128]{1,0:T(8,128)S(1)}, u32[]{:S(2)}, u32[]{:S(2)}) collective-permute-start(f32[320,128]{1,0:T(8,128)S(1)} %collective-permute-done.2.refs_3_), channel_id=1, source_target_pairs={{8,0},{16,8},{24,16},{28,24},{20,28},{12,20},{4,12},{0,4},{9,1},{1... | collective-permute-start | bytes 491528 | tf_op jit(solution)/shard_map/ppermute | solution.py:385
  11.8 0.1 collective-permute-start.6
  12.0 0.1 edges.1
  12.1 5.0 %collective-permute-start.1 = (f32[5,8,128]{2,1,0:T(8,128)S(1)}, f32[5,8,128]{2,1,0:T(8,128)S(1)}, u32[]{:S(2)}, u32[]{:S(2)}) collective-permute-start(f32[5,8,128]{2,1,0:T(8,128)S(1)} %edges.1), channel_id=1, source_target_pairs={{0,28},{8,20},{16,12},{24,4},{28,0},{20,8},{12,16},{4,24},{1,29},{... | collective-permute-start | bytes 61448 | tf_op jit(solution)/shard_map/ppermute | solution.py:397
  17.1 2.0 %collective-permute-start.8 = (f32[320,128]{1,0:T(8,128)S(1)}, f32[320,128]{1,0:T(8,128)S(1)}, u32[]{:S(2)}, u32[]{:S(2)}) collective-permute-start(f32[320,128]{1,0:T(8,128)S(1)} %collective-permute-done.5.refs_2_), channel_id=1, source_target_pairs={{8,0},{16,8},{24,16},{28,24},{20,28},{12,20},{4,12},{0,4},{9,1},{1... | collective-permute-start | bytes 491528 | tf_op jit(solution)/shard_map/ppermute | solution.py:385
  19.2 0.7 %constant_dynamic-slice_fusion.weights = f32[1,16]{1,0:T(1,128)S(1)} fusion(f32[8,16]{1,0:T(8,128)} %constant.17.clone, s32[]{:T(128)S(6)} %select_n.3), kind=kLoop, calls=%fused_computation | loop fusion | bytes 132 | tf_op jit(solution)/shard_map/dynamic_slice | solution.py:401
  20.6 0.2 slots.1
  20.8 1.7 %collective-permute-done.1.last_edges = f32[5,8,128]{2,1,0:T(8,128)S(1)} collective-permute-done((f32[5,8,128]{2,1,0:T(8,128)S(1)}, f32[5,8,128]{2,1,0:T(8,128)S(1)}, u32[]{:S(2)}, u32[]{:S(2)}) %collective-permute-start.1) | collective-permute-done | bytes 20512 | tf_op jit(solution)/shard_map/ppermute | solution.py:397
  22.5 2.0 %collective-permute-start.10 = (f32[320,128]{1,0:T(8,128)S(1)}, f32[320,128]{1,0:T(8,128)S(1)}, u32[]{:S(2)}, u32[]{:S(2)}) collective-permute-start(f32[320,128]{1,0:T(8,128)S(1)} %collective-permute-done.6.refs_4_), channel_id=1, source_target_pairs={{0,8},{8,16},{16,24},{24,28},{28,20},{20,12},{12,4},{4,0},{1,9},{9... | collective-permute-start | bytes 491528 | tf_op jit(solution)/shard_map/ppermute | solution.py:384
  24.6 2.0 %collective-permute-start.12 = (f32[320,128]{1,0:T(8,128)S(1)}, f32[320,128]{1,0:T(8,128)S(1)}, u32[]{:S(2)}, u32[]{:S(2)}) collective-permute-start(f32[320,128]{1,0:T(8,128)S(1)} %collective-permute-done.8.refs_6_), channel_id=1, source_target_pairs={{8,0},{16,8},{24,16},{28,24},{20,28},{12,20},{4,12},{0,4},{9,1},{1... | collective-permute-start | bytes 491528 | tf_op jit(solution)/shard_map/ppermute | solution.py:385
  26.5 0.8 %early.1 = (f32[640,128]{1,0:T(8,128)S(1)}, f32[640,128]{1,0:T(8,128)S(1)}) custom-call(f32[1,16]{1,0:T(1,128)S(1)} %constant_dynamic-slice_fusion.weights, f32[5,1,128,128]{3,2,1,0:T(8,128)S(1)} %copy-done, f32[320,128]{1,0:T(8,128)S(1)} %collective-permute-done.refs_0_, f32[320,128]{1,0:T(8,128)S(1)} %collective-permute-done.4.refs_1_, ...), custom_call_target="tpu_custom_call" | custom-call | tf_op jit(solution)/shard_map/early/pallas_call | solution.py:431
  27.3 1.6 %collective-permute-done.9.right_second = f32[320,128]{1,0:T(8,128)S(1)} collective-permute-done((f32[320,128]{1,0:T(8,128)S(1)}, f32[320,128]{1,0:T(8,128)S(1)}, u32[]{:S(2)}, u32[]{:S(2)}) %collective-permute-start.9) | collective-permute-done | bytes 163872 | tf_op jit(solution)/shard_map/ppermute | solution.py:385
  28.9 0.6 %collective-permute-start.14 = (f32[320,128]{1,0:T(8,128)S(1)}, f32[320,128]{1,0:T(8,128)S(1)}, u32[]{:S(2)}, u32[]{:S(2)}) collective-permute-start(f32[320,128]{1,0:T(8,128)S(1)} %collective-permute-done.9.right_second), channel_id=1, source_target_pairs={{8,0},{16,8},{24,16},{28,24},{20,28},{12,20},{4,12},{0,4},{9,1},{1... | collective-permute-start | bytes 491528 | tf_op jit(solution)/shard_map/ppermute | solution.py:440
  29.5 1.7 %collective-permute-start.13 = (f32[320,128]{1,0:T(8,128)S(1)}, f32[320,128]{1,0:T(8,128)S(1)}, u32[]{:S(2)}, u32[]{:S(2)}) collective-permute-start(f32[320,128]{1,0:T(8,128)S(1)} %collective-permute-done.10.left_first), channel_id=1, source_target_pairs={{0,8},{8,16},{16,24},{24,28},{28,20},{20,12},{12,4},{4,0},{1,9},{9... | collective-permute-start | bytes 491528 | tf_op jit(solution)/shard_map/ppermute | solution.py:439
  31.3 0.2 collective-permute-done.11.left_second
  31.5 0.7 %partial.1 = (f32[640,128]{1,0:T(8,128)S(1)}, f32[640,128]{1,0:T(8,128)S(1)}, f32[5,8,128]{2,1,0:T(8,128)S(1)}) custom-call(f32[1,16]{1,0:T(1,128)S(1)} %constant_dynamic-slice_fusion.weights, f32[640,128]{1,0:T(8,128)S(1)} %get-tuple-element.48.early_smooth, f32[640,128]{1,0:T(8,128)S(1)} %get-tuple-element.49.early_slope, ...), custom_call_target="tpu_custom_call" | custom-call | tf_op jit(solution)/shard_map/partial/pallas_call | solution.py:442
  32.2 0.1 collective-permute-start.15
  32.3 1.6 %collective-permute-start.16 = (f32[5,8,128]{2,1,0:T(8,128)S(1)}, f32[5,8,128]{2,1,0:T(8,128)S(1)}, u32[]{:S(2)}, u32[]{:S(2)}) collective-permute-start(f32[5,8,128]{2,1,0:T(8,128)S(1)} %get-tuple-element.57), channel_id=1, source_target_pairs={{0,1},{1,0},{2,3},{3,2},{4,5},{5,4},{6,7},{7,6},{8,9},{9,8},{10,11... | collective-permute-start | bytes 61448 | tf_op jit(solution)/shard_map/ppermute | solution.py:452
  33.9 0.4 collective-permute-done.14.last_second
  34.2 0.6 %collective-permute-done.13.last_first = f32[320,128]{1,0:T(8,128)S(1)} collective-permute-done((f32[320,128]{1,0:T(8,128)S(1)}, f32[320,128]{1,0:T(8,128)S(1)}, u32[]{:S(2)}, u32[]{:S(2)}) %collective-permute-start.13) | collective-permute-done | bytes 163872 | tf_op jit(solution)/shard_map/ppermute | solution.py:439
  34.9 1.2 %bulk.1 = (f32[5,1,128,128]{3,2,1,0:T(8,128)S(1)}, f32[1,256]{1,0:T(1,128)S(1)}) custom-call(f32[1,16]{1,0:T(1,128)S(1)} %constant_dynamic-slice_fusion.weights, f32[640,128]{1,0:T(8,128)S(1)} %get-tuple-element.52.smooth, f32[640,128]{1,0:T(8,128)S(1)} %get-tuple-element.53.slope, f32[320,128]{1,0:T(8,128)S(1)} %collective-permute-done.13.last_first, ...), custom_call_target="tpu_custom_call" | custom-call | tf_op jit(solution)/shard_map/bulk/pallas_call | solution.py:456
  36.1 1.0 %close.1 = (f32[5,8,128]{2,1,0:T(8,128)S(1)}, f32[32,128]{1,0:T(8,128)}) custom-call(s32[1,1]{1,0:T(1,128)} %bitcast.1.place_x, f32[5,8,128]{2,1,0:T(8,128)S(1)} %collective-permute-done.15.edges_next, f32[5,8,128]{2,1,0:T(8,128)S(1)} %collective-permute-done.16.edges_pair, f32[4,8,128]{2,1,0:T(8,128)S(1)} %get-tuple-element.58.flow_edges, ...), custom_call_target="tpu_custom_call" | custom-call | tf_op jit(solution)/shard_map/close/pallas_call | solution.py:482
  37.1 3.5 %all-to-all-start = ((f32[32,1,128]{2,1,0:T(1,128)}), f32[32,1,128]{2,1,0:T(1,128)S(1)}, u32[]{:S(2)}, u32[]{:S(2)}) async-start(f32[32,1,128]{2,1,0:T(1,128)} %bitcast.3), calls=%async_computation | async-start | bytes 32768 | tf_op jit(solution)/shard_map/all_to_all | solution.py:500
  40.6 0.9 %store.1 = f32[5,1,128,128]{3,2,1,0:T(8,128)} custom-call(f32[5,1,128,128]{3,2,1,0:T(8,128)S(1)} %get-tuple-element.56.held, f32[5,8,128]{2,1,0:T(8,128)S(1)} %get-tuple-element.64.fixes), custom_call_target="tpu_custom_call" | custom-call | tf_op jit(solution)/shard_map/store/pallas_call | solution.py:501
  41.5 6.3 %all-to-all-done = f32[32,1,128]{2,1,0:T(1,128)S(1)} async-done(((f32[32,1,128]{2,1,0:T(1,128)}), f32[32,1,128]{2,1,0:T(1,128)S(1)}, u32[]{:S(2)}, u32[]{:S(2)}) %all-to-all-start) | async-done | bytes 16416 | tf_op jit(solution)/shard_map/all_to_all | solution.py:500
  47.7 0.6 %reduce_sum.9 = f32[128]{0:T(128)} reduce(f32[32,1,128]{2,1,0:T(1,128)S(1)} %all-to-all-done, f32[]{:T(128)} %constant.16.clone.1), dimensions={0,1}, to_apply=%region_0.0 | reduce | flops 3968 | bytes 16900 | tf_op jit(solution)/shard_map/reduce_sum | solution.py:509
  (28 shorter events, 0.2 us)
Async XLA Ops:
  0.6 11.3 %copy-start = (f32[5,1,128,128]{3,2,1,0:T(8,128)S(1)}, f32[5,1,128,128]{3,2,1,0:T(8,128)}, u32[]{:S(2)}) copy-start(f32[5,1,128,128]{3,2,1,0:T(8,128)} %source.2) | copy-start | bytes 983044
  1.7 18.8 %copy-start.1 = (f32[3,1,128,128]{3,2,1,0:T(8,128)S(1)}, f32[3,1,128,128]{3,2,1,0:T(8,128)}, u32[]{:S(2)}) copy-start(f32[3,1,128,128]{3,2,1,0:T(8,128)} %velocity.3) | copy-start | bytes 589828
  1.7 7.8 %collective-permute-start.2 = (f32[320,128]{1,0:T(8,128)S(1)}, f32[320,128]{1,0:T(8,128)S(1)}, u32[]{:S(2)}, u32[]{:S(2)}) collective-permute-start(f32[320,128]{1,0:T(8,128)S(1)} %get-tuple-element.66), channel_id=1, source_target_pairs={{8,0},{16,8},{24,16},{28,24},{20,28},{12,20},{4,12},{0,4},{9,1},{1... | collective-permute-start | bytes 491528 | tf_op jit(solution)/shard_map/ppermute | solution.py:385
  4.7 7.1 %collective-permute-start = (f32[320,128]{1,0:T(8,128)S(1)}, f32[320,128]{1,0:T(8,128)S(1)}, u32[]{:S(2)}, u32[]{:S(2)}) collective-permute-start(f32[320,128]{1,0:T(8,128)S(1)} %get-tuple-element.67), channel_id=1, source_target_pairs={{0,8},{8,16},{16,24},{24,28},{28,20},{20,12},{12,4},{4,0},{1,9},{9... | collective-permute-start | bytes 491528 | tf_op jit(solution)/shard_map/ppermute | solution.py:384
  4.9 12.3 %collective-permute-start.4 = (f32[320,128]{1,0:T(8,128)S(1)}, f32[320,128]{1,0:T(8,128)S(1)}, u32[]{:S(2)}, u32[]{:S(2)}) collective-permute-start(f32[320,128]{1,0:T(8,128)S(1)} %get-tuple-element.66), channel_id=1, source_target_pairs={{0,8},{8,16},{16,24},{24,28},{28,20},{20,12},{12,4},{4,0},{1,9},{9... | collective-permute-start | bytes 491528 | tf_op jit(solution)/shard_map/ppermute | solution.py:384
  6.8 10.3 %collective-permute-start.5 = (f32[320,128]{1,0:T(8,128)S(1)}, f32[320,128]{1,0:T(8,128)S(1)}, u32[]{:S(2)}, u32[]{:S(2)}) collective-permute-start(f32[320,128]{1,0:T(8,128)S(1)} %get-tuple-element.67), channel_id=1, source_target_pairs={{8,0},{16,8},{24,16},{28,24},{20,28},{12,20},{4,12},{0,4},{9,1},{1... | collective-permute-start | bytes 491528 | tf_op jit(solution)/shard_map/ppermute | solution.py:385
  9.5 12.9 %collective-permute-start.3 = (f32[320,128]{1,0:T(8,128)S(1)}, f32[320,128]{1,0:T(8,128)S(1)}, u32[]{:S(2)}, u32[]{:S(2)}) collective-permute-start(f32[320,128]{1,0:T(8,128)S(1)} %collective-permute-done.2.refs_3_), channel_id=1, source_target_pairs={{8,0},{16,8},{24,16},{28,24},{20,28},{12,20},{4,12},{0,4},{9,1},{1... | collective-permute-start | bytes 491528 | tf_op jit(solution)/shard_map/ppermute | solution.py:385
  11.8 10.6 %collective-permute-start.6 = (f32[320,128]{1,0:T(8,128)S(1)}, f32[320,128]{1,0:T(8,128)S(1)}, u32[]{:S(2)}, u32[]{:S(2)}) collective-permute-start(f32[320,128]{1,0:T(8,128)S(1)} %collective-permute-done.refs_0_), channel_id=1, source_target_pairs={{0,8},{8,16},{16,24},{24,28},{28,20},{20,12},{12,4},{4,0},{1,9},{9... | collective-permute-start | bytes 491528 | tf_op jit(solution)/shard_map/ppermute | solution.py:384
  11.9 8.6 %copy-start.2 = (f32[1,128,128]{2,1,0:T(8,128)S(1)}, f32[1,128,128]{2,1,0:T(8,128)}, u32[]{:S(2)}) copy-start(f32[1,128,128]{2,1,0:T(8,128)} %density.3) | copy-start | bytes 196612
  12.0 8.6 %copy-start.3 = (f32[1,128,128]{2,1,0:T(8,128)S(1)}, f32[1,128,128]{2,1,0:T(8,128)}, u32[]{:S(2)}) copy-start(f32[1,128,128]{2,1,0:T(8,128)} %pressure.3) | copy-start | bytes 196612
  12.0 8.6 %copy-start.5 = (s32[1,1,256]{2,1,0:T(1,128)S(1)}, s32[1,1,256]{2,1,0:T(1,128)}, u32[]{:S(2)}) copy-start(s32[1,1,256]{2,1,0:T(1,128)} %bins.1) | copy-start | bytes 3076
  12.0 8.6 %copy-start.6 = (f32[1,1,256]{2,1,0:T(1,128)S(1)}, f32[1,1,256]{2,1,0:T(1,128)}, u32[]{:S(2)}) copy-start(f32[1,1,256]{2,1,0:T(1,128)} %slot_weights.1) | copy-start | bytes 3076
  12.1 10.3 %collective-permute-start.1 = (f32[5,8,128]{2,1,0:T(8,128)S(1)}, f32[5,8,128]{2,1,0:T(8,128)S(1)}, u32[]{:S(2)}, u32[]{:S(2)}) collective-permute-start(f32[5,8,128]{2,1,0:T(8,128)S(1)} %edges.1), channel_id=1, source_target_pairs={{0,28},{8,20},{16,12},{24,4},{28,0},{20,8},{12,16},{4,24},{1,29},{... | collective-permute-start | bytes 61448 | tf_op jit(solution)/shard_map/ppermute | solution.py:397
  17.1 7.4 %collective-permute-start.7 = (f32[320,128]{1,0:T(8,128)S(1)}, f32[320,128]{1,0:T(8,128)S(1)}, u32[]{:S(2)}, u32[]{:S(2)}) collective-permute-start(f32[320,128]{1,0:T(8,128)S(1)} %collective-permute-done.4.refs_1_), channel_id=1, source_target_pairs={{0,8},{8,16},{16,24},{24,28},{28,20},{20,12},{12,4},{4,0},{1,9},{9... | collective-permute-start | bytes 491528 | tf_op jit(solution)/shard_map/ppermute | solution.py:384
  17.1 7.4 %collective-permute-start.8 = (f32[320,128]{1,0:T(8,128)S(1)}, f32[320,128]{1,0:T(8,128)S(1)}, u32[]{:S(2)}, u32[]{:S(2)}) collective-permute-start(f32[320,128]{1,0:T(8,128)S(1)} %collective-permute-done.5.refs_2_), channel_id=1, source_target_pairs={{8,0},{16,8},{24,16},{28,24},{20,28},{12,20},{4,12},{0,4},{9,1},{1... | collective-permute-start | bytes 491528 | tf_op jit(solution)/shard_map/ppermute | solution.py:385
  19.9 0.7 %copy-start.4 = (s32[1,1,256]{2,1,0:T(1,128)S(1)}, s32[1,1,256]{2,1,0:T(1,128)}, u32[]{:S(2)}) copy-start(s32[1,1,256]{2,1,0:T(1,128)} %cells.1) | copy-start | bytes 3076
  22.5 6.5 %collective-permute-start.9 = (f32[320,128]{1,0:T(8,128)S(1)}, f32[320,128]{1,0:T(8,128)S(1)}, u32[]{:S(2)}, u32[]{:S(2)}) collective-permute-start(f32[320,128]{1,0:T(8,128)S(1)} %collective-permute-done.3.refs_7_), channel_id=1, source_target_pairs={{8,0},{16,8},{24,16},{28,24},{20,28},{12,20},{4,12},{0,4},{9,1},{1... | collective-permute-start | bytes 491528 | tf_op jit(solution)/shard_map/ppermute | solution.py:385
  22.5 7.1 %collective-permute-start.10 = (f32[320,128]{1,0:T(8,128)S(1)}, f32[320,128]{1,0:T(8,128)S(1)}, u32[]{:S(2)}, u32[]{:S(2)}) collective-permute-start(f32[320,128]{1,0:T(8,128)S(1)} %collective-permute-done.6.refs_4_), channel_id=1, source_target_pairs={{0,8},{8,16},{16,24},{24,28},{28,20},{20,12},{12,4},{4,0},{1,9},{9... | collective-permute-start | bytes 491528 | tf_op jit(solution)/shard_map/ppermute | solution.py:384
  24.5 7.0 %collective-permute-start.11 = (f32[320,128]{1,0:T(8,128)S(1)}, f32[320,128]{1,0:T(8,128)S(1)}, u32[]{:S(2)}, u32[]{:S(2)}) collective-permute-start(f32[320,128]{1,0:T(8,128)S(1)} %collective-permute-done.7.refs_5_), channel_id=1, source_target_pairs={{0,8},{8,16},{16,24},{24,28},{28,20},{20,12},{12,4},{4,0},{1,9},{9... | collective-permute-start | bytes 491528 | tf_op jit(solution)/shard_map/ppermute | solution.py:384
  24.6 6.9 %collective-permute-start.12 = (f32[320,128]{1,0:T(8,128)S(1)}, f32[320,128]{1,0:T(8,128)S(1)}, u32[]{:S(2)}, u32[]{:S(2)}) collective-permute-start(f32[320,128]{1,0:T(8,128)S(1)} %collective-permute-done.8.refs_6_), channel_id=1, source_target_pairs={{8,0},{16,8},{24,16},{28,24},{20,28},{12,20},{4,12},{0,4},{9,1},{1... | collective-permute-start | bytes 491528 | tf_op jit(solution)/shard_map/ppermute | solution.py:385
  28.9 5.3 %collective-permute-start.14 = (f32[320,128]{1,0:T(8,128)S(1)}, f32[320,128]{1,0:T(8,128)S(1)}, u32[]{:S(2)}, u32[]{:S(2)}) collective-permute-start(f32[320,128]{1,0:T(8,128)S(1)} %collective-permute-done.9.right_second), channel_id=1, source_target_pairs={{8,0},{16,8},{24,16},{28,24},{20,28},{12,20},{4,12},{0,4},{9,1},{1... | collective-permute-start | bytes 491528 | tf_op jit(solution)/shard_map/ppermute | solution.py:440
  29.5 5.3 %collective-permute-start.13 = (f32[320,128]{1,0:T(8,128)S(1)}, f32[320,128]{1,0:T(8,128)S(1)}, u32[]{:S(2)}, u32[]{:S(2)}) collective-permute-start(f32[320,128]{1,0:T(8,128)S(1)} %collective-permute-done.10.left_first), channel_id=1, source_target_pairs={{0,8},{8,16},{16,24},{24,28},{28,20},{20,12},{12,4},{4,0},{1,9},{9... | collective-permute-start | bytes 491528 | tf_op jit(solution)/shard_map/ppermute | solution.py:439
  32.2 3.9 %collective-permute-start.15 = (f32[5,8,128]{2,1,0:T(8,128)S(1)}, f32[5,8,128]{2,1,0:T(8,128)S(1)}, u32[]{:S(2)}, u32[]{:S(2)}) collective-permute-start(f32[5,8,128]{2,1,0:T(8,128)S(1)} %get-tuple-element.57), channel_id=1, source_target_pairs={{0,3},{1,2},{2,1},{3,0},{4,7},{5,6},{6,5},{7,4},{8,11},{9,10},{10,... | collective-permute-start | bytes 61448 | tf_op jit(solution)/shard_map/ppermute | solution.py:452
  32.3 3.8 %collective-permute-start.16 = (f32[5,8,128]{2,1,0:T(8,128)S(1)}, f32[5,8,128]{2,1,0:T(8,128)S(1)}, u32[]{:S(2)}, u32[]{:S(2)}) collective-permute-start(f32[5,8,128]{2,1,0:T(8,128)S(1)} %get-tuple-element.57), channel_id=1, source_target_pairs={{0,1},{1,0},{2,3},{3,2},{4,5},{5,4},{6,7},{7,6},{8,9},{9,8},{10,11... | collective-permute-start | bytes 61448 | tf_op jit(solution)/shard_map/ppermute | solution.py:452
  37.1 10.6 %all-to-all-start = ((f32[32,1,128]{2,1,0:T(1,128)}), f32[32,1,128]{2,1,0:T(1,128)S(1)}, u32[]{:S(2)}, u32[]{:S(2)}) async-start(f32[32,1,128]{2,1,0:T(1,128)} %bitcast.3), calls=%async_computation | async-start | bytes 32768 | tf_op jit(solution)/shard_map/all_to_all | solution.py:500

commit v7 on v6

--- a/solution.py
+++ b/solution.py
@@ -336,7 +336,9 @@
     )
 
 
-def store_body(held, fixes, section):
+def store_body(held, fixes, totals, section, signal):
+    sums = jnp.sum(totals[...], axis=0, keepdims=True)
+    signal[...] = sums[0, : signal.shape[0]]
     fields, radial = section.shape[0], section.shape[2]
     lane = lax.broadcasted_iota(jnp.int32, (TILE, LANES), 1)
     outer = (lane < EDGE) | (lane >= LANES - EDGE)
@@ -498,15 +500,18 @@
         place,
     )
     totals = lax.all_to_all(totals, ("az", "rx"), 0, 0, tiled=True)
-    section = pl.pallas_call(
+    section, signal = pl.pallas_call(
         store_body,
-        out_shape=jax.ShapeDtypeStruct(adjoint.shape, f32),
-        in_specs=in_vmem(2),
-        out_specs=in_vmem(1)[0],
+        out_shape=(
+            jax.ShapeDtypeStruct(adjoint.shape, f32),
+            jax.ShapeDtypeStruct((BIN_DEV,), f32),
+        ),
+        in_specs=in_vmem(3),
+        out_specs=tuple(in_vmem(2)),
         compiler_params=params,
         name="store",
-    )(held, fixes)
-    return section, jnp.sum(totals, axis=0)[:BIN_DEV]
+    )(held, fixes, totals)
+    return section, signal
 
 
 def solution(mesh):

time: 48.5 us -> 48 us (0.990)
  blocking collectives: 0 us -> 10.5 us
  waiting for transfers between devices: 13.5 us -> 7.19 us
  starting transfers between devices: 26.2 us -> 22.7 us
  Pallas kernels: 4.88 us -> 4.26 us
  other arithmetic: 0.56 us -> 0 us
    all_to_all x0 -> x1, blocking collectives: none -> 10.5 us  [local(): totals = lax.all_to_all(totals, ('az', 'rx'), 0, 0, tiled=True)]
    all_to_all x1 -> x0, waiting for transfers between devices: 6.27 us -> none  [local(): totals = lax.all_to_all(totals, ('az', 'rx'), 0, 0, tiled=True)]
    all_to_all x1 -> x0, starting transfers between devices: 3.48 us -> none  [local(): totals = lax.all_to_all(totals, ('az', 'rx'), 0, 0, tiled=True)]
    pallas_call x1, Pallas kernels: 0.98 us -> 0.36 us  [local(): pl.pallas_call(functools.partial(close_body, blocks_x), out_shape=(edge_s...]
    reduce_sum x1 -> x0, other arithmetic: 0.56 us -> none  [local(): return (section, jnp.sum(totals, axis=0)[:BIN_DEV])]
  transfers between devices with their start and end apart: 18 -> 17, of which waited for: 7 -> 6; matrix products, arithmetic and copies ran while one was open for 1% -> 1% of each run, Pallas kernels for 8% -> 6%
where the time goes in v7:
time: 48 us; the launch traced here: 47.8 us
  starting transfers between devices  22.7 us (47%)
  blocking collectives  10.5 us (22%)
  waiting for transfers between devices  7.19 us (15%)
  Pallas kernels  4.26 us (9%)
  local copies, waits for them, and re-layouts  1.79 us (4%)
  between operations  1.43 us (3%)
    all_to_all x1, blocking collectives, local(): totals = lax.all_to_all(totals, ('az', 'rx'), 0, 0, tiled=True)  10.5 us
    ppermute x6, starting transfers between devices, local(): right.append(lax.ppermute(from_right[part], 'az', back))  9.34 us
    ppermute x1, starting transfers between devices, local(): last_edges = lax.ppermute(last_edges, 'az', across)  5.02 us
    ppermute x6, starting transfers between devices, local(): left.append(lax.ppermute(from_left[part], 'az', onward))  4.3 us
    ppermute x6, waiting for transfers between devices, local(): right.append(lax.ppermute(from_right[part], 'az', back))  4.28 us
    ppermute x1, starting transfers between devices, local(): last_first = lax.ppermute(from_left[0], 'az', onward)  1.71 us
    ppermute x1, waiting for transfers between devices, local(): last_edges = lax.ppermute(last_edges, 'az', across)  1.69 us
    ppermute x1, starting transfers between devices, local(): lax.ppermute(edges, 'rx', pairs)  1.62 us
  transfers between devices with their start and end apart: 17, of which 6 were waited for; matrix products, arithmetic and copies ran while one was open for 1% of the time, Pallas kernels for 6%

profile of v7, /device:TPU:0, one launch (start us, length us, event | category | flops | bytes accessed | tf_op | source)
XLA Modules:
  0.0 47.8 jit_solution(13106834916465157946)
XLA Ops:
  0.6 1.1 %fusion = (f32[320,128]{1,0:T(8,128)S(1)}, f32[320,128]{1,0:T(8,128)S(1)}) fusion(f32[640,128]{1,0:T(8,128)} %bitcast.6), kind=kLoop, calls=%fused_computation.1 | loop fusion | bytes 655360 | tf_op jit(solution)/shard_map/slice | solution.py:379
  1.7 3.0 %collective-permute-start.2 = (f32[320,128]{1,0:T(8,128)S(1)}, f32[320,128]{1,0:T(8,128)S(1)}, u32[]{:S(2)}, u32[]{:S(2)}) collective-permute-start(f32[320,128]{1,0:T(8,128)S(1)} %get-tuple-element.66), channel_id=1, source_target_pairs={{8,0},{16,8},{24,16},{28,24},{20,28},{12,20},{4,12},{0,4},{9,1},{1... | collective-permute-start | bytes 491528 | tf_op jit(solution)/shard_map/ppermute | solution.py:387
  4.7 0.2 collective-permute-start
  4.9 2.0 %collective-permute-start.4 = (f32[320,128]{1,0:T(8,128)S(1)}, f32[320,128]{1,0:T(8,128)S(1)}, u32[]{:S(2)}, u32[]{:S(2)}) collective-permute-start(f32[320,128]{1,0:T(8,128)S(1)} %get-tuple-element.66), channel_id=1, source_target_pairs={{0,8},{8,16},{16,24},{24,28},{28,20},{20,12},{12,4},{4,0},{1,9},{9... | collective-permute-start | bytes 491528 | tf_op jit(solution)/shard_map/ppermute | solution.py:386
  6.8 0.1 collective-permute-start.5
  6.9 2.6 %collective-permute-done.2.refs_3_ = f32[320,128]{1,0:T(8,128)S(1)} collective-permute-done((f32[320,128]{1,0:T(8,128)S(1)}, f32[320,128]{1,0:T(8,128)S(1)}, u32[]{:S(2)}, u32[]{:S(2)}) %collective-permute-start.2) | collective-permute-done | bytes 163872 | tf_op jit(solution)/shard_map/ppermute | solution.py:387
  9.5 2.3 %collective-permute-start.3 = (f32[320,128]{1,0:T(8,128)S(1)}, f32[320,128]{1,0:T(8,128)S(1)}, u32[]{:S(2)}, u32[]{:S(2)}) collective-permute-start(f32[320,128]{1,0:T(8,128)S(1)} %collective-permute-done.2.refs_3_), channel_id=1, source_target_pairs={{8,0},{16,8},{24,16},{28,24},{20,28},{12,20},{4,12},{0,4},{9,1},{1... | collective-permute-start | bytes 491528 | tf_op jit(solution)/shard_map/ppermute | solution.py:387
  11.8 0.0 collective-permute-done.refs_0_
  11.8 0.1 collective-permute-start.6
  12.0 0.1 edges.1
  12.1 5.0 %collective-permute-start.1 = (f32[5,8,128]{2,1,0:T(8,128)S(1)}, f32[5,8,128]{2,1,0:T(8,128)S(1)}, u32[]{:S(2)}, u32[]{:S(2)}) collective-permute-start(f32[5,8,128]{2,1,0:T(8,128)S(1)} %edges.1), channel_id=1, source_target_pairs={{0,28},{8,20},{16,12},{24,4},{28,0},{20,8},{12,16},{4,24},{1,29},{... | collective-permute-start | bytes 61448 | tf_op jit(solution)/shard_map/ppermute | solution.py:399
  17.1 2.0 %collective-permute-start.8 = (f32[320,128]{1,0:T(8,128)S(1)}, f32[320,128]{1,0:T(8,128)S(1)}, u32[]{:S(2)}, u32[]{:S(2)}) collective-permute-start(f32[320,128]{1,0:T(8,128)S(1)} %collective-permute-done.5.refs_2_), channel_id=1, source_target_pairs={{8,0},{16,8},{24,16},{28,24},{20,28},{12,20},{4,12},{0,4},{9,1},{1... | collective-permute-start | bytes 491528 | tf_op jit(solution)/shard_map/ppermute | solution.py:387
  19.2 0.7 %constant_dynamic-slice_fusion.weights = f32[1,16]{1,0:T(1,128)S(1)} fusion(f32[8,16]{1,0:T(8,128)} %constant.15.clone, s32[]{:T(128)S(6)} %select_n.3), kind=kLoop, calls=%fused_computation | loop fusion | bytes 132 | tf_op jit(solution)/shard_map/dynamic_slice | solution.py:403
  20.6 0.2 slots.1
  20.8 1.7 %collective-permute-done.1.last_edges = f32[5,8,128]{2,1,0:T(8,128)S(1)} collective-permute-done((f32[5,8,128]{2,1,0:T(8,128)S(1)}, f32[5,8,128]{2,1,0:T(8,128)S(1)}, u32[]{:S(2)}, u32[]{:S(2)}) %collective-permute-start.1) | collective-permute-done | bytes 20512 | tf_op jit(solution)/shard_map/ppermute | solution.py:399
  22.5 2.0 %collective-permute-start.10 = (f32[320,128]{1,0:T(8,128)S(1)}, f32[320,128]{1,0:T(8,128)S(1)}, u32[]{:S(2)}, u32[]{:S(2)}) collective-permute-start(f32[320,128]{1,0:T(8,128)S(1)} %collective-permute-done.6.refs_4_), channel_id=1, source_target_pairs={{0,8},{8,16},{16,24},{24,28},{28,20},{20,12},{12,4},{4,0},{1,9},{9... | collective-permute-start | bytes 491528 | tf_op jit(solution)/shard_map/ppermute | solution.py:386
  24.5 0.1 collective-permute-start.11
  24.6 2.0 %collective-permute-start.12 = (f32[320,128]{1,0:T(8,128)S(1)}, f32[320,128]{1,0:T(8,128)S(1)}, u32[]{:S(2)}, u32[]{:S(2)}) collective-permute-start(f32[320,128]{1,0:T(8,128)S(1)} %collective-permute-done.8.refs_6_), channel_id=1, source_target_pairs={{8,0},{16,8},{24,16},{28,24},{20,28},{12,20},{4,12},{0,4},{9,1},{1... | collective-permute-start | bytes 491528 | tf_op jit(solution)/shard_map/ppermute | solution.py:387
  26.5 0.8 %early.1 = (f32[640,128]{1,0:T(8,128)S(1)}, f32[640,128]{1,0:T(8,128)S(1)}) custom-call(f32[1,16]{1,0:T(1,128)S(1)} %constant_dynamic-slice_fusion.weights, f32[5,1,128,128]{3,2,1,0:T(8,128)S(1)} %copy-done, f32[320,128]{1,0:T(8,128)S(1)} %collective-permute-done.refs_0_, f32[320,128]{1,0:T(8,128)S(1)} %collective-permute-done.4.refs_1_, ...), custom_call_target="tpu_custom_call" | custom-call | tf_op jit(solution)/shard_map/early/pallas_call | solution.py:433
  27.3 1.6 %collective-permute-done.9.right_second = f32[320,128]{1,0:T(8,128)S(1)} collective-permute-done((f32[320,128]{1,0:T(8,128)S(1)}, f32[320,128]{1,0:T(8,128)S(1)}, u32[]{:S(2)}, u32[]{:S(2)}) %collective-permute-start.9) | collective-permute-done | bytes 163872 | tf_op jit(solution)/shard_map/ppermute | solution.py:387
  28.9 0.6 %collective-permute-start.14 = (f32[320,128]{1,0:T(8,128)S(1)}, f32[320,128]{1,0:T(8,128)S(1)}, u32[]{:S(2)}, u32[]{:S(2)}) collective-permute-start(f32[320,128]{1,0:T(8,128)S(1)} %collective-permute-done.9.right_second), channel_id=1, source_target_pairs={{8,0},{16,8},{24,16},{28,24},{20,28},{12,20},{4,12},{0,4},{9,1},{1... | collective-permute-start | bytes 491528 | tf_op jit(solution)/shard_map/ppermute | solution.py:442
  29.5 1.7 %collective-permute-start.13 = (f32[320,128]{1,0:T(8,128)S(1)}, f32[320,128]{1,0:T(8,128)S(1)}, u32[]{:S(2)}, u32[]{:S(2)}) collective-permute-start(f32[320,128]{1,0:T(8,128)S(1)} %collective-permute-done.10.left_first), channel_id=1, source_target_pairs={{0,8},{8,16},{16,24},{24,28},{28,20},{20,12},{12,4},{4,0},{1,9},{9... | collective-permute-start | bytes 491528 | tf_op jit(solution)/shard_map/ppermute | solution.py:441
  31.3 0.2 collective-permute-done.11.left_second
  31.5 0.7 %partial.1 = (f32[640,128]{1,0:T(8,128)S(1)}, f32[640,128]{1,0:T(8,128)S(1)}, f32[5,8,128]{2,1,0:T(8,128)S(1)}) custom-call(f32[1,16]{1,0:T(1,128)S(1)} %constant_dynamic-slice_fusion.weights, f32[640,128]{1,0:T(8,128)S(1)} %get-tuple-element.48.early_smooth, f32[640,128]{1,0:T(8,128)S(1)} %get-tuple-element.49.early_slope, ...), custom_call_target="tpu_custom_call" | custom-call | tf_op jit(solution)/shard_map/partial/pallas_call | solution.py:444
  32.2 0.1 collective-permute-start.15
  32.3 1.6 %collective-permute-start.16 = (f32[5,8,128]{2,1,0:T(8,128)S(1)}, f32[5,8,128]{2,1,0:T(8,128)S(1)}, u32[]{:S(2)}, u32[]{:S(2)}) collective-permute-start(f32[5,8,128]{2,1,0:T(8,128)S(1)} %get-tuple-element.57), channel_id=1, source_target_pairs={{0,1},{1,0},{2,3},{3,2},{4,5},{5,4},{6,7},{7,6},{8,9},{9,8},{10,11... | collective-permute-start | bytes 61448 | tf_op jit(solution)/shard_map/ppermute | solution.py:454
  33.9 0.4 collective-permute-done.14.last_second
  34.2 0.6 %collective-permute-done.13.last_first = f32[320,128]{1,0:T(8,128)S(1)} collective-permute-done((f32[320,128]{1,0:T(8,128)S(1)}, f32[320,128]{1,0:T(8,128)S(1)}, u32[]{:S(2)}, u32[]{:S(2)}) %collective-permute-start.13) | collective-permute-done | bytes 163872 | tf_op jit(solution)/shard_map/ppermute | solution.py:441
  34.9 1.2 %bulk.1 = (f32[5,1,128,128]{3,2,1,0:T(8,128)S(1)}, f32[1,256]{1,0:T(1,128)S(1)}) custom-call(f32[1,16]{1,0:T(1,128)S(1)} %constant_dynamic-slice_fusion.weights, f32[640,128]{1,0:T(8,128)S(1)} %get-tuple-element.52.smooth, f32[640,128]{1,0:T(8,128)S(1)} %get-tuple-element.53.slope, f32[320,128]{1,0:T(8,128)S(1)} %collective-permute-done.13.last_first, ...), custom_call_target="tpu_custom_call" | custom-call | tf_op jit(solution)/shard_map/bulk/pallas_call | solution.py:458
  36.1 0.4 close.1
  36.5 10.5 %all_to_all.11 = f32[32,1,128]{2,1,0:T(1,128)S(1)} all-to-all(f32[32,1,128]{2,1,0:T(1,128)S(1)} %bitcast.8), channel_id=1, replica_groups=mesh['az'=8,'rx'=4] {'az','rx'}, dimensions={0} | all-to-all | bytes 32768 | tf_op jit(solution)/shard_map/all_to_all | solution.py:502
  46.9 0.9 %store.1 = (f32[5,1,128,128]{3,2,1,0:T(8,128)}, f32[8]{0:T(128)}) custom-call(f32[5,1,128,128]{3,2,1,0:T(8,128)S(1)} %get-tuple-element.56.held, f32[5,8,128]{2,1,0:T(8,128)S(1)} %get-tuple-element.64.fixes, f32[32,128]{1,0:T(8,128)S(1)} %bitcast.7), custom_call_target="tpu_custom_call" | custom-call | tf_op jit(solution)/shard_map/store/pallas_call | solution.py:503
  (26 shorter events, 0.1 us)
Async XLA Ops:
  0.6 11.3 %copy-start = (f32[5,1,128,128]{3,2,1,0:T(8,128)S(1)}, f32[5,1,128,128]{3,2,1,0:T(8,128)}, u32[]{:S(2)}) copy-start(f32[5,1,128,128]{3,2,1,0:T(8,128)} %source.2) | copy-start | bytes 983044
  1.7 18.8 %copy-start.1 = (f32[3,1,128,128]{3,2,1,0:T(8,128)S(1)}, f32[3,1,128,128]{3,2,1,0:T(8,128)}, u32[]{:S(2)}) copy-start(f32[3,1,128,128]{3,2,1,0:T(8,128)} %velocity.3) | copy-start | bytes 589828
  1.7 7.8 %collective-permute-start.2 = (f32[320,128]{1,0:T(8,128)S(1)}, f32[320,128]{1,0:T(8,128)S(1)}, u32[]{:S(2)}, u32[]{:S(2)}) collective-permute-start(f32[320,128]{1,0:T(8,128)S(1)} %get-tuple-element.66), channel_id=1, source_target_pairs={{8,0},{16,8},{24,16},{28,24},{20,28},{12,20},{4,12},{0,4},{9,1},{1... | collective-permute-start | bytes 491528 | tf_op jit(solution)/shard_map/ppermute | solution.py:387
  4.7 7.1 %collective-permute-start = (f32[320,128]{1,0:T(8,128)S(1)}, f32[320,128]{1,0:T(8,128)S(1)}, u32[]{:S(2)}, u32[]{:S(2)}) collective-permute-start(f32[320,128]{1,0:T(8,128)S(1)} %get-tuple-element.67), channel_id=1, source_target_pairs={{0,8},{8,16},{16,24},{24,28},{28,20},{20,12},{12,4},{4,0},{1,9},{9... | collective-permute-start | bytes 491528 | tf_op jit(solution)/shard_map/ppermute | solution.py:386
  4.9 12.3 %collective-permute-start.4 = (f32[320,128]{1,0:T(8,128)S(1)}, f32[320,128]{1,0:T(8,128)S(1)}, u32[]{:S(2)}, u32[]{:S(2)}) collective-permute-start(f32[320,128]{1,0:T(8,128)S(1)} %get-tuple-element.66), channel_id=1, source_target_pairs={{0,8},{8,16},{16,24},{24,28},{28,20},{20,12},{12,4},{4,0},{1,9},{9... | collective-permute-start | bytes 491528 | tf_op jit(solution)/shard_map/ppermute | solution.py:386
  6.8 10.3 %collective-permute-start.5 = (f32[320,128]{1,0:T(8,128)S(1)}, f32[320,128]{1,0:T(8,128)S(1)}, u32[]{:S(2)}, u32[]{:S(2)}) collective-permute-start(f32[320,128]{1,0:T(8,128)S(1)} %get-tuple-element.67), channel_id=1, source_target_pairs={{8,0},{16,8},{24,16},{28,24},{20,28},{12,20},{4,12},{0,4},{9,1},{1... | collective-permute-start | bytes 491528 | tf_op jit(solution)/shard_map/ppermute | solution.py:387
  9.5 12.9 %collective-permute-start.3 = (f32[320,128]{1,0:T(8,128)S(1)}, f32[320,128]{1,0:T(8,128)S(1)}, u32[]{:S(2)}, u32[]{:S(2)}) collective-permute-start(f32[320,128]{1,0:T(8,128)S(1)} %collective-permute-done.2.refs_3_), channel_id=1, source_target_pairs={{8,0},{16,8},{24,16},{28,24},{20,28},{12,20},{4,12},{0,4},{9,1},{1... | collective-permute-start | bytes 491528 | tf_op jit(solution)/shard_map/ppermute | solution.py:387
  11.8 10.6 %collective-permute-start.6 = (f32[320,128]{1,0:T(8,128)S(1)}, f32[320,128]{1,0:T(8,128)S(1)}, u32[]{:S(2)}, u32[]{:S(2)}) collective-permute-start(f32[320,128]{1,0:T(8,128)S(1)} %collective-permute-done.refs_0_), channel_id=1, source_target_pairs={{0,8},{8,16},{16,24},{24,28},{28,20},{20,12},{12,4},{4,0},{1,9},{9... | collective-permute-start | bytes 491528 | tf_op jit(solution)/shard_map/ppermute | solution.py:386
  11.9 8.6 %copy-start.2 = (f32[1,128,128]{2,1,0:T(8,128)S(1)}, f32[1,128,128]{2,1,0:T(8,128)}, u32[]{:S(2)}) copy-start(f32[1,128,128]{2,1,0:T(8,128)} %density.3) | copy-start | bytes 196612
  12.0 8.6 %copy-start.3 = (f32[1,128,128]{2,1,0:T(8,128)S(1)}, f32[1,128,128]{2,1,0:T(8,128)}, u32[]{:S(2)}) copy-start(f32[1,128,128]{2,1,0:T(8,128)} %pressure.3) | copy-start | bytes 196612
  12.0 8.6 %copy-start.5 = (s32[1,1,256]{2,1,0:T(1,128)S(1)}, s32[1,1,256]{2,1,0:T(1,128)}, u32[]{:S(2)}) copy-start(s32[1,1,256]{2,1,0:T(1,128)} %bins.1) | copy-start | bytes 3076
  12.0 8.6 %copy-start.6 = (f32[1,1,256]{2,1,0:T(1,128)S(1)}, f32[1,1,256]{2,1,0:T(1,128)}, u32[]{:S(2)}) copy-start(f32[1,1,256]{2,1,0:T(1,128)} %slot_weights.1) | copy-start | bytes 3076
  12.1 10.3 %collective-permute-start.1 = (f32[5,8,128]{2,1,0:T(8,128)S(1)}, f32[5,8,128]{2,1,0:T(8,128)S(1)}, u32[]{:S(2)}, u32[]{:S(2)}) collective-permute-start(f32[5,8,128]{2,1,0:T(8,128)S(1)} %edges.1), channel_id=1, source_target_pairs={{0,28},{8,20},{16,12},{24,4},{28,0},{20,8},{12,16},{4,24},{1,29},{... | collective-permute-start | bytes 61448 | tf_op jit(solution)/shard_map/ppermute | solution.py:399
  17.1 7.4 %collective-permute-start.7 = (f32[320,128]{1,0:T(8,128)S(1)}, f32[320,128]{1,0:T(8,128)S(1)}, u32[]{:S(2)}, u32[]{:S(2)}) collective-permute-start(f32[320,128]{1,0:T(8,128)S(1)} %collective-permute-done.4.refs_1_), channel_id=1, source_target_pairs={{0,8},{8,16},{16,24},{24,28},{28,20},{20,12},{12,4},{4,0},{1,9},{9... | collective-permute-start | bytes 491528 | tf_op jit(solution)/shard_map/ppermute | solution.py:386
  17.1 7.4 %collective-permute-start.8 = (f32[320,128]{1,0:T(8,128)S(1)}, f32[320,128]{1,0:T(8,128)S(1)}, u32[]{:S(2)}, u32[]{:S(2)}) collective-permute-start(f32[320,128]{1,0:T(8,128)S(1)} %collective-permute-done.5.refs_2_), channel_id=1, source_target_pairs={{8,0},{16,8},{24,16},{28,24},{20,28},{12,20},{4,12},{0,4},{9,1},{1... | collective-permute-start | bytes 491528 | tf_op jit(solution)/shard_map/ppermute | solution.py:387
  19.9 0.7 %copy-start.4 = (s32[1,1,256]{2,1,0:T(1,128)S(1)}, s32[1,1,256]{2,1,0:T(1,128)}, u32[]{:S(2)}) copy-start(s32[1,1,256]{2,1,0:T(1,128)} %cells.1) | copy-start | bytes 3076
  22.5 6.5 %collective-permute-start.9 = (f32[320,128]{1,0:T(8,128)S(1)}, f32[320,128]{1,0:T(8,128)S(1)}, u32[]{:S(2)}, u32[]{:S(2)}) collective-permute-start(f32[320,128]{1,0:T(8,128)S(1)} %collective-permute-done.3.refs_7_), channel_id=1, source_target_pairs={{8,0},{16,8},{24,16},{28,24},{20,28},{12,20},{4,12},{0,4},{9,1},{1... | collective-permute-start | bytes 491528 | tf_op jit(solution)/shard_map/ppermute | solution.py:387
  22.5 7.1 %collective-permute-start.10 = (f32[320,128]{1,0:T(8,128)S(1)}, f32[320,128]{1,0:T(8,128)S(1)}, u32[]{:S(2)}, u32[]{:S(2)}) collective-permute-start(f32[320,128]{1,0:T(8,128)S(1)} %collective-permute-done.6.refs_4_), channel_id=1, source_target_pairs={{0,8},{8,16},{16,24},{24,28},{28,20},{20,12},{12,4},{4,0},{1,9},{9... | collective-permute-start | bytes 491528 | tf_op jit(solution)/shard_map/ppermute | solution.py:386
  24.5 7.0 %collective-permute-start.11 = (f32[320,128]{1,0:T(8,128)S(1)}, f32[320,128]{1,0:T(8,128)S(1)}, u32[]{:S(2)}, u32[]{:S(2)}) collective-permute-start(f32[320,128]{1,0:T(8,128)S(1)} %collective-permute-done.7.refs_5_), channel_id=1, source_target_pairs={{0,8},{8,16},{16,24},{24,28},{28,20},{20,12},{12,4},{4,0},{1,9},{9... | collective-permute-start | bytes 491528 | tf_op jit(solution)/shard_map/ppermute | solution.py:386
  24.6 6.9 %collective-permute-start.12 = (f32[320,128]{1,0:T(8,128)S(1)}, f32[320,128]{1,0:T(8,128)S(1)}, u32[]{:S(2)}, u32[]{:S(2)}) collective-permute-start(f32[320,128]{1,0:T(8,128)S(1)} %collective-permute-done.8.refs_6_), channel_id=1, source_target_pairs={{8,0},{16,8},{24,16},{28,24},{20,28},{12,20},{4,12},{0,4},{9,1},{1... | collective-permute-start | bytes 491528 | tf_op jit(solution)/shard_map/ppermute | solution.py:387
  28.9 5.3 %collective-permute-start.14 = (f32[320,128]{1,0:T(8,128)S(1)}, f32[320,128]{1,0:T(8,128)S(1)}, u32[]{:S(2)}, u32[]{:S(2)}) collective-permute-start(f32[320,128]{1,0:T(8,128)S(1)} %collective-permute-done.9.right_second), channel_id=1, source_target_pairs={{8,0},{16,8},{24,16},{28,24},{20,28},{12,20},{4,12},{0,4},{9,1},{1... | collective-permute-start | bytes 491528 | tf_op jit(solution)/shard_map/ppermute | solution.py:442
  29.5 5.3 %collective-permute-start.13 = (f32[320,128]{1,0:T(8,128)S(1)}, f32[320,128]{1,0:T(8,128)S(1)}, u32[]{:S(2)}, u32[]{:S(2)}) collective-permute-start(f32[320,128]{1,0:T(8,128)S(1)} %collective-permute-done.10.left_first), channel_id=1, source_target_pairs={{0,8},{8,16},{16,24},{24,28},{28,20},{20,12},{12,4},{4,0},{1,9},{9... | collective-permute-start | bytes 491528 | tf_op jit(solution)/shard_map/ppermute | solution.py:441
  32.2 3.9 %collective-permute-start.15 = (f32[5,8,128]{2,1,0:T(8,128)S(1)}, f32[5,8,128]{2,1,0:T(8,128)S(1)}, u32[]{:S(2)}, u32[]{:S(2)}) collective-permute-start(f32[5,8,128]{2,1,0:T(8,128)S(1)} %get-tuple-element.57), channel_id=1, source_target_pairs={{0,3},{1,2},{2,1},{3,0},{4,7},{5,6},{6,5},{7,4},{8,11},{9,10},{10,... | collective-permute-start | bytes 61448 | tf_op jit(solution)/shard_map/ppermute | solution.py:454
  32.3 3.8 %collective-permute-start.16 = (f32[5,8,128]{2,1,0:T(8,128)S(1)}, f32[5,8,128]{2,1,0:T(8,128)S(1)}, u32[]{:S(2)}, u32[]{:S(2)}) collective-permute-start(f32[5,8,128]{2,1,0:T(8,128)S(1)} %get-tuple-element.57), channel_id=1, source_target_pairs={{0,1},{1,0},{2,3},{3,2},{4,5},{5,4},{6,7},{7,6},{8,9},{9,8},{10,11... | collective-permute-start | bytes 61448 | tf_op jit(solution)/shard_map/ppermute | solution.py:454

commit v8 on v7

--- a/solution.py
+++ b/solution.py
@@ -89,7 +89,9 @@
 
 def early_body(weights, source, *refs):
     count = weights.shape[1] // 2
-    halves, (smooth, slope) = refs[:-2], refs[-2:]
+    halves, (smooth, slope, spread) = refs[:-3], refs[-3:]
+    for k in range(2 * count):
+        spread[k] = jnp.full((TILE, LANES), weights[0, k], jnp.float32)
     fields, radial = source.shape[0], source.shape[2]
     half = halves[0].shape[0]
     for field in range(fields):
@@ -118,7 +120,7 @@
     slope,
     edges,
 ):
-    count, fields = weights.shape[1] // 2, edges.shape[0]
+    count, fields = weights.shape[0] // 2, edges.shape[0]
     half, radial = left_first.shape[0], smooth.shape[0] // fields
     lefts, rights = (left_first, left_second), (right_first, right_second)
     for field in range(fields):
@@ -127,12 +129,12 @@
             at = field * radial + row
             rows, part = pl.ds(at, TILE), pl.ds(at % half, TILE)
             left, right = lefts[at // half][part, :], rights[at // half][part, :]
-            near, far = weights[0, count - 3], weights[0, count - 2]
+            near, far = weights[count - 3], weights[count - 2]
             tiles.append(early_smooth[rows, :] + (near * left + far * right))
             smooth[rows, :] = tiles[-1]
-            near, far = weights[0, 2 * count - 3], weights[0, 2 * count - 2]
+            near, far = weights[2 * count - 3], weights[2 * count - 2]
             slope[rows, :] = early_slope[rows, :] + (near * left + far * right)
-        edges[field] = packed_edges(tiles) + weights[0, count - 1] * last_edges[field]
+        edges[field] = packed_edges(tiles) + weights[count - 1] * last_edges[field]
 
 
 def slots_body(
@@ -218,9 +220,9 @@
     picked,
 ):
     fields, radial = section.shape[0], section.shape[2]
-    count = weights.shape[1] // 2
+    count = weights.shape[0] // 2
     half = last_first.shape[0]
-    last_weight, last_slope = weights[0, count - 1], weights[0, 2 * count - 1]
+    last_weight, last_slope = weights[count - 1], weights[2 * count - 1]
 
     def last(at):
         source = last_first if at < half else last_second
@@ -424,17 +426,21 @@
                 (weights, tables, from_right[1])
             )
         if step == steps - 1:
-            smooth, slope, from_right[1] = lax.optimization_barrier(
-                (smooth, slope, from_right[1])
+            smooth, slope, spread, from_right[1] = lax.optimization_barrier(
+                (smooth, slope, spread, from_right[1])
             )
             continue
         halves += from_left + from_right
         if step == steps - 2:
-            smooth, slope = pl.pallas_call(
+            smooth, slope, spread = pl.pallas_call(
                 early_body,
-                out_shape=(jax.ShapeDtypeStruct((rows, LANES), f32),) * 2,
+                out_shape=(
+                    jax.ShapeDtypeStruct((rows, LANES), f32),
+                    jax.ShapeDtypeStruct((rows, LANES), f32),
+                    jax.ShapeDtypeStruct((2 * thetas, TILE, LANES), f32),
+                ),
                 in_specs=in_smem(1) + in_vmem(1 + len(halves)),
-                out_specs=tuple(in_vmem(2)),
+                out_specs=tuple(in_vmem(3)),
                 compiler_params=params,
                 name="early",
             )(weights, adjoint, *halves)
@@ -444,11 +450,11 @@
     smooth, slope, edges = pl.pallas_call(
         partial_body,
         out_shape=(jax.ShapeDtypeStruct((rows, LANES), f32),) * 2 + (edge_shape,),
-        in_specs=in_smem(1) + in_vmem(7),
+        in_specs=in_vmem(8),
         out_specs=tuple(in_vmem(3)),
         compiler_params=params,
         name="partial",
-    )(weights, smooth, slope, *from_left, *from_right, last_edges)
+    )(spread, smooth, slope, *from_left, *from_right, last_edges)
     pairs = [(b, b ^ 1) for b in range(blocks_x)]
     nexts = [(b, (b + (1 if b % 2 else -1)) % blocks_x) for b in range(blocks_x)]
     edges_next, edges_pair = lax.ppermute(edges, "rx", nexts), lax.ppermute(edges, "rx", pairs)
@@ -461,7 +467,7 @@
             jax.ShapeDtypeStruct(adjoint.shape, f32),
             jax.ShapeDtypeStruct((1, slots), f32),
         ),
-        in_specs=in_smem(1) + in_vmem(9),
+        in_specs=in_vmem(10),
         out_specs=tuple(in_vmem(2)),
         scratch_shapes=[
             pltpu.VMEM((fields, radial + 2 * TILE, LANES), f32),
@@ -470,7 +476,7 @@
         compiler_params=params,
         name="bulk",
     )(
-        weights,
+        spread,
         smooth,
         slope,
         last_first,

time: 48 us -> 47.5 us (0.990)
  Pallas kernels: 4.26 us -> 3.19 us
  waiting for transfers between devices: 7.19 us -> 7.72 us
    pallas_call x1, Pallas kernels: 1.21 us -> 0.67 us  [local(): pl.pallas_call(bulk_body, out_shape=(jax.ShapeDtypeStruct(adjoint.shape,...]
    ppermute x1, waiting for transfers between devices: 0.36 us -> 0.89 us  [local(): last_second = lax.ppermute(from_right[1], 'az', back)]
    pallas_call x1, Pallas kernels: 0.73 us -> 0.2 us  [local(): pl.pallas_call(partial_body, out_shape=(jax.ShapeDtypeStruct((rows, LANES...]
  transfers between devices with their start and end apart: 17 -> 17, of which waited for: 6 -> 6; matrix products, arithmetic and copies ran while one was open for 1% -> 1% of each run, Pallas kernels for 6% -> 4%
where the time goes in v8:
time: 47.5 us; the launch traced here: 47.3 us
  starting transfers between devices  22.7 us (48%)
  blocking collectives  10.5 us (22%)
  waiting for transfers between devices  7.72 us (16%)
  Pallas kernels  3.19 us (7%)
  local copies, waits for them, and re-layouts  1.79 us (4%)
  between operations  1.43 us (3%)
    all_to_all x1, blocking collectives, local(): totals = lax.all_to_all(totals, ('az', 'rx'), 0, 0, tiled=True)  10.5 us
    ppermute x6, starting transfers between devices, local(): right.append(lax.ppermute(from_right[part], 'az', back))  9.34 us
    ppermute x1, starting transfers between devices, local(): last_edges = lax.ppermute(last_edges, 'az', across)  5.02 us
    ppermute x6, starting transfers between devices, local(): left.append(lax.ppermute(from_left[part], 'az', onward))  4.3 us
    ppermute x6, waiting for transfers between devices, local(): right.append(lax.ppermute(from_right[part], 'az', back))  4.27 us
    ppermute x1, starting transfers between devices, local(): last_first = lax.ppermute(from_left[0], 'az', onward)  1.71 us
    ppermute x1, waiting for transfers between devices, local(): last_edges = lax.ppermute(last_edges, 'az', across)  1.69 us
    ppermute x1, starting transfers between devices, local(): lax.ppermute(edges, 'rx', pairs)  1.62 us
  transfers between devices with their start and end apart: 17, of which 6 were waited for; matrix products, arithmetic and copies ran while one was open for 1% of the time, Pallas kernels for 4%

profile of v8, /device:TPU:0, one launch (start us, length us, event | category | flops | bytes accessed | tf_op | source)
XLA Modules:
  0.0 47.3 jit_solution(13981173784686391389)
XLA Ops:
  0.6 1.1 %fusion = (f32[320,128]{1,0:T(8,128)S(1)}, f32[320,128]{1,0:T(8,128)S(1)}) fusion(f32[640,128]{1,0:T(8,128)} %bitcast.6), kind=kLoop, calls=%fused_computation.1 | loop fusion | bytes 655360 | tf_op jit(solution)/shard_map/slice | solution.py:381
  1.7 3.0 %collective-permute-start.2 = (f32[320,128]{1,0:T(8,128)S(1)}, f32[320,128]{1,0:T(8,128)S(1)}, u32[]{:S(2)}, u32[]{:S(2)}) collective-permute-start(f32[320,128]{1,0:T(8,128)S(1)} %get-tuple-element.70), channel_id=1, source_target_pairs={{8,0},{16,8},{24,16},{28,24},{20,28},{12,20},{4,12},{0,4},{9,1},{1... | collective-permute-start | bytes 491528 | tf_op jit(solution)/shard_map/ppermute | solution.py:389
  4.7 0.2 collective-permute-start
  4.9 2.0 %collective-permute-start.4 = (f32[320,128]{1,0:T(8,128)S(1)}, f32[320,128]{1,0:T(8,128)S(1)}, u32[]{:S(2)}, u32[]{:S(2)}) collective-permute-start(f32[320,128]{1,0:T(8,128)S(1)} %get-tuple-element.70), channel_id=1, source_target_pairs={{0,8},{8,16},{16,24},{24,28},{28,20},{20,12},{12,4},{4,0},{1,9},{9... | collective-permute-start | bytes 491528 | tf_op jit(solution)/shard_map/ppermute | solution.py:388
  6.8 0.1 collective-permute-start.5
  6.9 2.6 %collective-permute-done.2.refs_3_ = f32[320,128]{1,0:T(8,128)S(1)} collective-permute-done((f32[320,128]{1,0:T(8,128)S(1)}, f32[320,128]{1,0:T(8,128)S(1)}, u32[]{:S(2)}, u32[]{:S(2)}) %collective-permute-start.2) | collective-permute-done | bytes 163872 | tf_op jit(solution)/shard_map/ppermute | solution.py:389
  9.5 2.3 %collective-permute-start.3 = (f32[320,128]{1,0:T(8,128)S(1)}, f32[320,128]{1,0:T(8,128)S(1)}, u32[]{:S(2)}, u32[]{:S(2)}) collective-permute-start(f32[320,128]{1,0:T(8,128)S(1)} %collective-permute-done.2.refs_3_), channel_id=1, source_target_pairs={{8,0},{16,8},{24,16},{28,24},{20,28},{12,20},{4,12},{0,4},{9,1},{1... | collective-permute-start | bytes 491528 | tf_op jit(solution)/shard_map/ppermute | solution.py:389
  11.8 0.0 collective-permute-done.refs_0_
  11.8 0.1 collective-permute-start.6
  12.0 0.1 edges.1
  12.1 5.0 %collective-permute-start.1 = (f32[5,8,128]{2,1,0:T(8,128)S(1)}, f32[5,8,128]{2,1,0:T(8,128)S(1)}, u32[]{:S(2)}, u32[]{:S(2)}) collective-permute-start(f32[5,8,128]{2,1,0:T(8,128)S(1)} %edges.1), channel_id=1, source_target_pairs={{0,28},{8,20},{16,12},{24,4},{28,0},{20,8},{12,16},{4,24},{1,29},{... | collective-permute-start | bytes 61448 | tf_op jit(solution)/shard_map/ppermute | solution.py:401
  17.1 2.0 %collective-permute-start.8 = (f32[320,128]{1,0:T(8,128)S(1)}, f32[320,128]{1,0:T(8,128)S(1)}, u32[]{:S(2)}, u32[]{:S(2)}) collective-permute-start(f32[320,128]{1,0:T(8,128)S(1)} %collective-permute-done.5.refs_2_), channel_id=1, source_target_pairs={{8,0},{16,8},{24,16},{28,24},{20,28},{12,20},{4,12},{0,4},{9,1},{1... | collective-permute-start | bytes 491528 | tf_op jit(solution)/shard_map/ppermute | solution.py:389
  19.2 0.7 %constant_dynamic-slice_fusion.weights = f32[1,16]{1,0:T(1,128)S(1)} fusion(f32[8,16]{1,0:T(8,128)} %constant.15.clone, s32[]{:T(128)S(6)} %select_n.3), kind=kLoop, calls=%fused_computation | loop fusion | bytes 132 | tf_op jit(solution)/shard_map/dynamic_slice | solution.py:405
  20.6 0.2 slots.1
  20.8 1.7 %collective-permute-done.1.last_edges = f32[5,8,128]{2,1,0:T(8,128)S(1)} collective-permute-done((f32[5,8,128]{2,1,0:T(8,128)S(1)}, f32[5,8,128]{2,1,0:T(8,128)S(1)}, u32[]{:S(2)}, u32[]{:S(2)}) %collective-permute-start.1) | collective-permute-done | bytes 20512 | tf_op jit(solution)/shard_map/ppermute | solution.py:401
  22.5 2.0 %collective-permute-start.10 = (f32[320,128]{1,0:T(8,128)S(1)}, f32[320,128]{1,0:T(8,128)S(1)}, u32[]{:S(2)}, u32[]{:S(2)}) collective-permute-start(f32[320,128]{1,0:T(8,128)S(1)} %collective-permute-done.6.refs_4_), channel_id=1, source_target_pairs={{0,8},{8,16},{16,24},{24,28},{28,20},{20,12},{12,4},{4,0},{1,9},{9... | collective-permute-start | bytes 491528 | tf_op jit(solution)/shard_map/ppermute | solution.py:388
  24.5 0.1 collective-permute-start.11
  24.6 2.0 %collective-permute-start.12 = (f32[320,128]{1,0:T(8,128)S(1)}, f32[320,128]{1,0:T(8,128)S(1)}, u32[]{:S(2)}, u32[]{:S(2)}) collective-permute-start(f32[320,128]{1,0:T(8,128)S(1)} %collective-permute-done.8.refs_6_), channel_id=1, source_target_pairs={{8,0},{16,8},{24,16},{28,24},{20,28},{12,20},{4,12},{0,4},{9,1},{1... | collective-permute-start | bytes 491528 | tf_op jit(solution)/shard_map/ppermute | solution.py:389
  26.5 0.8 %early.1 = (f32[640,128]{1,0:T(8,128)S(1)}, f32[640,128]{1,0:T(8,128)S(1)}, f32[16,8,128]{2,1,0:T(8,128)S(1)}) custom-call(f32[1,16]{1,0:T(1,128)S(1)} %constant_dynamic-slice_fusion.weights, f32[5,1,128,128]{3,2,1,0:T(8,128)S(1)} %copy-done, f32[320,128]{1,0:T(8,128)S(1)} %collective-permute-done.refs_0_, f32[320,128]{1,0:T(8,128)S(1)} %collective-permute-done.4.refs_1_, ...), custom_call_target="tpu_custom_call" | custom-call | tf_op jit(solution)/shard_map/early/pallas_call | solution.py:435
  27.3 1.6 %collective-permute-done.9.right_second = f32[320,128]{1,0:T(8,128)S(1)} collective-permute-done((f32[320,128]{1,0:T(8,128)S(1)}, f32[320,128]{1,0:T(8,128)S(1)}, u32[]{:S(2)}, u32[]{:S(2)}) %collective-permute-start.9) | collective-permute-done | bytes 163872 | tf_op jit(solution)/shard_map/ppermute | solution.py:389
  28.9 0.6 %collective-permute-start.14 = (f32[320,128]{1,0:T(8,128)S(1)}, f32[320,128]{1,0:T(8,128)S(1)}, u32[]{:S(2)}, u32[]{:S(2)}) collective-permute-start(f32[320,128]{1,0:T(8,128)S(1)} %collective-permute-done.9.right_second), channel_id=1, source_target_pairs={{8,0},{16,8},{24,16},{28,24},{20,28},{12,20},{4,12},{0,4},{9,1},{1... | collective-permute-start | bytes 491528 | tf_op jit(solution)/shard_map/ppermute | solution.py:448
  29.5 1.7 %collective-permute-start.13 = (f32[320,128]{1,0:T(8,128)S(1)}, f32[320,128]{1,0:T(8,128)S(1)}, u32[]{:S(2)}, u32[]{:S(2)}) collective-permute-start(f32[320,128]{1,0:T(8,128)S(1)} %collective-permute-done.10.left_first), channel_id=1, source_target_pairs={{0,8},{8,16},{16,24},{24,28},{28,20},{20,12},{12,4},{4,0},{1,9},{9... | collective-permute-start | bytes 491528 | tf_op jit(solution)/shard_map/ppermute | solution.py:447
  31.3 0.2 collective-permute-done.11.left_second
  31.5 0.2 partial.1
  31.7 0.1 collective-permute-start.15
  31.7 1.6 %collective-permute-start.16 = (f32[5,8,128]{2,1,0:T(8,128)S(1)}, f32[5,8,128]{2,1,0:T(8,128)S(1)}, u32[]{:S(2)}, u32[]{:S(2)}) collective-permute-start(f32[5,8,128]{2,1,0:T(8,128)S(1)} %get-tuple-element.61), channel_id=1, source_target_pairs={{0,1},{1,0},{2,3},{3,2},{4,5},{5,4},{6,7},{7,6},{8,9},{9,8},{10,11... | collective-permute-start | bytes 61448 | tf_op jit(solution)/shard_map/ppermute | solution.py:460
  33.4 0.9 %collective-permute-done.14.last_second = f32[320,128]{1,0:T(8,128)S(1)} collective-permute-done((f32[320,128]{1,0:T(8,128)S(1)}, f32[320,128]{1,0:T(8,128)S(1)}, u32[]{:S(2)}, u32[]{:S(2)}) %collective-permute-start.14) | collective-permute-done | bytes 163872 | tf_op jit(solution)/shard_map/ppermute | solution.py:448
  34.2 0.6 %collective-permute-done.13.last_first = f32[320,128]{1,0:T(8,128)S(1)} collective-permute-done((f32[320,128]{1,0:T(8,128)S(1)}, f32[320,128]{1,0:T(8,128)S(1)}, u32[]{:S(2)}, u32[]{:S(2)}) %collective-permute-start.13) | collective-permute-done | bytes 163872 | tf_op jit(solution)/shard_map/ppermute | solution.py:447
  34.9 0.7 %bulk.1 = (f32[5,1,128,128]{3,2,1,0:T(8,128)S(1)}, f32[1,256]{1,0:T(1,128)S(1)}) custom-call(f32[16,8,128]{2,1,0:T(8,128)S(1)} %get-tuple-element.51.weights, f32[640,128]{1,0:T(8,128)S(1)} %get-tuple-element.56.smooth, f32[640,128]{1,0:T(8,128)S(1)} %get-tuple-element.57.slope, f32[320,128]{1,0:T(8,128)S(1)} %collective-permute-done.13.last_first, ...), custom_call_target="tpu_custom_call" | custom-call | tf_op jit(solution)/shard_map/bulk/pallas_call | solution.py:464
  35.6 0.4 close.1
  35.9 10.5 %all_to_all.11 = f32[32,1,128]{2,1,0:T(1,128)S(1)} all-to-all(f32[32,1,128]{2,1,0:T(1,128)S(1)} %bitcast.8), channel_id=1, replica_groups=mesh['az'=8,'rx'=4] {'az','rx'}, dimensions={0} | all-to-all | bytes 32768 | tf_op jit(solution)/shard_map/all_to_all | solution.py:508
  46.4 0.9 %store.1 = (f32[5,1,128,128]{3,2,1,0:T(8,128)}, f32[8]{0:T(128)}) custom-call(f32[5,1,128,128]{3,2,1,0:T(8,128)S(1)} %get-tuple-element.60.held, f32[5,8,128]{2,1,0:T(8,128)S(1)} %get-tuple-element.68.fixes, f32[32,128]{1,0:T(8,128)S(1)} %bitcast.7), custom_call_target="tpu_custom_call" | custom-call | tf_op jit(solution)/shard_map/store/pallas_call | solution.py:509
  (26 shorter events, 0.1 us)
Async XLA Ops:
  0.6 11.3 %copy-start = (f32[5,1,128,128]{3,2,1,0:T(8,128)S(1)}, f32[5,1,128,128]{3,2,1,0:T(8,128)}, u32[]{:S(2)}) copy-start(f32[5,1,128,128]{3,2,1,0:T(8,128)} %source.2) | copy-start | bytes 983044
  1.7 18.8 %copy-start.1 = (f32[3,1,128,128]{3,2,1,0:T(8,128)S(1)}, f32[3,1,128,128]{3,2,1,0:T(8,128)}, u32[]{:S(2)}) copy-start(f32[3,1,128,128]{3,2,1,0:T(8,128)} %velocity.3) | copy-start | bytes 589828
  1.7 7.8 %collective-permute-start.2 = (f32[320,128]{1,0:T(8,128)S(1)}, f32[320,128]{1,0:T(8,128)S(1)}, u32[]{:S(2)}, u32[]{:S(2)}) collective-permute-start(f32[320,128]{1,0:T(8,128)S(1)} %get-tuple-element.70), channel_id=1, source_target_pairs={{8,0},{16,8},{24,16},{28,24},{20,28},{12,20},{4,12},{0,4},{9,1},{1... | collective-permute-start | bytes 491528 | tf_op jit(solution)/shard_map/ppermute | solution.py:389
  4.7 7.1 %collective-permute-start = (f32[320,128]{1,0:T(8,128)S(1)}, f32[320,128]{1,0:T(8,128)S(1)}, u32[]{:S(2)}, u32[]{:S(2)}) collective-permute-start(f32[320,128]{1,0:T(8,128)S(1)} %get-tuple-element.71), channel_id=1, source_target_pairs={{0,8},{8,16},{16,24},{24,28},{28,20},{20,12},{12,4},{4,0},{1,9},{9... | collective-permute-start | bytes 491528 | tf_op jit(solution)/shard_map/ppermute | solution.py:388
  4.9 12.3 %collective-permute-start.4 = (f32[320,128]{1,0:T(8,128)S(1)}, f32[320,128]{1,0:T(8,128)S(1)}, u32[]{:S(2)}, u32[]{:S(2)}) collective-permute-start(f32[320,128]{1,0:T(8,128)S(1)} %get-tuple-element.70), channel_id=1, source_target_pairs={{0,8},{8,16},{16,24},{24,28},{28,20},{20,12},{12,4},{4,0},{1,9},{9... | collective-permute-start | bytes 491528 | tf_op jit(solution)/shard_map/ppermute | solution.py:388
  6.8 10.3 %collective-permute-start.5 = (f32[320,128]{1,0:T(8,128)S(1)}, f32[320,128]{1,0:T(8,128)S(1)}, u32[]{:S(2)}, u32[]{:S(2)}) collective-permute-start(f32[320,128]{1,0:T(8,128)S(1)} %get-tuple-element.71), channel_id=1, source_target_pairs={{8,0},{16,8},{24,16},{28,24},{20,28},{12,20},{4,12},{0,4},{9,1},{1... | collective-permute-start | bytes 491528 | tf_op jit(solution)/shard_map/ppermute | solution.py:389
  9.5 12.9 %collective-permute-start.3 = (f32[320,128]{1,0:T(8,128)S(1)}, f32[320,128]{1,0:T(8,128)S(1)}, u32[]{:S(2)}, u32[]{:S(2)}) collective-permute-start(f32[320,128]{1,0:T(8,128)S(1)} %collective-permute-done.2.refs_3_), channel_id=1, source_target_pairs={{8,0},{16,8},{24,16},{28,24},{20,28},{12,20},{4,12},{0,4},{9,1},{1... | collective-permute-start | bytes 491528 | tf_op jit(solution)/shard_map/ppermute | solution.py:389
  11.8 10.6 %collective-permute-start.6 = (f32[320,128]{1,0:T(8,128)S(1)}, f32[320,128]{1,0:T(8,128)S(1)}, u32[]{:S(2)}, u32[]{:S(2)}) collective-permute-start(f32[320,128]{1,0:T(8,128)S(1)} %collective-permute-done.refs_0_), channel_id=1, source_target_pairs={{0,8},{8,16},{16,24},{24,28},{28,20},{20,12},{12,4},{4,0},{1,9},{9... | collective-permute-start | bytes 491528 | tf_op jit(solution)/shard_map/ppermute | solution.py:388
  11.9 8.6 %copy-start.2 = (f32[1,128,128]{2,1,0:T(8,128)S(1)}, f32[1,128,128]{2,1,0:T(8,128)}, u32[]{:S(2)}) copy-start(f32[1,128,128]{2,1,0:T(8,128)} %density.3) | copy-start | bytes 196612
  12.0 8.6 %copy-start.3 = (f32[1,128,128]{2,1,0:T(8,128)S(1)}, f32[1,128,128]{2,1,0:T(8,128)}, u32[]{:S(2)}) copy-start(f32[1,128,128]{2,1,0:T(8,128)} %pressure.3) | copy-start | bytes 196612
  12.0 8.6 %copy-start.5 = (s32[1,1,256]{2,1,0:T(1,128)S(1)}, s32[1,1,256]{2,1,0:T(1,128)}, u32[]{:S(2)}) copy-start(s32[1,1,256]{2,1,0:T(1,128)} %bins.1) | copy-start | bytes 3076
  12.0 8.6 %copy-start.6 = (f32[1,1,256]{2,1,0:T(1,128)S(1)}, f32[1,1,256]{2,1,0:T(1,128)}, u32[]{:S(2)}) copy-start(f32[1,1,256]{2,1,0:T(1,128)} %slot_weights.1) | copy-start | bytes 3076
  12.1 10.3 %collective-permute-start.1 = (f32[5,8,128]{2,1,0:T(8,128)S(1)}, f32[5,8,128]{2,1,0:T(8,128)S(1)}, u32[]{:S(2)}, u32[]{:S(2)}) collective-permute-start(f32[5,8,128]{2,1,0:T(8,128)S(1)} %edges.1), channel_id=1, source_target_pairs={{0,28},{8,20},{16,12},{24,4},{28,0},{20,8},{12,16},{4,24},{1,29},{... | collective-permute-start | bytes 61448 | tf_op jit(solution)/shard_map/ppermute | solution.py:401
  17.1 7.4 %collective-permute-start.7 = (f32[320,128]{1,0:T(8,128)S(1)}, f32[320,128]{1,0:T(8,128)S(1)}, u32[]{:S(2)}, u32[]{:S(2)}) collective-permute-start(f32[320,128]{1,0:T(8,128)S(1)} %collective-permute-done.4.refs_1_), channel_id=1, source_target_pairs={{0,8},{8,16},{16,24},{24,28},{28,20},{20,12},{12,4},{4,0},{1,9},{9... | collective-permute-start | bytes 491528 | tf_op jit(solution)/shard_map/ppermute | solution.py:388
  17.1 7.4 %collective-permute-start.8 = (f32[320,128]{1,0:T(8,128)S(1)}, f32[320,128]{1,0:T(8,128)S(1)}, u32[]{:S(2)}, u32[]{:S(2)}) collective-permute-start(f32[320,128]{1,0:T(8,128)S(1)} %collective-permute-done.5.refs_2_), channel_id=1, source_target_pairs={{8,0},{16,8},{24,16},{28,24},{20,28},{12,20},{4,12},{0,4},{9,1},{1... | collective-permute-start | bytes 491528 | tf_op jit(solution)/shard_map/ppermute | solution.py:389
  19.9 0.7 %copy-start.4 = (s32[1,1,256]{2,1,0:T(1,128)S(1)}, s32[1,1,256]{2,1,0:T(1,128)}, u32[]{:S(2)}) copy-start(s32[1,1,256]{2,1,0:T(1,128)} %cells.1) | copy-start | bytes 3076
  22.5 6.5 %collective-permute-start.9 = (f32[320,128]{1,0:T(8,128)S(1)}, f32[320,128]{1,0:T(8,128)S(1)}, u32[]{:S(2)}, u32[]{:S(2)}) collective-permute-start(f32[320,128]{1,0:T(8,128)S(1)} %collective-permute-done.3.refs_7_), channel_id=1, source_target_pairs={{8,0},{16,8},{24,16},{28,24},{20,28},{12,20},{4,12},{0,4},{9,1},{1... | collective-permute-start | bytes 491528 | tf_op jit(solution)/shard_map/ppermute | solution.py:389
  22.5 7.1 %collective-permute-start.10 = (f32[320,128]{1,0:T(8,128)S(1)}, f32[320,128]{1,0:T(8,128)S(1)}, u32[]{:S(2)}, u32[]{:S(2)}) collective-permute-start(f32[320,128]{1,0:T(8,128)S(1)} %collective-permute-done.6.refs_4_), channel_id=1, source_target_pairs={{0,8},{8,16},{16,24},{24,28},{28,20},{20,12},{12,4},{4,0},{1,9},{9... | collective-permute-start | bytes 491528 | tf_op jit(solution)/shard_map/ppermute | solution.py:388
  24.5 7.0 %collective-permute-start.11 = (f32[320,128]{1,0:T(8,128)S(1)}, f32[320,128]{1,0:T(8,128)S(1)}, u32[]{:S(2)}, u32[]{:S(2)}) collective-permute-start(f32[320,128]{1,0:T(8,128)S(1)} %collective-permute-done.7.refs_5_), channel_id=1, source_target_pairs={{0,8},{8,16},{16,24},{24,28},{28,20},{20,12},{12,4},{4,0},{1,9},{9... | collective-permute-start | bytes 491528 | tf_op jit(solution)/shard_map/ppermute | solution.py:388
  24.6 6.9 %collective-permute-start.12 = (f32[320,128]{1,0:T(8,128)S(1)}, f32[320,128]{1,0:T(8,128)S(1)}, u32[]{:S(2)}, u32[]{:S(2)}) collective-permute-start(f32[320,128]{1,0:T(8,128)S(1)} %collective-permute-done.8.refs_6_), channel_id=1, source_target_pairs={{8,0},{16,8},{24,16},{28,24},{20,28},{12,20},{4,12},{0,4},{9,1},{1... | collective-permute-start | bytes 491528 | tf_op jit(solution)/shard_map/ppermute | solution.py:389
  28.9 5.3 %collective-permute-start.14 = (f32[320,128]{1,0:T(8,128)S(1)}, f32[320,128]{1,0:T(8,128)S(1)}, u32[]{:S(2)}, u32[]{:S(2)}) collective-permute-start(f32[320,128]{1,0:T(8,128)S(1)} %collective-permute-done.9.right_second), channel_id=1, source_target_pairs={{8,0},{16,8},{24,16},{28,24},{20,28},{12,20},{4,12},{0,4},{9,1},{1... | collective-permute-start | bytes 491528 | tf_op jit(solution)/shard_map/ppermute | solution.py:448
  29.5 5.3 %collective-permute-start.13 = (f32[320,128]{1,0:T(8,128)S(1)}, f32[320,128]{1,0:T(8,128)S(1)}, u32[]{:S(2)}, u32[]{:S(2)}) collective-permute-start(f32[320,128]{1,0:T(8,128)S(1)} %collective-permute-done.10.left_first), channel_id=1, source_target_pairs={{0,8},{8,16},{16,24},{24,28},{28,20},{20,12},{12,4},{4,0},{1,9},{9... | collective-permute-start | bytes 491528 | tf_op jit(solution)/shard_map/ppermute | solution.py:447
  31.7 3.9 %collective-permute-start.15 = (f32[5,8,128]{2,1,0:T(8,128)S(1)}, f32[5,8,128]{2,1,0:T(8,128)S(1)}, u32[]{:S(2)}, u32[]{:S(2)}) collective-permute-start(f32[5,8,128]{2,1,0:T(8,128)S(1)} %get-tuple-element.61), channel_id=1, source_target_pairs={{0,3},{1,2},{2,1},{3,0},{4,7},{5,6},{6,5},{7,4},{8,11},{9,10},{10,... | collective-permute-start | bytes 61448 | tf_op jit(solution)/shard_map/ppermute | solution.py:460
  31.7 3.8 %collective-permute-start.16 = (f32[5,8,128]{2,1,0:T(8,128)S(1)}, f32[5,8,128]{2,1,0:T(8,128)S(1)}, u32[]{:S(2)}, u32[]{:S(2)}) collective-permute-start(f32[5,8,128]{2,1,0:T(8,128)S(1)} %get-tuple-element.61), channel_id=1, source_target_pairs={{0,1},{1,0},{2,3},{3,2},{4,5},{5,4},{6,7},{7,6},{8,9},{9,8},{10,11... | collective-permute-start | bytes 61448 | tf_op jit(solution)/shard_map/ppermute | solution.py:460

commit v9 on v8

--- a/solution.py
+++ b/solution.py
@@ -138,7 +138,9 @@
 
 
 def slots_body(
+    blocks_x,
     live_count,
+    place_x,
     cells,
     bins,
     slot_weights,
@@ -152,6 +154,7 @@
     edge_column,
     edge_line,
     flow_edges,
+    sides,
 ):
     slots, radial = cells.shape[2], density.shape[1]
     cell, own_bin = cells[0], bins[0]
@@ -182,6 +185,11 @@
     ):
         tiles = [make(pl.ds(at, TILE)) for at in range(0, radial, TILE)]
         flow_edges[which] = packed_edges(tiles)
+    slot = lax.broadcasted_iota(jnp.int32, (TILE, LANES), 1) & (SLOT - 1)
+    paired = (slot < EDGE) == ((place_x[0, 0] & 1) == 1)
+    inner = jnp.where((place_x[0, 0] == 0) | (place_x[0, 0] == blocks_x - 1), 0.0, 1.0)
+    sides[0] = jnp.where(paired, 1.0, 0.0)
+    sides[1] = jnp.where(paired, 0.0, inner)
 
 
 def three_parts(value):
@@ -288,8 +296,7 @@
 
 
 def close_body(
-    blocks_x,
-    place_x,
+    sides,
     edges_next,
     edges_pair,
     flow_edges,
@@ -304,12 +311,9 @@
     fields = fixes.shape[0]
     lane = lax.broadcasted_iota(jnp.int32, (TILE, LANES), 1)
     slot = lane & (SLOT - 1)
-    odd = (place_x[0, 0] & 1) == 1
-    paired = (slot < EDGE) == odd
-    inner = jnp.where((place_x[0, 0] == 0) | (place_x[0, 0] == blocks_x - 1), 0.0, 1.0)
     g = []
     for field in range(fields):
-        halo = jnp.where(paired, edges_pair[field], inner * edges_next[field])
+        halo = sides[0] * edges_pair[field] + sides[1] * edges_next[field]
         total = None
         for k, coef in enumerate(axial_coefs(), 1):
             after = jnp.where(slot + k >= EDGE, pltpu.roll(halo, LANES - k, 1), 0.0)
@@ -377,6 +381,7 @@
     back = [(b, a) for a, b in onward]
 
     across = [(order[i], order[(i + thetas // 2) % thetas]) for i in range(thetas)]
+    place_x = jnp.reshape(lax.axis_index("rx"), (1, 1))
     flat = adjoint.reshape(rows, LANES)
     own = [flat[:half], flat[half:]]
     steps = thetas // 2 - 1
@@ -406,7 +411,7 @@
                 jnp.asarray(ring_weights(thetas)), lax.axis_index("az"), 1, axis=0
             )
             tables = pl.pallas_call(
-                slots_body,
+                functools.partial(slots_body, blocks_x),
                 out_shape=(
                     jax.ShapeDtypeStruct((LANES, slots), jnp.bfloat16),
                     jax.ShapeDtypeStruct((radial, slots), f32),
@@ -415,12 +420,13 @@
                     jax.ShapeDtypeStruct((LANES, slots), jnp.bfloat16),
                     jax.ShapeDtypeStruct((TILE, slots), f32),
                     jax.ShapeDtypeStruct((4, TILE, LANES), f32),
+                    jax.ShapeDtypeStruct((2, TILE, LANES), f32),
                 ),
-                in_specs=in_smem(1) + in_vmem(6),
-                out_specs=tuple(in_vmem(7)),
+                in_specs=in_smem(2) + in_vmem(6),
+                out_specs=tuple(in_vmem(8)),
                 compiler_params=params,
                 name="slots",
-            )(fwh_count, fwh_cell, fwh_bin, fwh_weight, density, velocity, pressure)
+            )(fwh_count, place_x, fwh_cell, fwh_bin, fwh_weight, density, velocity, pressure)
         if step == 1:
             weights, tables, from_right[1] = lax.optimization_barrier(
                 (weights, tables, from_right[1])
@@ -458,9 +464,8 @@
     pairs = [(b, b ^ 1) for b in range(blocks_x)]
     nexts = [(b, (b + (1 if b % 2 else -1)) % blocks_x) for b in range(blocks_x)]
     edges_next, edges_pair = lax.ppermute(edges, "rx", nexts), lax.ppermute(edges, "rx", pairs)
-    place_x = jnp.reshape(lax.axis_index("rx"), (1, 1))
-
-    column, line, owner, place, edge_column, edge_line, flow_edges = tables
+
+    column, line, owner, place, edge_column, edge_line, flow_edges, sides = tables
     held, values = pl.pallas_call(
         bulk_body,
         out_shape=(
@@ -488,14 +493,14 @@
         line,
     )
     fixes, totals = pl.pallas_call(
-        functools.partial(close_body, blocks_x),
+        close_body,
         out_shape=(edge_shape, jax.ShapeDtypeStruct((devices, LANES), f32)),
-        in_specs=in_smem(1) + in_vmem(8),
+        in_specs=in_vmem(9),
         out_specs=tuple(in_vmem(2)),
         compiler_params=params,
         name="close",
     )(
-        place_x,
+        sides,
         edges_next,
         edges_pair,
         flow_edges,

time: 47.5 us -> 47.5 us (level)
  local copies, waits for them, and re-layouts: 1.79 us -> 2.41 us
  waiting for transfers between devices: 7.72 us -> 7.13 us
    unnamed x14, local copies, waits for them, and re-layouts: 0.03 us -> 0.65 us
    ppermute x1, waiting for transfers between devices: 1.69 us -> 1.08 us  [local(): last_edges = lax.ppermute(last_edges, 'az', across)]
where the time goes in v9:
time: 47.5 us; the launch traced here: 47.3 us
  starting transfers between devices  22.7 us (48%)
  blocking collectives  10.4 us (22%)
  waiting for transfers between devices  7.13 us (15%)
  Pallas kernels  3.19 us (7%)
  local copies, waits for them, and re-layouts  2.41 us (5%)
  between operations  1.42 us (3%)
    all_to_all x1, blocking collectives, local(): totals = lax.all_to_all(totals, ('az', 'rx'), 0, 0, tiled=True)  10.4 us
    ppermute x6, starting transfers between devices, local(): right.append(lax.ppermute(from_right[part], 'az', back))  9.34 us
    ppermute x1, starting transfers between devices, local(): last_edges = lax.ppermute(last_edges, 'az', across)  5.02 us
    ppermute x6, starting transfers between devices, local(): left.append(lax.ppermute(from_left[part], 'az', onward))  4.3 us
    ppermute x6, waiting for transfers between devices, local(): right.append(lax.ppermute(from_right[part], 'az', back))  4.28 us
    ppermute x1, starting transfers between devices, local(): last_first = lax.ppermute(from_left[0], 'az', onward)  1.71 us
    ppermute x1, starting transfers between devices, local(): lax.ppermute(edges, 'rx', pairs)  1.62 us
    ppermute x1, waiting for transfers between devices, local(): last_edges = lax.ppermute(last_edges, 'az', across)  1.08 us
  transfers between devices with their start and end apart: 17, of which 6 were waited for; matrix products, arithmetic and copies ran while one was open for 1% of the time, Pallas kernels for 4%

profile of v9, /device:TPU:0, one launch (start us, length us, event | category | flops | bytes accessed | tf_op | source)
XLA Modules:
  0.0 47.3 jit_solution(14105739293240907196)
XLA Ops:
  0.6 1.1 %fusion = (f32[320,128]{1,0:T(8,128)S(1)}, f32[320,128]{1,0:T(8,128)S(1)}) fusion(f32[640,128]{1,0:T(8,128)} %bitcast.6), kind=kLoop, calls=%fused_computation.1 | loop fusion | bytes 655360 | tf_op jit(solution)/shard_map/slice | solution.py:386
  1.7 3.0 %collective-permute-start.2 = (f32[320,128]{1,0:T(8,128)S(1)}, f32[320,128]{1,0:T(8,128)S(1)}, u32[]{:S(2)}, u32[]{:S(2)}) collective-permute-start(f32[320,128]{1,0:T(8,128)S(1)} %get-tuple-element.74), channel_id=1, source_target_pairs={{8,0},{16,8},{24,16},{28,24},{20,28},{12,20},{4,12},{0,4},{9,1},{1... | collective-permute-start | bytes 491528 | tf_op jit(solution)/shard_map/ppermute | solution.py:394
  4.7 0.2 collective-permute-start
  4.9 2.0 %collective-permute-start.4 = (f32[320,128]{1,0:T(8,128)S(1)}, f32[320,128]{1,0:T(8,128)S(1)}, u32[]{:S(2)}, u32[]{:S(2)}) collective-permute-start(f32[320,128]{1,0:T(8,128)S(1)} %get-tuple-element.74), channel_id=1, source_target_pairs={{0,8},{8,16},{16,24},{24,28},{28,20},{20,12},{12,4},{4,0},{1,9},{9... | collective-permute-start | bytes 491528 | tf_op jit(solution)/shard_map/ppermute | solution.py:393
  6.8 0.1 collective-permute-start.5
  6.9 2.6 %collective-permute-done.2.refs_3_ = f32[320,128]{1,0:T(8,128)S(1)} collective-permute-done((f32[320,128]{1,0:T(8,128)S(1)}, f32[320,128]{1,0:T(8,128)S(1)}, u32[]{:S(2)}, u32[]{:S(2)}) %collective-permute-start.2) | collective-permute-done | bytes 163872 | tf_op jit(solution)/shard_map/ppermute | solution.py:394
  9.5 2.3 %collective-permute-start.3 = (f32[320,128]{1,0:T(8,128)S(1)}, f32[320,128]{1,0:T(8,128)S(1)}, u32[]{:S(2)}, u32[]{:S(2)}) collective-permute-start(f32[320,128]{1,0:T(8,128)S(1)} %collective-permute-done.2.refs_3_), channel_id=1, source_target_pairs={{8,0},{16,8},{24,16},{28,24},{20,28},{12,20},{4,12},{0,4},{9,1},{1... | collective-permute-start | bytes 491528 | tf_op jit(solution)/shard_map/ppermute | solution.py:394
  11.8 0.1 collective-permute-start.6
  12.0 0.1 edges.1
  12.1 5.0 %collective-permute-start.1 = (f32[5,8,128]{2,1,0:T(8,128)S(1)}, f32[5,8,128]{2,1,0:T(8,128)S(1)}, u32[]{:S(2)}, u32[]{:S(2)}) collective-permute-start(f32[5,8,128]{2,1,0:T(8,128)S(1)} %edges.1), channel_id=1, source_target_pairs={{0,28},{8,20},{16,12},{24,4},{28,0},{20,8},{12,16},{4,24},{1,29},{... | collective-permute-start | bytes 61448 | tf_op jit(solution)/shard_map/ppermute | solution.py:406
  17.1 2.0 %collective-permute-start.8 = (f32[320,128]{1,0:T(8,128)S(1)}, f32[320,128]{1,0:T(8,128)S(1)}, u32[]{:S(2)}, u32[]{:S(2)}) collective-permute-start(f32[320,128]{1,0:T(8,128)S(1)} %collective-permute-done.5.refs_2_), channel_id=1, source_target_pairs={{8,0},{16,8},{24,16},{28,24},{20,28},{12,20},{4,12},{0,4},{9,1},{1... | collective-permute-start | bytes 491528 | tf_op jit(solution)/shard_map/ppermute | solution.py:394
  19.2 0.7 %constant_dynamic-slice_fusion.weights = f32[1,16]{1,0:T(1,128)S(1)} fusion(f32[8,16]{1,0:T(8,128)} %constant.15.clone, s32[]{:T(128)S(6)} %select_n.3), kind=kLoop, calls=%fused_computation | loop fusion | bytes 132 | tf_op jit(solution)/shard_map/dynamic_slice | solution.py:410
  20.6 0.6 %copy-done.4 = s32[1,1,256]{2,1,0:T(1,128)S(1)} copy-done((s32[1,1,256]{2,1,0:T(1,128)S(1)}, s32[1,1,256]{2,1,0:T(1,128)}, u32[]{:S(2)}) %copy-start.4) | copy-done | bytes 1048
  21.2 0.2 slots.1
  21.4 1.1 %collective-permute-done.1.last_edges = f32[5,8,128]{2,1,0:T(8,128)S(1)} collective-permute-done((f32[5,8,128]{2,1,0:T(8,128)S(1)}, f32[5,8,128]{2,1,0:T(8,128)S(1)}, u32[]{:S(2)}, u32[]{:S(2)}) %collective-permute-start.1) | collective-permute-done | bytes 20512 | tf_op jit(solution)/shard_map/ppermute | solution.py:406
  22.5 2.0 %collective-permute-start.10 = (f32[320,128]{1,0:T(8,128)S(1)}, f32[320,128]{1,0:T(8,128)S(1)}, u32[]{:S(2)}, u32[]{:S(2)}) collective-permute-start(f32[320,128]{1,0:T(8,128)S(1)} %collective-permute-done.6.refs_4_), channel_id=1, source_target_pairs={{0,8},{8,16},{16,24},{24,28},{28,20},{20,12},{12,4},{4,0},{1,9},{9... | collective-permute-start | bytes 491528 | tf_op jit(solution)/shard_map/ppermute | solution.py:393
  24.5 0.1 collective-permute-start.11
  24.6 2.0 %collective-permute-start.12 = (f32[320,128]{1,0:T(8,128)S(1)}, f32[320,128]{1,0:T(8,128)S(1)}, u32[]{:S(2)}, u32[]{:S(2)}) collective-permute-start(f32[320,128]{1,0:T(8,128)S(1)} %collective-permute-done.8.refs_6_), channel_id=1, source_target_pairs={{8,0},{16,8},{24,16},{28,24},{20,28},{12,20},{4,12},{0,4},{9,1},{1... | collective-permute-start | bytes 491528 | tf_op jit(solution)/shard_map/ppermute | solution.py:394
  26.5 0.7 %early.1 = (f32[640,128]{1,0:T(8,128)S(1)}, f32[640,128]{1,0:T(8,128)S(1)}, f32[16,8,128]{2,1,0:T(8,128)S(1)}) custom-call(f32[1,16]{1,0:T(1,128)S(1)} %constant_dynamic-slice_fusion.weights, f32[5,1,128,128]{3,2,1,0:T(8,128)S(1)} %copy-done, f32[320,128]{1,0:T(8,128)S(1)} %collective-permute-done.refs_0_, f32[320,128]{1,0:T(8,128)S(1)} %collective-permute-done.4.refs_1_, ...), custom_call_target="tpu_custom_call" | custom-call | tf_op jit(solution)/shard_map/early/pallas_call | solution.py:441
  27.3 1.7 %collective-permute-done.9.right_second = f32[320,128]{1,0:T(8,128)S(1)} collective-permute-done((f32[320,128]{1,0:T(8,128)S(1)}, f32[320,128]{1,0:T(8,128)S(1)}, u32[]{:S(2)}, u32[]{:S(2)}) %collective-permute-start.9) | collective-permute-done | bytes 163872 | tf_op jit(solution)/shard_map/ppermute | solution.py:394
  28.9 0.6 %collective-permute-start.14 = (f32[320,128]{1,0:T(8,128)S(1)}, f32[320,128]{1,0:T(8,128)S(1)}, u32[]{:S(2)}, u32[]{:S(2)}) collective-permute-start(f32[320,128]{1,0:T(8,128)S(1)} %collective-permute-done.9.right_second), channel_id=1, source_target_pairs={{8,0},{16,8},{24,16},{28,24},{20,28},{12,20},{4,12},{0,4},{9,1},{1... | collective-permute-start | bytes 491528 | tf_op jit(solution)/shard_map/ppermute | solution.py:454
  29.5 1.7 %collective-permute-start.13 = (f32[320,128]{1,0:T(8,128)S(1)}, f32[320,128]{1,0:T(8,128)S(1)}, u32[]{:S(2)}, u32[]{:S(2)}) collective-permute-start(f32[320,128]{1,0:T(8,128)S(1)} %collective-permute-done.10.left_first), channel_id=1, source_target_pairs={{0,8},{8,16},{16,24},{24,28},{28,20},{20,12},{12,4},{4,0},{1,9},{9... | collective-permute-start | bytes 491528 | tf_op jit(solution)/shard_map/ppermute | solution.py:453
  31.3 0.2 collective-permute-done.11.left_second
  31.5 0.2 partial.1
  31.7 0.1 collective-permute-start.15
  31.7 1.6 %collective-permute-start.16 = (f32[5,8,128]{2,1,0:T(8,128)S(1)}, f32[5,8,128]{2,1,0:T(8,128)S(1)}, u32[]{:S(2)}, u32[]{:S(2)}) collective-permute-start(f32[5,8,128]{2,1,0:T(8,128)S(1)} %get-tuple-element.65), channel_id=1, source_target_pairs={{0,1},{1,0},{2,3},{3,2},{4,5},{5,4},{6,7},{7,6},{8,9},{9,8},{10,11... | collective-permute-start | bytes 61448 | tf_op jit(solution)/shard_map/ppermute | solution.py:466
  33.4 0.9 %collective-permute-done.14.last_second = f32[320,128]{1,0:T(8,128)S(1)} collective-permute-done((f32[320,128]{1,0:T(8,128)S(1)}, f32[320,128]{1,0:T(8,128)S(1)}, u32[]{:S(2)}, u32[]{:S(2)}) %collective-permute-start.14) | collective-permute-done | bytes 163872 | tf_op jit(solution)/shard_map/ppermute | solution.py:454
  34.2 0.6 %collective-permute-done.13.last_first = f32[320,128]{1,0:T(8,128)S(1)} collective-permute-done((f32[320,128]{1,0:T(8,128)S(1)}, f32[320,128]{1,0:T(8,128)S(1)}, u32[]{:S(2)}, u32[]{:S(2)}) %collective-permute-start.13) | collective-permute-done | bytes 163872 | tf_op jit(solution)/shard_map/ppermute | solution.py:453
  34.9 0.7 %bulk.1 = (f32[5,1,128,128]{3,2,1,0:T(8,128)S(1)}, f32[1,256]{1,0:T(1,128)S(1)}) custom-call(f32[16,8,128]{2,1,0:T(8,128)S(1)} %get-tuple-element.54.weights, f32[640,128]{1,0:T(8,128)S(1)} %get-tuple-element.59.smooth, f32[640,128]{1,0:T(8,128)S(1)} %get-tuple-element.60.slope, f32[320,128]{1,0:T(8,128)S(1)} %collective-permute-done.13.last_first, ...), custom_call_target="tpu_custom_call" | custom-call | tf_op jit(solution)/shard_map/bulk/pallas_call | solution.py:469
  35.6 0.4 close.1
  35.9 10.4 %all_to_all.11 = f32[32,1,128]{2,1,0:T(1,128)S(1)} all-to-all(f32[32,1,128]{2,1,0:T(1,128)S(1)} %bitcast.8), channel_id=1, replica_groups=mesh['az'=8,'rx'=4] {'az','rx'}, dimensions={0} | all-to-all | bytes 32768 | tf_op jit(solution)/shard_map/all_to_all | solution.py:513
  46.4 0.9 %store.1 = (f32[5,1,128,128]{3,2,1,0:T(8,128)}, f32[8]{0:T(128)}) custom-call(f32[5,1,128,128]{3,2,1,0:T(8,128)S(1)} %get-tuple-element.63.held, f32[5,8,128]{2,1,0:T(8,128)S(1)} %get-tuple-element.72.fixes, f32[32,128]{1,0:T(8,128)S(1)} %bitcast.7), custom_call_target="tpu_custom_call" | custom-call | tf_op jit(solution)/shard_map/store/pallas_call | solution.py:514
  (26 shorter events, 0.1 us)
Async XLA Ops:
  0.6 11.3 %copy-start = (f32[5,1,128,128]{3,2,1,0:T(8,128)S(1)}, f32[5,1,128,128]{3,2,1,0:T(8,128)}, u32[]{:S(2)}) copy-start(f32[5,1,128,128]{3,2,1,0:T(8,128)} %source.2) | copy-start | bytes 983044
  1.7 18.8 %copy-start.1 = (f32[3,1,128,128]{3,2,1,0:T(8,128)S(1)}, f32[3,1,128,128]{3,2,1,0:T(8,128)}, u32[]{:S(2)}) copy-start(f32[3,1,128,128]{3,2,1,0:T(8,128)} %velocity.3) | copy-start | bytes 589828
  1.7 7.8 %collective-permute-start.2 = (f32[320,128]{1,0:T(8,128)S(1)}, f32[320,128]{1,0:T(8,128)S(1)}, u32[]{:S(2)}, u32[]{:S(2)}) collective-permute-start(f32[320,128]{1,0:T(8,128)S(1)} %get-tuple-element.74), channel_id=1, source_target_pairs={{8,0},{16,8},{24,16},{28,24},{20,28},{12,20},{4,12},{0,4},{9,1},{1... | collective-permute-start | bytes 491528 | tf_op jit(solution)/shard_map/ppermute | solution.py:394
  4.7 7.1 %collective-permute-start = (f32[320,128]{1,0:T(8,128)S(1)}, f32[320,128]{1,0:T(8,128)S(1)}, u32[]{:S(2)}, u32[]{:S(2)}) collective-permute-start(f32[320,128]{1,0:T(8,128)S(1)} %get-tuple-element.75), channel_id=1, source_target_pairs={{0,8},{8,16},{16,24},{24,28},{28,20},{20,12},{12,4},{4,0},{1,9},{9... | collective-permute-start | bytes 491528 | tf_op jit(solution)/shard_map/ppermute | solution.py:393
  4.9 12.3 %collective-permute-start.4 = (f32[320,128]{1,0:T(8,128)S(1)}, f32[320,128]{1,0:T(8,128)S(1)}, u32[]{:S(2)}, u32[]{:S(2)}) collective-permute-start(f32[320,128]{1,0:T(8,128)S(1)} %get-tuple-element.74), channel_id=1, source_target_pairs={{0,8},{8,16},{16,24},{24,28},{28,20},{20,12},{12,4},{4,0},{1,9},{9... | collective-permute-start | bytes 491528 | tf_op jit(solution)/shard_map/ppermute | solution.py:393
  6.8 10.3 %collective-permute-start.5 = (f32[320,128]{1,0:T(8,128)S(1)}, f32[320,128]{1,0:T(8,128)S(1)}, u32[]{:S(2)}, u32[]{:S(2)}) collective-permute-start(f32[320,128]{1,0:T(8,128)S(1)} %get-tuple-element.75), channel_id=1, source_target_pairs={{8,0},{16,8},{24,16},{28,24},{20,28},{12,20},{4,12},{0,4},{9,1},{1... | collective-permute-start | bytes 491528 | tf_op jit(solution)/shard_map/ppermute | solution.py:394
  9.5 12.9 %collective-permute-start.3 = (f32[320,128]{1,0:T(8,128)S(1)}, f32[320,128]{1,0:T(8,128)S(1)}, u32[]{:S(2)}, u32[]{:S(2)}) collective-permute-start(f32[320,128]{1,0:T(8,128)S(1)} %collective-permute-done.2.refs_3_), channel_id=1, source_target_pairs={{8,0},{16,8},{24,16},{28,24},{20,28},{12,20},{4,12},{0,4},{9,1},{1... | collective-permute-start | bytes 491528 | tf_op jit(solution)/shard_map/ppermute | solution.py:394
  11.8 10.6 %collective-permute-start.6 = (f32[320,128]{1,0:T(8,128)S(1)}, f32[320,128]{1,0:T(8,128)S(1)}, u32[]{:S(2)}, u32[]{:S(2)}) collective-permute-start(f32[320,128]{1,0:T(8,128)S(1)} %collective-permute-done.refs_0_), channel_id=1, source_target_pairs={{0,8},{8,16},{16,24},{24,28},{28,20},{20,12},{12,4},{4,0},{1,9},{9... | collective-permute-start | bytes 491528 | tf_op jit(solution)/shard_map/ppermute | solution.py:393
  11.9 8.6 %copy-start.2 = (f32[1,128,128]{2,1,0:T(8,128)S(1)}, f32[1,128,128]{2,1,0:T(8,128)}, u32[]{:S(2)}) copy-start(f32[1,128,128]{2,1,0:T(8,128)} %density.3) | copy-start | bytes 196612
  12.0 8.6 %copy-start.3 = (f32[1,128,128]{2,1,0:T(8,128)S(1)}, f32[1,128,128]{2,1,0:T(8,128)}, u32[]{:S(2)}) copy-start(f32[1,128,128]{2,1,0:T(8,128)} %pressure.3) | copy-start | bytes 196612
  12.0 8.6 %copy-start.5 = (s32[1,1,256]{2,1,0:T(1,128)S(1)}, s32[1,1,256]{2,1,0:T(1,128)}, u32[]{:S(2)}) copy-start(s32[1,1,256]{2,1,0:T(1,128)} %bins.1) | copy-start | bytes 3076
  12.0 8.6 %copy-start.6 = (f32[1,1,256]{2,1,0:T(1,128)S(1)}, f32[1,1,256]{2,1,0:T(1,128)}, u32[]{:S(2)}) copy-start(f32[1,1,256]{2,1,0:T(1,128)} %slot_weights.1) | copy-start | bytes 3076
  12.1 10.3 %collective-permute-start.1 = (f32[5,8,128]{2,1,0:T(8,128)S(1)}, f32[5,8,128]{2,1,0:T(8,128)S(1)}, u32[]{:S(2)}, u32[]{:S(2)}) collective-permute-start(f32[5,8,128]{2,1,0:T(8,128)S(1)} %edges.1), channel_id=1, source_target_pairs={{0,28},{8,20},{16,12},{24,4},{28,0},{20,8},{12,16},{4,24},{1,29},{... | collective-permute-start | bytes 61448 | tf_op jit(solution)/shard_map/ppermute | solution.py:406
  17.1 7.4 %collective-permute-start.7 = (f32[320,128]{1,0:T(8,128)S(1)}, f32[320,128]{1,0:T(8,128)S(1)}, u32[]{:S(2)}, u32[]{:S(2)}) collective-permute-start(f32[320,128]{1,0:T(8,128)S(1)} %collective-permute-done.4.refs_1_), channel_id=1, source_target_pairs={{0,8},{8,16},{16,24},{24,28},{28,20},{20,12},{12,4},{4,0},{1,9},{9... | collective-permute-start | bytes 491528 | tf_op jit(solution)/shard_map/ppermute | solution.py:393
  17.1 7.4 %collective-permute-start.8 = (f32[320,128]{1,0:T(8,128)S(1)}, f32[320,128]{1,0:T(8,128)S(1)}, u32[]{:S(2)}, u32[]{:S(2)}) collective-permute-start(f32[320,128]{1,0:T(8,128)S(1)} %collective-permute-done.5.refs_2_), channel_id=1, source_target_pairs={{8,0},{16,8},{24,16},{28,24},{20,28},{12,20},{4,12},{0,4},{9,1},{1... | collective-permute-start | bytes 491528 | tf_op jit(solution)/shard_map/ppermute | solution.py:394
  20.5 0.7 %copy-start.4 = (s32[1,1,256]{2,1,0:T(1,128)S(1)}, s32[1,1,256]{2,1,0:T(1,128)}, u32[]{:S(2)}) copy-start(s32[1,1,256]{2,1,0:T(1,128)} %cells.1) | copy-start | bytes 3076
  22.5 6.5 %collective-permute-start.9 = (f32[320,128]{1,0:T(8,128)S(1)}, f32[320,128]{1,0:T(8,128)S(1)}, u32[]{:S(2)}, u32[]{:S(2)}) collective-permute-start(f32[320,128]{1,0:T(8,128)S(1)} %collective-permute-done.3.refs_7_), channel_id=1, source_target_pairs={{8,0},{16,8},{24,16},{28,24},{20,28},{12,20},{4,12},{0,4},{9,1},{1... | collective-permute-start | bytes 491528 | tf_op jit(solution)/shard_map/ppermute | solution.py:394
  22.5 7.1 %collective-permute-start.10 = (f32[320,128]{1,0:T(8,128)S(1)}, f32[320,128]{1,0:T(8,128)S(1)}, u32[]{:S(2)}, u32[]{:S(2)}) collective-permute-start(f32[320,128]{1,0:T(8,128)S(1)} %collective-permute-done.6.refs_4_), channel_id=1, source_target_pairs={{0,8},{8,16},{16,24},{24,28},{28,20},{20,12},{12,4},{4,0},{1,9},{9... | collective-permute-start | bytes 491528 | tf_op jit(solution)/shard_map/ppermute | solution.py:393
  24.5 7.0 %collective-permute-start.11 = (f32[320,128]{1,0:T(8,128)S(1)}, f32[320,128]{1,0:T(8,128)S(1)}, u32[]{:S(2)}, u32[]{:S(2)}) collective-permute-start(f32[320,128]{1,0:T(8,128)S(1)} %collective-permute-done.7.refs_5_), channel_id=1, source_target_pairs={{0,8},{8,16},{16,24},{24,28},{28,20},{20,12},{12,4},{4,0},{1,9},{9... | collective-permute-start | bytes 491528 | tf_op jit(solution)/shard_map/ppermute | solution.py:393
  24.6 6.9 %collective-permute-start.12 = (f32[320,128]{1,0:T(8,128)S(1)}, f32[320,128]{1,0:T(8,128)S(1)}, u32[]{:S(2)}, u32[]{:S(2)}) collective-permute-start(f32[320,128]{1,0:T(8,128)S(1)} %collective-permute-done.8.refs_6_), channel_id=1, source_target_pairs={{8,0},{16,8},{24,16},{28,24},{20,28},{12,20},{4,12},{0,4},{9,1},{1... | collective-permute-start | bytes 491528 | tf_op jit(solution)/shard_map/ppermute | solution.py:394
  28.9 5.3 %collective-permute-start.14 = (f32[320,128]{1,0:T(8,128)S(1)}, f32[320,128]{1,0:T(8,128)S(1)}, u32[]{:S(2)}, u32[]{:S(2)}) collective-permute-start(f32[320,128]{1,0:T(8,128)S(1)} %collective-permute-done.9.right_second), channel_id=1, source_target_pairs={{8,0},{16,8},{24,16},{28,24},{20,28},{12,20},{4,12},{0,4},{9,1},{1... | collective-permute-start | bytes 491528 | tf_op jit(solution)/shard_map/ppermute | solution.py:454
  29.5 5.3 %collective-permute-start.13 = (f32[320,128]{1,0:T(8,128)S(1)}, f32[320,128]{1,0:T(8,128)S(1)}, u32[]{:S(2)}, u32[]{:S(2)}) collective-permute-start(f32[320,128]{1,0:T(8,128)S(1)} %collective-permute-done.10.left_first), channel_id=1, source_target_pairs={{0,8},{8,16},{16,24},{24,28},{28,20},{20,12},{12,4},{4,0},{1,9},{9... | collective-permute-start | bytes 491528 | tf_op jit(solution)/shard_map/ppermute | solution.py:453
  31.7 3.9 %collective-permute-start.15 = (f32[5,8,128]{2,1,0:T(8,128)S(1)}, f32[5,8,128]{2,1,0:T(8,128)S(1)}, u32[]{:S(2)}, u32[]{:S(2)}) collective-permute-start(f32[5,8,128]{2,1,0:T(8,128)S(1)} %get-tuple-element.65), channel_id=1, source_target_pairs={{0,3},{1,2},{2,1},{3,0},{4,7},{5,6},{6,5},{7,4},{8,11},{9,10},{10,... | collective-permute-start | bytes 61448 | tf_op jit(solution)/shard_map/ppermute | solution.py:466
  31.7 3.9 %collective-permute-start.16 = (f32[5,8,128]{2,1,0:T(8,128)S(1)}, f32[5,8,128]{2,1,0:T(8,128)S(1)}, u32[]{:S(2)}, u32[]{:S(2)}) collective-permute-start(f32[5,8,128]{2,1,0:T(8,128)S(1)} %get-tuple-element.65), channel_id=1, source_target_pairs={{0,1},{1,0},{2,3},{3,2},{4,5},{5,4},{6,7},{7,6},{8,9},{9,8},{10,11... | collective-permute-start | bytes 61448 | tf_op jit(solution)/shard_map/ppermute | solution.py:466

commit v10 on v9

--- a/solution.py
+++ b/solution.py
@@ -80,31 +80,30 @@
     return packed
 
 
-def edges_body(source, edges):
-    fields, radial = source.shape[0], source.shape[2]
+def edges_body(first, second, edges):
+    fields, half = edges.shape[0], first.shape[0]
+    radial = 2 * half // fields
     for field in range(fields):
-        tiles = [source[field, 0, pl.ds(row, TILE), :] for row in range(0, radial, TILE)]
+        places = range(field * radial, (field + 1) * radial, TILE)
+        tiles = [(first if at < half else second)[pl.ds(at % half, TILE), :] for at in places]
         edges[field] = packed_edges(tiles)
 
 
-def early_body(weights, source, *refs):
+def early_body(weights, *refs):
     count = weights.shape[1] // 2
     halves, (smooth, slope, spread) = refs[:-3], refs[-3:]
     for k in range(2 * count):
         spread[k] = jnp.full((TILE, LANES), weights[0, k], jnp.float32)
-    fields, radial = source.shape[0], source.shape[2]
     half = halves[0].shape[0]
-    for field in range(fields):
-        for row in range(0, radial, TILE):
-            at = field * radial + row
-            value = source[field, 0, pl.ds(row, TILE), :]
-            first, second = weights[0, 0] * value, weights[0, count] * value
-            for k in range(len(halves) // 2):
-                value = halves[2 * k + at // half][pl.ds(at % half, TILE), :]
-                first = first + weights[0, 1 + k] * value
-                second = second + weights[0, count + 1 + k] * value
-            smooth[pl.ds(at, TILE), :] = first
-            slope[pl.ds(at, TILE), :] = second
+    for at in range(0, 2 * half, TILE):
+        first = second = None
+        for k in range(len(halves) // 2):
+            value = halves[2 * k + at // half][pl.ds(at % half, TILE), :]
+            terms = weights[0, k] * value, weights[0, count + k] * value
+            first = terms[0] if first is None else first + terms[0]
+            second = terms[1] if second is None else second + terms[1]
+        smooth[pl.ds(at, TILE), :] = first
+        slope[pl.ds(at, TILE), :] = second
 
 
 def partial_body(
@@ -394,15 +393,15 @@
             right.append(lax.ppermute(from_right[part], "az", back))
         from_left, from_right = left, right
         if step == 0:
-            source, from_left[0] = lax.optimization_barrier((adjoint, from_left[0]))
+            source, from_left[0] = lax.optimization_barrier((own[1], from_left[0]))
             last_edges = pl.pallas_call(
                 edges_body,
                 out_shape=edge_shape,
-                in_specs=in_vmem(1),
+                in_specs=in_vmem(2),
                 out_specs=in_vmem(1)[0],
                 compiler_params=params,
                 name="edges",
-            )(source)
+            )(own[0], source)
             last_edges = lax.ppermute(last_edges, "az", across)
         if step == 0 + 1:
             last_edges, from_right[1] = lax.optimization_barrier((last_edges, from_right[1]))
@@ -445,11 +444,11 @@
                     jax.ShapeDtypeStruct((rows, LANES), f32),
                     jax.ShapeDtypeStruct((2 * thetas, TILE, LANES), f32),
                 ),
-                in_specs=in_smem(1) + in_vmem(1 + len(halves)),
+                in_specs=in_smem(1) + in_vmem(2 + len(halves)),
                 out_specs=tuple(in_vmem(3)),
                 compiler_params=params,
                 name="early",
-            )(weights, adjoint, *halves)
+            )(weights, *own, *halves)
     last_first = lax.ppermute(from_left[0], "az", onward)
     last_second = lax.ppermute(from_right[1], "az", back)
 

time: 47.5 us -> 47.4 us (level)
  no operation moved by 1% of the time
where the time goes in v10:
time: 47.4 us; the launch traced here: 47.2 us
  starting transfers between devices  22.7 us (48%)
  blocking collectives  10.4 us (22%)
  waiting for transfers between devices  7.13 us (15%)
  Pallas kernels  3.19 us (7%)
  local copies, waits for them, and re-layouts  2.35 us (5%)
  between operations  1.41 us (3%)
    all_to_all x1, blocking collectives, local(): totals = lax.all_to_all(totals, ('az', 'rx'), 0, 0, tiled=True)  10.4 us
    ppermute x6, starting transfers between devices, local(): right.append(lax.ppermute(from_right[part], 'az', back))  9.34 us
    ppermute x1, starting transfers between devices, local(): last_edges = lax.ppermute(last_edges, 'az', across)  5.02 us
    ppermute x6, starting transfers between devices, local(): left.append(lax.ppermute(from_left[part], 'az', onward))  4.3 us
    ppermute x6, waiting for transfers between devices, local(): right.append(lax.ppermute(from_right[part], 'az', back))  4.28 us
    ppermute x1, starting transfers between devices, local(): last_first = lax.ppermute(from_left[0], 'az', onward)  1.72 us
    ppermute x1, starting transfers between devices, local(): lax.ppermute(edges, 'rx', pairs)  1.62 us
    ppermute x1, waiting for transfers between devices, local(): last_edges = lax.ppermute(last_edges, 'az', across)  1.09 us
  transfers between devices with their start and end apart: 17, of which 6 were waited for; matrix products, arithmetic and copies ran while one was open for 1% of the time, Pallas kernels for 4%

profile of v10, /device:TPU:0, one launch (start us, length us, event | category | flops | bytes accessed | tf_op | source)
XLA Modules:
  0.0 47.2 jit_solution(6497816592565277599)
XLA Ops:
  0.6 1.0 %fusion = (f32[320,128]{1,0:T(8,128)S(1)}, f32[320,128]{1,0:T(8,128)S(1)}) fusion(f32[640,128]{1,0:T(8,128)} %bitcast.8), kind=kLoop, calls=%fused_computation.1 | loop fusion | bytes 655360 | tf_op jit(solution)/shard_map/slice | solution.py:385
  1.7 3.0 %collective-permute-start.2 = (f32[320,128]{1,0:T(8,128)S(1)}, f32[320,128]{1,0:T(8,128)S(1)}, u32[]{:S(2)}, u32[]{:S(2)}) collective-permute-start(f32[320,128]{1,0:T(8,128)S(1)} %get-tuple-element.46.second.refs_1_), channel_id=1, source_target_pairs={{8,0},{16,8},{24,16},{28,24},{20,28},{12,20},{4,12},{0,4},{9,1},{1... | collective-permute-start | bytes 491528 | tf_op jit(solution)/shard_map/ppermute | solution.py:393
  4.7 0.2 collective-permute-start
  4.8 2.0 %collective-permute-start.4 = (f32[320,128]{1,0:T(8,128)S(1)}, f32[320,128]{1,0:T(8,128)S(1)}, u32[]{:S(2)}, u32[]{:S(2)}) collective-permute-start(f32[320,128]{1,0:T(8,128)S(1)} %get-tuple-element.46.second.refs_1_), channel_id=1, source_target_pairs={{0,8},{8,16},{16,24},{24,28},{28,20},{20,12},{12,4},{4,0},{1,9},{9... | collective-permute-start | bytes 491528 | tf_op jit(solution)/shard_map/ppermute | solution.py:392
  6.8 0.1 collective-permute-start.5
  6.8 2.6 %collective-permute-done.2.refs_5_ = f32[320,128]{1,0:T(8,128)S(1)} collective-permute-done((f32[320,128]{1,0:T(8,128)S(1)}, f32[320,128]{1,0:T(8,128)S(1)}, u32[]{:S(2)}, u32[]{:S(2)}) %collective-permute-start.2) | collective-permute-done | bytes 163872 | tf_op jit(solution)/shard_map/ppermute | solution.py:393
  9.5 2.3 %collective-permute-start.3 = (f32[320,128]{1,0:T(8,128)S(1)}, f32[320,128]{1,0:T(8,128)S(1)}, u32[]{:S(2)}, u32[]{:S(2)}) collective-permute-start(f32[320,128]{1,0:T(8,128)S(1)} %collective-permute-done.2.refs_5_), channel_id=1, source_target_pairs={{8,0},{16,8},{24,16},{28,24},{20,28},{12,20},{4,12},{0,4},{9,1},{1... | collective-permute-start | bytes 491528 | tf_op jit(solution)/shard_map/ppermute | solution.py:393
  11.8 0.1 collective-permute-start.6
  11.9 0.1 edges.1
  12.1 5.0 %collective-permute-start.1 = (f32[5,8,128]{2,1,0:T(8,128)S(1)}, f32[5,8,128]{2,1,0:T(8,128)S(1)}, u32[]{:S(2)}, u32[]{:S(2)}) collective-permute-start(f32[5,8,128]{2,1,0:T(8,128)S(1)} %edges.1), channel_id=1, source_target_pairs={{0,28},{8,20},{16,12},{24,4},{28,0},{20,8},{12,16},{4,24},{1,29},{... | collective-permute-start | bytes 61448 | tf_op jit(solution)/shard_map/ppermute | solution.py:405
  17.1 2.0 %collective-permute-start.8 = (f32[320,128]{1,0:T(8,128)S(1)}, f32[320,128]{1,0:T(8,128)S(1)}, u32[]{:S(2)}, u32[]{:S(2)}) collective-permute-start(f32[320,128]{1,0:T(8,128)S(1)} %collective-permute-done.5.refs_4_), channel_id=1, source_target_pairs={{8,0},{16,8},{24,16},{28,24},{20,28},{12,20},{4,12},{0,4},{9,1},{1... | collective-permute-start | bytes 491528 | tf_op jit(solution)/shard_map/ppermute | solution.py:393
  19.1 0.7 %constant_dynamic-slice_fusion.weights = f32[1,16]{1,0:T(1,128)S(1)} fusion(f32[8,16]{1,0:T(8,128)} %constant.15.clone, s32[]{:T(128)S(6)} %select_n.3), kind=kLoop, calls=%fused_computation | loop fusion | bytes 132 | tf_op jit(solution)/shard_map/dynamic_slice | solution.py:409
  20.5 0.6 %copy-done.3 = s32[1,1,256]{2,1,0:T(1,128)S(1)} copy-done((s32[1,1,256]{2,1,0:T(1,128)S(1)}, s32[1,1,256]{2,1,0:T(1,128)}, u32[]{:S(2)}) %copy-start.3) | copy-done | bytes 1048
  21.1 0.2 slots.1
  21.3 1.1 %collective-permute-done.1.last_edges = f32[5,8,128]{2,1,0:T(8,128)S(1)} collective-permute-done((f32[5,8,128]{2,1,0:T(8,128)S(1)}, f32[5,8,128]{2,1,0:T(8,128)S(1)}, u32[]{:S(2)}, u32[]{:S(2)}) %collective-permute-start.1) | collective-permute-done | bytes 20512 | tf_op jit(solution)/shard_map/ppermute | solution.py:405
  22.4 2.0 %collective-permute-start.10 = (f32[320,128]{1,0:T(8,128)S(1)}, f32[320,128]{1,0:T(8,128)S(1)}, u32[]{:S(2)}, u32[]{:S(2)}) collective-permute-start(f32[320,128]{1,0:T(8,128)S(1)} %collective-permute-done.6.refs_6_), channel_id=1, source_target_pairs={{0,8},{8,16},{16,24},{24,28},{28,20},{20,12},{12,4},{4,0},{1,9},{9... | collective-permute-start | bytes 491528 | tf_op jit(solution)/shard_map/ppermute | solution.py:392
  24.4 0.1 collective-permute-start.11
  24.5 2.0 %collective-permute-start.12 = (f32[320,128]{1,0:T(8,128)S(1)}, f32[320,128]{1,0:T(8,128)S(1)}, u32[]{:S(2)}, u32[]{:S(2)}) collective-permute-start(f32[320,128]{1,0:T(8,128)S(1)} %collective-permute-done.8.refs_8_), channel_id=1, source_target_pairs={{8,0},{16,8},{24,16},{28,24},{20,28},{12,20},{4,12},{0,4},{9,1},{1... | collective-permute-start | bytes 491528 | tf_op jit(solution)/shard_map/ppermute | solution.py:393
  26.5 0.7 %early.1 = (f32[640,128]{1,0:T(8,128)S(1)}, f32[640,128]{1,0:T(8,128)S(1)}, f32[16,8,128]{2,1,0:T(8,128)S(1)}) custom-call(f32[1,16]{1,0:T(1,128)S(1)} %constant_dynamic-slice_fusion.weights, f32[320,128]{1,0:T(8,128)S(1)} %get-tuple-element.75.first.refs_0_, f32[320,128]{1,0:T(8,128)S(1)} %get-tuple-element.46.second.refs_1_, ...), custom_call_target="tpu_custom_call" | custom-call | tf_op jit(solution)/shard_map/early/pallas_call | solution.py:440
  27.2 1.6 %collective-permute-done.9.right_second = f32[320,128]{1,0:T(8,128)S(1)} collective-permute-done((f32[320,128]{1,0:T(8,128)S(1)}, f32[320,128]{1,0:T(8,128)S(1)}, u32[]{:S(2)}, u32[]{:S(2)}) %collective-permute-start.9) | collective-permute-done | bytes 163872 | tf_op jit(solution)/shard_map/ppermute | solution.py:393
  28.9 0.6 %collective-permute-start.14 = (f32[320,128]{1,0:T(8,128)S(1)}, f32[320,128]{1,0:T(8,128)S(1)}, u32[]{:S(2)}, u32[]{:S(2)}) collective-permute-start(f32[320,128]{1,0:T(8,128)S(1)} %collective-permute-done.9.right_second), channel_id=1, source_target_pairs={{8,0},{16,8},{24,16},{28,24},{20,28},{12,20},{4,12},{0,4},{9,1},{1... | collective-permute-start | bytes 491528 | tf_op jit(solution)/shard_map/ppermute | solution.py:453
  29.5 1.7 %collective-permute-start.13 = (f32[320,128]{1,0:T(8,128)S(1)}, f32[320,128]{1,0:T(8,128)S(1)}, u32[]{:S(2)}, u32[]{:S(2)}) collective-permute-start(f32[320,128]{1,0:T(8,128)S(1)} %collective-permute-done.10.left_first), channel_id=1, source_target_pairs={{0,8},{8,16},{16,24},{24,28},{28,20},{20,12},{12,4},{4,0},{1,9},{9... | collective-permute-start | bytes 491528 | tf_op jit(solution)/shard_map/ppermute | solution.py:452
  31.2 0.2 collective-permute-done.11.left_second
  31.4 0.2 partial.1
  31.6 0.1 collective-permute-start.15
  31.7 1.6 %collective-permute-start.16 = (f32[5,8,128]{2,1,0:T(8,128)S(1)}, f32[5,8,128]{2,1,0:T(8,128)S(1)}, u32[]{:S(2)}, u32[]{:S(2)}) collective-permute-start(f32[5,8,128]{2,1,0:T(8,128)S(1)} %get-tuple-element.65), channel_id=1, source_target_pairs={{0,1},{1,0},{2,3},{3,2},{4,5},{5,4},{6,7},{7,6},{8,9},{9,8},{10,11... | collective-permute-start | bytes 61448 | tf_op jit(solution)/shard_map/ppermute | solution.py:465
  33.3 0.9 %collective-permute-done.14.last_second = f32[320,128]{1,0:T(8,128)S(1)} collective-permute-done((f32[320,128]{1,0:T(8,128)S(1)}, f32[320,128]{1,0:T(8,128)S(1)}, u32[]{:S(2)}, u32[]{:S(2)}) %collective-permute-start.14) | collective-permute-done | bytes 163872 | tf_op jit(solution)/shard_map/ppermute | solution.py:453
  34.2 0.6 %collective-permute-done.13.last_first = f32[320,128]{1,0:T(8,128)S(1)} collective-permute-done((f32[320,128]{1,0:T(8,128)S(1)}, f32[320,128]{1,0:T(8,128)S(1)}, u32[]{:S(2)}, u32[]{:S(2)}) %collective-permute-start.13) | collective-permute-done | bytes 163872 | tf_op jit(solution)/shard_map/ppermute | solution.py:452
  34.8 0.7 %bulk.1 = (f32[5,1,128,128]{3,2,1,0:T(8,128)S(1)}, f32[1,256]{1,0:T(1,128)S(1)}) custom-call(f32[16,8,128]{2,1,0:T(8,128)S(1)} %get-tuple-element.54.weights, f32[640,128]{1,0:T(8,128)S(1)} %get-tuple-element.59.smooth, f32[640,128]{1,0:T(8,128)S(1)} %get-tuple-element.60.slope, f32[320,128]{1,0:T(8,128)S(1)} %collective-permute-done.13.last_first, ...), custom_call_target="tpu_custom_call" | custom-call | tf_op jit(solution)/shard_map/bulk/pallas_call | solution.py:468
  35.5 0.4 close.1
  35.9 10.4 %all_to_all.11 = f32[32,1,128]{2,1,0:T(1,128)S(1)} all-to-all(f32[32,1,128]{2,1,0:T(1,128)S(1)} %bitcast.7), channel_id=1, replica_groups=mesh['az'=8,'rx'=4] {'az','rx'}, dimensions={0} | all-to-all | bytes 32768 | tf_op jit(solution)/shard_map/all_to_all | solution.py:512
  46.3 0.9 %store.1 = (f32[5,1,128,128]{3,2,1,0:T(8,128)}, f32[8]{0:T(128)}) custom-call(f32[5,1,128,128]{3,2,1,0:T(8,128)S(1)} %get-tuple-element.63.held, f32[5,8,128]{2,1,0:T(8,128)S(1)} %get-tuple-element.72.fixes, f32[32,128]{1,0:T(8,128)S(1)} %bitcast.6), custom_call_target="tpu_custom_call" | custom-call | tf_op jit(solution)/shard_map/store/pallas_call | solution.py:513
  (24 shorter events, 0.1 us)
Async XLA Ops:
  1.6 18.8 %copy-start = (f32[3,1,128,128]{3,2,1,0:T(8,128)S(1)}, f32[3,1,128,128]{3,2,1,0:T(8,128)}, u32[]{:S(2)}) copy-start(f32[3,1,128,128]{3,2,1,0:T(8,128)} %velocity.3) | copy-start | bytes 589828
  1.7 7.8 %collective-permute-start.2 = (f32[320,128]{1,0:T(8,128)S(1)}, f32[320,128]{1,0:T(8,128)S(1)}, u32[]{:S(2)}, u32[]{:S(2)}) collective-permute-start(f32[320,128]{1,0:T(8,128)S(1)} %get-tuple-element.46.second.refs_1_), channel_id=1, source_target_pairs={{8,0},{16,8},{24,16},{28,24},{20,28},{12,20},{4,12},{0,4},{9,1},{1... | collective-permute-start | bytes 491528 | tf_op jit(solution)/shard_map/ppermute | solution.py:393
  4.7 7.1 %collective-permute-start = (f32[320,128]{1,0:T(8,128)S(1)}, f32[320,128]{1,0:T(8,128)S(1)}, u32[]{:S(2)}, u32[]{:S(2)}) collective-permute-start(f32[320,128]{1,0:T(8,128)S(1)} %get-tuple-element.75.first.refs_0_), channel_id=1, source_target_pairs={{0,8},{8,16},{16,24},{24,28},{28,20},{20,12},{12,4},{4,0},{1,9},{9... | collective-permute-start | bytes 491528 | tf_op jit(solution)/shard_map/ppermute | solution.py:392
  4.8 12.3 %collective-permute-start.4 = (f32[320,128]{1,0:T(8,128)S(1)}, f32[320,128]{1,0:T(8,128)S(1)}, u32[]{:S(2)}, u32[]{:S(2)}) collective-permute-start(f32[320,128]{1,0:T(8,128)S(1)} %get-tuple-element.46.second.refs_1_), channel_id=1, source_target_pairs={{0,8},{8,16},{16,24},{24,28},{28,20},{20,12},{12,4},{4,0},{1,9},{9... | collective-permute-start | bytes 491528 | tf_op jit(solution)/shard_map/ppermute | solution.py:392
  6.8 10.3 %collective-permute-start.5 = (f32[320,128]{1,0:T(8,128)S(1)}, f32[320,128]{1,0:T(8,128)S(1)}, u32[]{:S(2)}, u32[]{:S(2)}) collective-permute-start(f32[320,128]{1,0:T(8,128)S(1)} %get-tuple-element.75.first.refs_0_), channel_id=1, source_target_pairs={{8,0},{16,8},{24,16},{28,24},{20,28},{12,20},{4,12},{0,4},{9,1},{1... | collective-permute-start | bytes 491528 | tf_op jit(solution)/shard_map/ppermute | solution.py:393
  9.5 12.9 %collective-permute-start.3 = (f32[320,128]{1,0:T(8,128)S(1)}, f32[320,128]{1,0:T(8,128)S(1)}, u32[]{:S(2)}, u32[]{:S(2)}) collective-permute-start(f32[320,128]{1,0:T(8,128)S(1)} %collective-permute-done.2.refs_5_), channel_id=1, source_target_pairs={{8,0},{16,8},{24,16},{28,24},{20,28},{12,20},{4,12},{0,4},{9,1},{1... | collective-permute-start | bytes 491528 | tf_op jit(solution)/shard_map/ppermute | solution.py:393
  11.8 10.6 %collective-permute-start.6 = (f32[320,128]{1,0:T(8,128)S(1)}, f32[320,128]{1,0:T(8,128)S(1)}, u32[]{:S(2)}, u32[]{:S(2)}) collective-permute-start(f32[320,128]{1,0:T(8,128)S(1)} %collective-permute-done.refs_2_), channel_id=1, source_target_pairs={{0,8},{8,16},{16,24},{24,28},{28,20},{20,12},{12,4},{4,0},{1,9},{9... | collective-permute-start | bytes 491528 | tf_op jit(solution)/shard_map/ppermute | solution.py:392
  11.9 8.6 %copy-start.1 = (f32[1,128,128]{2,1,0:T(8,128)S(1)}, f32[1,128,128]{2,1,0:T(8,128)}, u32[]{:S(2)}) copy-start(f32[1,128,128]{2,1,0:T(8,128)} %density.3) | copy-start | bytes 196612
  11.9 8.6 %copy-start.2 = (f32[1,128,128]{2,1,0:T(8,128)S(1)}, f32[1,128,128]{2,1,0:T(8,128)}, u32[]{:S(2)}) copy-start(f32[1,128,128]{2,1,0:T(8,128)} %pressure.3) | copy-start | bytes 196612
  11.9 8.6 %copy-start.4 = (s32[1,1,256]{2,1,0:T(1,128)S(1)}, s32[1,1,256]{2,1,0:T(1,128)}, u32[]{:S(2)}) copy-start(s32[1,1,256]{2,1,0:T(1,128)} %bins.1) | copy-start | bytes 3076
  11.9 8.6 %copy-start.5 = (f32[1,1,256]{2,1,0:T(1,128)S(1)}, f32[1,1,256]{2,1,0:T(1,128)}, u32[]{:S(2)}) copy-start(f32[1,1,256]{2,1,0:T(1,128)} %slot_weights.1) | copy-start | bytes 3076
  12.1 10.3 %collective-permute-start.1 = (f32[5,8,128]{2,1,0:T(8,128)S(1)}, f32[5,8,128]{2,1,0:T(8,128)S(1)}, u32[]{:S(2)}, u32[]{:S(2)}) collective-permute-start(f32[5,8,128]{2,1,0:T(8,128)S(1)} %edges.1), channel_id=1, source_target_pairs={{0,28},{8,20},{16,12},{24,4},{28,0},{20,8},{12,16},{4,24},{1,29},{... | collective-permute-start | bytes 61448 | tf_op jit(solution)/shard_map/ppermute | solution.py:405
  17.1 7.4 %collective-permute-start.7 = (f32[320,128]{1,0:T(8,128)S(1)}, f32[320,128]{1,0:T(8,128)S(1)}, u32[]{:S(2)}, u32[]{:S(2)}) collective-permute-start(f32[320,128]{1,0:T(8,128)S(1)} %collective-permute-done.4.refs_3_), channel_id=1, source_target_pairs={{0,8},{8,16},{16,24},{24,28},{28,20},{20,12},{12,4},{4,0},{1,9},{9... | collective-permute-start | bytes 491528 | tf_op jit(solution)/shard_map/ppermute | solution.py:392
  17.1 7.4 %collective-permute-start.8 = (f32[320,128]{1,0:T(8,128)S(1)}, f32[320,128]{1,0:T(8,128)S(1)}, u32[]{:S(2)}, u32[]{:S(2)}) collective-permute-start(f32[320,128]{1,0:T(8,128)S(1)} %collective-permute-done.5.refs_4_), channel_id=1, source_target_pairs={{8,0},{16,8},{24,16},{28,24},{20,28},{12,20},{4,12},{0,4},{9,1},{1... | collective-permute-start | bytes 491528 | tf_op jit(solution)/shard_map/ppermute | solution.py:393
  20.4 0.7 %copy-start.3 = (s32[1,1,256]{2,1,0:T(1,128)S(1)}, s32[1,1,256]{2,1,0:T(1,128)}, u32[]{:S(2)}) copy-start(s32[1,1,256]{2,1,0:T(1,128)} %cells.1) | copy-start | bytes 3076
  22.4 6.5 %collective-permute-start.9 = (f32[320,128]{1,0:T(8,128)S(1)}, f32[320,128]{1,0:T(8,128)S(1)}, u32[]{:S(2)}, u32[]{:S(2)}) collective-permute-start(f32[320,128]{1,0:T(8,128)S(1)} %collective-permute-done.3.refs_9_), channel_id=1, source_target_pairs={{8,0},{16,8},{24,16},{28,24},{20,28},{12,20},{4,12},{0,4},{9,1},{1... | collective-permute-start | bytes 491528 | tf_op jit(solution)/shard_map/ppermute | solution.py:393
  22.4 7.1 %collective-permute-start.10 = (f32[320,128]{1,0:T(8,128)S(1)}, f32[320,128]{1,0:T(8,128)S(1)}, u32[]{:S(2)}, u32[]{:S(2)}) collective-permute-start(f32[320,128]{1,0:T(8,128)S(1)} %collective-permute-done.6.refs_6_), channel_id=1, source_target_pairs={{0,8},{8,16},{16,24},{24,28},{28,20},{20,12},{12,4},{4,0},{1,9},{9... | collective-permute-start | bytes 491528 | tf_op jit(solution)/shard_map/ppermute | solution.py:392
  24.4 7.0 %collective-permute-start.11 = (f32[320,128]{1,0:T(8,128)S(1)}, f32[320,128]{1,0:T(8,128)S(1)}, u32[]{:S(2)}, u32[]{:S(2)}) collective-permute-start(f32[320,128]{1,0:T(8,128)S(1)} %collective-permute-done.7.refs_7_), channel_id=1, source_target_pairs={{0,8},{8,16},{16,24},{24,28},{28,20},{20,12},{12,4},{4,0},{1,9},{9... | collective-permute-start | bytes 491528 | tf_op jit(solution)/shard_map/ppermute | solution.py:392
  24.5 6.9 %collective-permute-start.12 = (f32[320,128]{1,0:T(8,128)S(1)}, f32[320,128]{1,0:T(8,128)S(1)}, u32[]{:S(2)}, u32[]{:S(2)}) collective-permute-start(f32[320,128]{1,0:T(8,128)S(1)} %collective-permute-done.8.refs_8_), channel_id=1, source_target_pairs={{8,0},{16,8},{24,16},{28,24},{20,28},{12,20},{4,12},{0,4},{9,1},{1... | collective-permute-start | bytes 491528 | tf_op jit(solution)/shard_map/ppermute | solution.py:393
  28.9 5.3 %collective-permute-start.14 = (f32[320,128]{1,0:T(8,128)S(1)}, f32[320,128]{1,0:T(8,128)S(1)}, u32[]{:S(2)}, u32[]{:S(2)}) collective-permute-start(f32[320,128]{1,0:T(8,128)S(1)} %collective-permute-done.9.right_second), channel_id=1, source_target_pairs={{8,0},{16,8},{24,16},{28,24},{20,28},{12,20},{4,12},{0,4},{9,1},{1... | collective-permute-start | bytes 491528 | tf_op jit(solution)/shard_map/ppermute | solution.py:453
  29.5 5.3 %collective-permute-start.13 = (f32[320,128]{1,0:T(8,128)S(1)}, f32[320,128]{1,0:T(8,128)S(1)}, u32[]{:S(2)}, u32[]{:S(2)}) collective-permute-start(f32[320,128]{1,0:T(8,128)S(1)} %collective-permute-done.10.left_first), channel_id=1, source_target_pairs={{0,8},{8,16},{16,24},{24,28},{28,20},{20,12},{12,4},{4,0},{1,9},{9... | collective-permute-start | bytes 491528 | tf_op jit(solution)/shard_map/ppermute | solution.py:452
  31.6 3.9 %collective-permute-start.15 = (f32[5,8,128]{2,1,0:T(8,128)S(1)}, f32[5,8,128]{2,1,0:T(8,128)S(1)}, u32[]{:S(2)}, u32[]{:S(2)}) collective-permute-start(f32[5,8,128]{2,1,0:T(8,128)S(1)} %get-tuple-element.65), channel_id=1, source_target_pairs={{0,3},{1,2},{2,1},{3,0},{4,7},{5,6},{6,5},{7,4},{8,11},{9,10},{10,... | collective-permute-start | bytes 61448 | tf_op jit(solution)/shard_map/ppermute | solution.py:465
  31.7 3.9 %collective-permute-start.16 = (f32[5,8,128]{2,1,0:T(8,128)S(1)}, f32[5,8,128]{2,1,0:T(8,128)S(1)}, u32[]{:S(2)}, u32[]{:S(2)}) collective-permute-start(f32[5,8,128]{2,1,0:T(8,128)S(1)} %get-tuple-element.65), channel_id=1, source_target_pairs={{0,1},{1,0},{2,3},{3,2},{4,5},{5,4},{6,7},{7,6},{8,9},{9,8},{10,11... | collective-permute-start | bytes 61448 | tf_op jit(solution)/shard_map/ppermute | solution.py:465
